TPU v7x, 32 devices: a whole 2x2x4 slice. The times are simulated.
32 devices in a mesh: dp: 8 (over z, y), chan: 4 (over x, core).
Axes of the slice: x: 2, y: 2, z: 4, core: 2. Of those that a mesh axis runs over, the one named last changes fastest.
Arguments:
- images: bfloat16 [256, 10, 14, 1536], P('dp', None, None, 'chan'), may hold values from -6 to 6
- aspect: int32 [256], P('dp'), may hold values from 0 to 1
- reduce_weight: bfloat16 [1536, 768], P('chan'), may hold values from -400 to 400
- reduce_gain: float32 [768], replicated, may hold values from 0.1 to 1.9
- reduce_bias: float32 [768], replicated, may hold values from -3 to 3
- first_weight: bfloat16 [3, 3, 128, 768], replicated, may hold values from -6 to 6
- first_gain: float32 [768], replicated, may hold values from 0.1 to 1.9
- first_bias: float32 [768], replicated, may hold values from -3 to 3
- second_weight: bfloat16 [3, 3, 128, 768], replicated, may hold values from -6 to 6
- second_gain: float32 [768], replicated, may hold values from 0.1 to 1.9
- second_bias: float32 [768], replicated, may hold values from -3 to 3
- expand_weight: bfloat16 [768, 1536], P('chan'), may hold values from -400 to 400
- expand_gain: float32 [1536], P('chan'), may hold values from 0.1 to 1.9
- expand_bias: float32 [1536], P('chan'), may hold values from -3 to 3
- excite_down: bfloat16 [1536, 768], P('chan'), may hold values from -0.3125 to 0.3125
- excite_down_bias: float32 [768], replicated, may hold values from -3 to 3
- excite_up: bfloat16 [768, 1536], P(None, 'chan'), may hold values from -0.4375 to 0.4375
- excite_up_bias: float32 [1536], P('chan'), may hold values from -3 to 3
- skip_gain: float32 [1], replicated, may hold values from 3 to 6
- out_grad: bfloat16 [256, 10, 14, 1536], P('dp', None, None, 'chan'), may hold values from -6 to 6
Outputs:
- block_out: bfloat16 [256, 10, 14, 1536], P('dp', None, None, 'chan')
- images_grad: float32 [256, 10, 14, 1536], P('dp', None, None, 'chan')
- reduce_weight_grad: float32 [1536, 768], P('chan')
- reduce_gain_grad: float32 [768], replicated
- reduce_bias_grad: float32 [768], replicated
- first_weight_grad: float32 [3, 3, 128, 768], replicated
- first_gain_grad: float32 [768], replicated
- first_bias_grad: float32 [768], replicated
- second_weight_grad: float32 [3, 3, 128, 768], replicated
- second_gain_grad: float32 [768], replicated
- second_bias_grad: float32 [768], replicated
- expand_weight_grad: float32 [768, 1536], P('chan')
- expand_gain_grad: float32 [1536], P('chan')
- expand_bias_grad: float32 [1536], P('chan')
- excite_down_grad: float32 [1536, 768], P('chan')
- excite_down_bias_grad: float32 [768], replicated
- excite_up_grad: float32 [768, 1536], P(None, 'chan')
- excite_up_bias_grad: float32 [1536], P('chan')
- skip_gain_grad: float32 [1], replicated
Inputs may be any that keep to these rules, and one draw needn't show every extreme that they name: `aspect`: 0: the image is 10 rows by 14 columns as stored; 1: it is 14 rows by 10 columns, stored transposed.
All inputs are finite; a program needn't handle non-finite values.
Results may differ from a plain program's by a relative error of at most 0.025.
The roundings to bfloat16 on the way count: a program that leaves them out, or rounds other values in their place, can miss the bound.
Values may be sent and summed in bfloat16 or wider, within the bound.
A program may use at most 256 MiB of HBM per device.

v0:
```python
import jax
import jax.numpy as jnp
from jax import lax
from jax.sharding import PartitionSpec as P

INV_BETA = 1.0 / 1.16619037896906
ALPHA_RES = 0.2
GELU_SCALE = 1.7015
STD_EPSILON = 0.0001
PRECISE = lax.Precision.HIGHEST
NUMBERS = ("NHWC", "HWIO", "NHWC")


def gelu_scaled(value):
    return GELU_SCALE * jax.nn.gelu(value, approximate=True)


def gelu_plain(value):
    return jax.nn.gelu(value, approximate=True)


def backward_of(function, primal, cotangent):
    _, pullback = jax.vjp(function, primal)
    return pullback(cotangent)[0]


def standardize(weight, axes):
    middle = jnp.mean(weight, axis=axes, keepdims=True)
    centered = weight - middle
    spread = jnp.mean(centered * centered, axis=axes, keepdims=True)
    fan_in = 1
    for dimension in axes:
        fan_in = fan_in * weight.shape[dimension]
    return centered * lax.rsqrt(spread * fan_in + STD_EPSILON)


def standardize_group(weight):
    return standardize(weight, (0, 1, 2))


def column_moments(total, squares, fan_in):
    middle = total / fan_in
    spread = squares / fan_in - middle * middle
    return (middle, lax.rsqrt(spread * fan_in + STD_EPSILON))


def standard_grad(summed, centered, rate, column_sum, column_cross, fan_in):
    return rate * (summed - column_sum / fan_in) - rate * rate * rate * centered * column_cross


def group_conv(values, kernel, groups):
    return lax.conv_general_dilated(
        values,
        kernel,
        (1, 1),
        "SAME",
        dimension_numbers=NUMBERS,
        feature_group_count=groups,
        preferred_element_type=jnp.float32,
    )


def group_input_grad(cotangent, kernel, groups):
    taps = kernel.shape[2]
    parted = kernel.reshape(3, 3, taps, groups, taps)
    swapped = jnp.transpose(parted, (0, 1, 4, 3, 2)).reshape(3, 3, taps, groups * taps)[::-1, ::-1]
    return group_conv(cotangent, swapped, groups)


def group_weight_grad(values, cotangent, groups):
    height, width = (values.shape[1], values.shape[2])
    taps = values.shape[3] // groups
    padded = jnp.pad(values, ((0, 0), (1, 1), (1, 1), (0, 0)))
    parted_grad = cotangent.reshape(cotangent.shape[:3] + (groups, taps))
    kernel_rows = []
    for shift_h in range(3):
        row_terms = []
        for shift_w in range(3):
            window = padded[:, shift_h : shift_h + height, shift_w : shift_w + width, :]
            window = window.reshape(window.shape[:3] + (groups, taps))
            product = jnp.einsum(
                "nhwgi,nhwgo->igo", window, parted_grad, preferred_element_type=jnp.float32
            )
            row_terms.append(product.reshape(taps, groups * taps))
        kernel_rows.append(jnp.stack(row_terms))
    return jnp.stack(kernel_rows)


def oriented_conv(values, kernel, aspects, groups):
    plain = group_conv(values, kernel, groups)
    turned = group_conv(values, jnp.transpose(kernel, (1, 0, 2, 3)), groups)
    return jnp.where((aspects == 1)[:, None, None, None], turned, plain)


def oriented_back(values, cotangent, kernel, aspects, groups):
    turned_mask = (aspects == 1)[:, None, None, None]
    nothing = jnp.zeros_like(cotangent)
    grad_plain = jnp.where(turned_mask, nothing, cotangent)
    grad_turned = jnp.where(turned_mask, cotangent, nothing)
    kernel_turned = jnp.transpose(kernel, (1, 0, 2, 3))
    grad_values = group_input_grad(grad_plain, kernel, groups) + group_input_grad(
        grad_turned, kernel_turned, groups
    )
    grad_kernel = group_weight_grad(values, grad_plain, groups)
    grad_kernel = grad_kernel + jnp.transpose(
        group_weight_grad(values, grad_turned, groups), (1, 0, 2, 3)
    )
    return (grad_values, grad_kernel)


def body(
    images,
    aspect,
    reduce_weight,
    reduce_gain,
    reduce_bias,
    first_weight,
    first_gain,
    first_bias,
    second_weight,
    second_gain,
    second_bias,
    expand_weight,
    expand_gain,
    expand_bias,
    excite_down,
    excite_down_bias,
    excite_up,
    excite_up_bias,
    skip_gain,
    out_grad,
):
    parts = lax.axis_size("chan")
    index = lax.axis_index("chan")
    n_images = images.shape[0]
    share = n_images // parts
    groups = first_weight.shape[3] // first_weight.shape[2]
    mid_share = expand_weight.shape[0]
    in_share = reduce_weight.shape[0]
    pixel_count = images.shape[1] * images.shape[2]
    reduce_fan = in_share * parts
    expand_fan = mid_share * parts
    reduce32 = reduce_weight.astype(jnp.float32)
    expand32 = expand_weight.astype(jnp.float32)
    moments = lax.psum(
        (
            jnp.sum(reduce32, axis=0),
            jnp.sum(reduce32 * reduce32, axis=0),
            jnp.sum(expand32, axis=0),
            jnp.sum(expand32 * expand32, axis=0),
        ),
        "chan",
    )
    reduce_mean, reduce_rate = column_moments(moments[0], moments[1], reduce_fan)
    expand_mean, expand_rate = column_moments(moments[2], moments[3], expand_fan)
    reduce_center = reduce32 - reduce_mean
    expand_center = expand32 - expand_mean
    kernel_reduce = (reduce_center * reduce_rate).astype(jnp.bfloat16)
    kernel_expand = (expand_center * expand_rate).astype(jnp.bfloat16)
    kernel_first = standardize_group(first_weight.astype(jnp.float32)).astype(jnp.bfloat16)
    kernel_second = standardize_group(second_weight.astype(jnp.float32)).astype(jnp.bfloat16)
    scaled = (images.astype(jnp.float32) * INV_BETA).astype(jnp.bfloat16)
    aspects = lax.dynamic_slice_in_dim(aspect, index * share, share, 0)
    rows = scaled
    pre_reduce = lax.psum_scatter(
        jnp.einsum("nhwc,cm->nhwm", rows, kernel_reduce, preferred_element_type=jnp.float32),
        "chan",
        scatter_dimension=0,
        tiled=True,
    )
    out_reduce = reduce_gain * pre_reduce + reduce_bias
    act_reduce = gelu_scaled(out_reduce).astype(jnp.bfloat16)
    pre_first = oriented_conv(act_reduce, kernel_first, aspects, groups)
    out_first = first_gain * pre_first + first_bias
    act_first = gelu_scaled(out_first).astype(jnp.bfloat16)
    pre_second = oriented_conv(act_first, kernel_second, aspects, groups)
    out_second = second_gain * pre_second + second_bias
    act_second = gelu_scaled(out_second).astype(jnp.bfloat16)
    act_columns = lax.all_to_all(act_second, "chan", split_axis=3, concat_axis=0, tiled=True)
    partials = jnp.einsum(
        "nhwm,mc->nhwc", act_columns, kernel_expand, preferred_element_type=jnp.float32
    )
    pre_expand = lax.psum_scatter(
        partials.astype(jnp.bfloat16), "chan", scatter_dimension=3, tiled=True
    ).astype(jnp.float32)
    out_expand = expand_gain * pre_expand + expand_bias
    pooled = jnp.mean(out_expand, axis=(1, 2))
    down_partial = jnp.dot(pooled, excite_down.astype(jnp.float32), precision=PRECISE)
    down = lax.psum(down_partial, "chan") + excite_down_bias
    hidden = gelu_plain(down)
    upper = jnp.dot(hidden, excite_up.astype(jnp.float32), precision=PRECISE) + excite_up_bias
    sigma = jax.nn.sigmoid(upper)
    gating = 2.0 * sigma
    branch = out_expand * gating[:, None, None, :]
    branch_scale = ALPHA_RES * skip_gain[0]
    block_out = (images.astype(jnp.float32) + branch_scale * branch).astype(jnp.bfloat16)
    grad_out = out_grad.astype(jnp.float32)
    skip_term = ALPHA_RES * jnp.sum(grad_out * branch)
    grad_branch = branch_scale * grad_out
    grad_gating = jnp.sum(grad_branch * out_expand, axis=(1, 2))
    grad_upper = grad_gating * 2.0 * sigma * (1.0 - sigma)
    excite_up_bias_grad = jnp.sum(grad_upper, axis=0)
    excite_up_grad = jnp.dot(hidden.T, grad_upper, precision=PRECISE)
    hidden_partial = jnp.dot(grad_upper, excite_up.astype(jnp.float32).T, precision=PRECISE)
    grad_hidden = lax.psum(hidden_partial.astype(jnp.bfloat16), "chan").astype(jnp.float32)
    grad_down = backward_of(gelu_plain, down, grad_hidden)
    excite_down_bias_grad = jnp.sum(grad_down, axis=0)
    excite_down_grad = jnp.dot(pooled.T, grad_down, precision=PRECISE)
    grad_pooled = jnp.dot(grad_down, excite_down.astype(jnp.float32).T, precision=PRECISE)
    grad_expand = (
        grad_branch * gating[:, None, None, :] + grad_pooled[:, None, None, :] / pixel_count
    )
    expand_gain_grad = jnp.sum(grad_expand * pre_expand, axis=(0, 1, 2))
    expand_bias_grad = jnp.sum(grad_expand, axis=(0, 1, 2))
    grad_pre_expand = (grad_expand * expand_gain).astype(jnp.bfloat16)
    start_columns = jnp.zeros(act_columns.shape, jnp.float32)
    start_kernel = jnp.zeros((mid_share, expand_weight.shape[1]), jnp.float32)
    piece = lax.all_gather(grad_pre_expand, "chan", axis=3, tiled=True)
    start = jnp.int32(0)
    grad_columns = start_columns
    grad_kernel = start_kernel
    kernel_part = lax.dynamic_slice_in_dim(kernel_expand, start, piece.shape[3], 1)
    grad_columns = grad_columns + jnp.einsum(
        "nhwc,mc->nhwm", piece, kernel_part, preferred_element_type=jnp.float32
    )
    grad_block = jnp.einsum("nhwm,nhwc->mc", act_columns, piece, preferred_element_type=jnp.float32)
    grad_kernel = lax.dynamic_update_slice_in_dim(grad_kernel, grad_block, start, 1)
    grad_columns, expand_rows = (grad_columns, grad_kernel)
    grad_act_second = lax.all_to_all(
        grad_columns.astype(jnp.bfloat16), "chan", split_axis=0, concat_axis=3, tiled=True
    )
    expand_column_sum = jnp.sum(expand_rows, axis=0)
    expand_cross = jnp.sum(expand_rows * expand_center, axis=0)
    expand_full = jnp.zeros((1, 1), jnp.float32)
    grad_second = backward_of(gelu_scaled, out_second, grad_act_second.astype(jnp.float32))
    second_gain_term = jnp.sum(grad_second * pre_second, axis=(0, 1, 2))
    second_bias_term = jnp.sum(grad_second, axis=(0, 1, 2))
    grad_pre_second = (grad_second * second_gain).astype(jnp.bfloat16)
    grad_act_first, grad_kernel_second = oriented_back(
        act_first, grad_pre_second, kernel_second, aspects, groups
    )
    grad_first = backward_of(gelu_scaled, out_first, grad_act_first)
    first_gain_term = jnp.sum(grad_first * pre_first, axis=(0, 1, 2))
    first_bias_term = jnp.sum(grad_first, axis=(0, 1, 2))
    grad_pre_first = (grad_first * first_gain).astype(jnp.bfloat16)
    grad_act_reduce, grad_kernel_first = oriented_back(
        act_reduce, grad_pre_first, kernel_first, aspects, groups
    )
    grad_reduce = backward_of(gelu_scaled, out_reduce, grad_act_reduce)
    reduce_gain_term = jnp.sum(grad_reduce * pre_reduce, axis=(0, 1, 2))
    reduce_bias_term = jnp.sum(grad_reduce, axis=(0, 1, 2))
    grad_pre_reduce = (grad_reduce * reduce_gain).astype(jnp.bfloat16)
    piece = lax.all_gather(grad_pre_reduce, "chan", axis=0, tiled=True)
    rows = scaled
    grad_kernel = jnp.einsum("nhwc,nhwm->cm", rows, piece, preferred_element_type=jnp.float32)
    grad_rows = jnp.einsum(
        "nhwm,cm->nhwc", piece, kernel_reduce, preferred_element_type=jnp.float32
    )
    grad_scaled = grad_rows
    grad_kernel_reduce, grad_scaled = (grad_kernel, grad_scaled)
    images_grad = grad_out + INV_BETA * grad_scaled
    reduce_column_sum = jnp.sum(grad_kernel_reduce, axis=0)
    reduce_cross = jnp.sum(grad_kernel_reduce * reduce_center, axis=0)
    sharded = lax.psum(
        (
            grad_kernel_reduce,
            expand_rows,
            excite_down_grad,
            excite_down_bias_grad,
            excite_up_grad,
            excite_up_bias_grad,
            expand_gain_grad,
            expand_bias_grad,
        ),
        "dp",
    )
    shared = lax.psum(
        (
            grad_kernel_first,
            grad_kernel_second,
            reduce_gain_term,
            reduce_bias_term,
            first_gain_term,
            first_bias_term,
            second_gain_term,
            second_bias_term,
            skip_term,
            reduce_column_sum,
            reduce_cross,
            expand_column_sum,
            expand_cross,
            expand_full,
        ),
        ("dp", "chan"),
    )
    expand_summed = sharded[1]
    reduce_weight_grad = standard_grad(
        sharded[0], reduce_center, reduce_rate, shared[9], shared[10], reduce_fan
    )
    expand_weight_grad = standard_grad(
        expand_summed, expand_center, expand_rate, shared[11], shared[12], expand_fan
    )
    first_weight_grad = backward_of(standardize_group, first_weight.astype(jnp.float32), shared[0])
    second_weight_grad = backward_of(
        standardize_group, second_weight.astype(jnp.float32), shared[1]
    )
    return (
        block_out,
        images_grad,
        reduce_weight_grad,
        shared[2],
        shared[3],
        first_weight_grad,
        shared[4],
        shared[5],
        second_weight_grad,
        shared[6],
        shared[7],
        expand_weight_grad,
        sharded[6],
        sharded[7],
        sharded[2],
        sharded[3],
        sharded[4],
        sharded[5],
        shared[8].reshape(1),
    )


def solution(mesh):
    placed = (
        P("dp", None, None, "chan"),
        P("dp"),
        P("chan", None),
        P(),
        P(),
        P(),
        P(),
        P(),
        P(),
        P(),
        P(),
        P("chan", None),
        P("chan"),
        P("chan"),
        P("chan", None),
        P(),
        P(None, "chan"),
        P("chan"),
        P(),
        P("dp", None, None, "chan"),
    )
    return jax.shard_map(
        body,
        mesh=mesh,
        in_specs=placed,
        out_specs=(
            P("dp", None, None, "chan"),
            P("dp", None, None, "chan"),
            P("chan", None),
            P(),
            P(),
            P(),
            P(),
            P(),
            P(),
            P(),
            P(),
            P("chan", None),
            P("chan"),
            P("chan"),
            P("chan", None),
            P(),
            P(None, "chan"),
            P("chan"),
            P(),
        ),
        check_vma=False,
    )
```

profile of v0, /device:TPU:0, one launch (start us, length us, event | category | flops | bytes accessed | tf_op | source)
XLA Modules:
  0.0 1309.2 jit_solution(16552987430906464153)
XLA Ops:
  9.8 12.8 all-reduce.6
  23.8 10.8 fusion.82
  34.6 2.8 copy.278
  42.1 3.4 copy.280
  50.2 91.7 %reduce-scatter.5.cloned.1.call-done = f32[8,10,14,768]{3,0,2,1:T(8,128)} async-done(((f32[32,10,14,768]{3,0,2,1:T(8,128)}), f32[8,10,14,768]{3,0,2,1:T(8,128)}) %reduce-scatter.5.cloned.1.call-update) | async-done | bytes 3440656 | tf_op jit(solution)/shard_map/reduce_scatter | solution.py:165
  142.0 3.4 multiply_convert_fusion.3
  145.4 4.2 fusion.106
  149.6 6.6 multiply_convert_fusion.2
  156.3 4.4 fusion.276
  160.7 8.3 fusion.72
  169.0 12.9 copy.282
  182.0 37.4 %reshape.338 = bf16[4,2,107520]{2,1,0:T(2,128)(2,1)} reshape(bf16[768,10,8,14]{3,2,1,0:T(8,128)(2,1)} %bitcast.508) | data formatting | bytes 3440640
  219.4 4.4 all-to-all-start
  224.5 21.1 %all-to-all-done = bf16[4,2,107520]{2,1,0:T(2,128)(2,1)} async-done(((bf16[4,2,107520]{2,1,0:T(2,128)(2,1)}), bf16[4,2,107520]{2,1,0:T(2,128)(2,1)}, u32[]{:S(2)}, u32[]{:S(2)}) %all-to-all-start) | async-done | bytes 1720352 | tf_op jit(solution)/shard_map/all_to_all | solution.py:179
  245.5 42.7 %reshape.339 = bf16[768,10,8,14]{3,2,1,0:T(8,128)(2,1)} reshape(bf16[4,2,107520]{2,1,0:T(2,128)(2,1)} %all-to-all-done) | data formatting | bytes 3440640
  288.3 20.3 %copy.283 = bf16[8,10,14,4,192]{4,0,3,2,1:T(8,128)(2,1)} copy(bf16[8,10,14,4,192]{2,0,1,4,3:T(8,128)(2,1)} %bitcast.510) | data formatting | bytes 3440640 | tf_op jit(solution)/shard_map/all_to_all | solution.py:179
  308.6 8.6 convolution_convert_fusion
  317.2 83.1 %copy.341 = bf16[32,10,14,1536]{0,2,1,3:T(8,128)(2,1)} copy(bf16[32,10,14,1536]{3,0,2,1:T(8,128)(2,1)} %convolution_convert_fusion) | data formatting | bytes 27525120
  400.3 72.3 %reshape.336 = bf16[1536,4480]{1,0:T(8,128)(2,1)} reshape(bf16[1536,10,14,32]{3,2,1,0:T(8,128)(2,1)} %bitcast.507) | data formatting | bytes 27525120
  473.3 106.2 %reduce-scatter.7.cloned.1.call-done = bf16[384,4480]{1,0:T(8,128)(2,1)} async-done(((bf16[1536,4480]{1,0:T(8,128)(2,1)}), bf16[384,4480]{1,0:T(8,128)(2,1)}) %reduce-scatter.7.cloned.1.call-update) | async-done | bytes 3440656
  579.5 18.1 %reshape.337 = bf16[384,10,14,32]{3,2,1,0:T(8,128)(2,1)} reshape(bf16[384,4480]{1,0:T(8,128)(2,1)} %reduce-scatter.7.cloned.1.call-done) | data formatting | bytes 6881280
  597.6 18.6 %copy.342 = bf16[32,10,14,384]{3,0,2,1:T(8,128)(2,1)} copy(bf16[32,10,14,384]{0,2,1,3:T(8,128)(2,1)} %bitcast.509) | data formatting | bytes 6881280
  616.3 4.9 fusion.6
  622.2 31.4 %all-reduce.11.cloned.1.call-done = f32[32,768]{1,0:T(8,128)} async-done(((f32[32,768]{1,0:T(8,128)}), f32[32,768]{1,0:T(8,128)}) %all-reduce.11.cloned.1.call-update) | async-done | bytes 98320 | tf_op jit(solution)/shard_map/psum | solution.py:189
  655.6 10.6 psum.194
  668.8 9.0 fusion.14
  681.4 2.8 rev.20
  686.5 3.2 rev.22
  691.9 3.2 rev.24
  697.3 2.8 rev.26
  700.1 5.2 copy.293
  705.3 3.0 copy.294
  708.3 6.7 conv_general_dilated.49
  714.9 6.7 conv_general_dilated.48
  722.3 37.5 %all-reduce.4 = (f32[384]{0:T(512)}, f32[384]{0:T(512)}, f32[768]{0:T(1024)}, f32[384]{0:T(512)}) all-reduce(f32[384]{0:T(512)S(1)} %get-tuple-element.96, f32[384]{0:T(512)S(1)} %get-tuple-element.99, f32[768]{0:T(1024)S(1)} %get-tuple-element.139, f32[384]{0:T(512)S(1)} %get-tuple-element.148), channel_id=1, replica_groups=mesh['dp'=8,'chan'=4] {'dp'}, use_global_device_ids=true, to_apply=%region_47.48 | all-reduce | flops 1920 | bytes 15360 | tf_op jit(solution)/shard_map/psum | solution.py:264
  764.1 2.6 all-gather.3.cloned.1.call-done
  766.7 8.7 convolution_convert_fusion.1
  775.4 2.8 copy.284
  778.2 4.7 all-to-all-start.1
  783.4 9.5 fusion.272
  792.9 21.4 %all-to-all-done.1 = bf16[32,10,14,192]{3,2,1,0:T(8,128)(2,1)} async-done(((bf16[32,10,14,192]{3,2,1,0:T(8,128)(2,1)}), bf16[32,10,14,192]{3,2,1,0:T(8,128)(2,1)}, u32[]{:S(2)}, u32[]{:S(2)}) %all-to-all-start.1) | async-done | bytes 1720352 | tf_op jit(solution)/shard_map/all_to_all | solution.py:229
  814.3 3.3 multiply_bitcast_fusion
  817.7 3.9 copy.286
  821.6 6.8 mul.791
  828.4 6.3 fusion.54
  860.3 4.2 fusion.267
  864.6 8.1 broadcast_select_fusion
  883.8 4.2 fusion.277
  888.1 7.6 fusion.271
  917.4 9.6 fusion.269
  927.1 18.4 %all-gather.5.cloned.1.call-done = bf16[32,10,14,768]{3,0,2,1:T(8,128)(2,1)} async-done(((bf16[8,10,14,768]{3,0,2,1:T(8,128)(2,1)}), bf16[32,10,14,768]{3,0,2,1:T(8,128)(2,1)}) %all-gather.5.cloned.1.call-update) | async-done | bytes 6881296 | tf_op jit(solution)/shard_map/all_gather | solution.py:253
  945.6 8.0 fusion.273
  953.6 3.5 fusion.270
  957.1 160.8 %all-reduce.13.cloned.1.call-done = (f32[3,3,128,768]{2,3,0,1:T(8,128)}, f32[3,3,128,768]{2,3,0,1:T(8,128)}) async-done(((f32[3,3,128,768]{2,3,0,1:T(8,128)}, f32[3,3,128,768]{2,3,0,1:T(8,128)}), (f32[3,3,128,768]{2,3,0,1:T(8,128)}, f32[3,3,128,768]{2,3,0,1:T(8,128)})) %all-reduce.13.cloned.1.call-update) | async-done | bytes 7077904 | tf_op jit(solution)/shard_map/psum | solution.py:277
  1117.9 3.3 fusion.34
  1124.6 2.4 fusion.264
  1127.0 2.4 broadcast_add_fusion
  1129.4 5.5 copy.298
  1134.9 3.8 broadcast_add_fusion.1
  1138.8 5.2 copy.297
  1144.0 47.2 %all-reduce.2 = (f32[768]{0:T(1024)S(1)}, f32[768]{0:T(1024)S(1)}, f32[768]{0:T(1024)}, f32[768]{0:T(1024)}, f32[768]{0:T(1024)}, /*index=5*/f32[768]{0:T(1024)}...) all-reduce(f32[768]{0:T(1024)S(1)} %get-tuple-element.109, ...), channel_id=1, replica_groups=mesh['dp'=8,'chan'=4] {'dp','chan'}, use_global_device_ids=true, to_apply=%region_22.23 | all-reduce | flops 9217 | bytes 73736 | tf_op jit(solution)/shard_map/psum | solution.py:277
  1191.2 10.7 convert_add_fusion
  1201.9 93.5 %all-reduce.15.cloned.1.call-done = (f32[384,768]{1,0:T(8,128)}, f32[192,1536]{1,0:T(8,128)}, f32[384,768]{1,0:T(8,128)}, f32[768,384]{1,0:T(8,128)}) async-done(((f32[384,768]{1,0:T(8,128)}, f32[192,1536]{1,0:T(8,128)}, f32[384,768]{1,0:T(8,128)}, f32[768,384]{1,0:T(8,128)}), (f32[384,768]{1,0:T(8,128)}, f32[192,1536]{1,0:T(8,128)}, f32[384,768]{1,0:T(8,128)}, ...) | async-done | bytes 4718608 | tf_op jit(solution)/shard_map/psum | solution.py:264
  1295.4 2.7 fusion.185
  (310 shorter events, 100.3 us)
Async XLA Ops:
  7.2 646.4 %copy-start = (bf16[768,384]{1,0:T(8,128)(2,1)S(1)}, bf16[768,384]{1,0:T(8,128)(2,1)}, u32[]{:S(2)}) copy-start(bf16[768,384]{1,0:T(8,128)(2,1)} %param.36) | copy-start | bytes 1769476
  7.2 134.7 %reduce-scatter.5.cloned.1.call-start = ((), (), s32[]{:S(2)}) async-start(), calls=%async_computation.4 | async-start | bytes 17203200 | tf_op jit(solution)/shard_map/reduce_scatter | solution.py:165
  48.8 93.2 %copy-start.87 = (f32[768]{0:T(1024)S(1)}, f32[768]{0:T(1024)}, u32[]{:S(2)}) copy-start(f32[768]{0:T(1024)} %param.24) | copy-start | bytes 9220
  48.8 93.2 %copy-start.89 = (f32[768]{0:T(1024)S(1)}, f32[768]{0:T(1024)}, u32[]{:S(2)}) copy-start(f32[768]{0:T(1024)} %param.23) | copy-start | bytes 9220
  50.2 814.3 %copy-start.91 = (pred[8]{0:T(512)(128)(4,1)}, pred[8]{0:T(512)(128)(4,1)S(1)}, u32[]{:S(2)}) copy-start(pred[8]{0:T(512)(128)(4,1)S(1)} %dynamic-slice_compare_fusion) | copy-start | bytes 28
  50.2 95.1 %copy-start.25 = (bf16[3,3,128,768]{2,3,1,0:T(8,128)(2,1)S(1)}, bf16[3,3,128,768]{2,3,1,0:T(8,128)(2,1)}, u32[]{:S(2)}) copy-start(bf16[3,3,128,768]{2,3,1,0:T(8,128)(2,1)} %copy.279) | copy-start | bytes 5308420
  145.4 4.2 copy-start.15
  145.4 4.2 copy-start.13
  145.4 4.2 copy-start.93
  145.4 4.2 copy-start.95
  149.6 6.7 copy-start.7
  156.3 4.4 copy-start.17
  156.3 4.4 copy-start.33
  156.3 4.4 copy-start.81
  156.3 4.4 copy-start.82
  160.7 8.4 copy-start.11
  219.4 26.1 %all-to-all-start = ((bf16[4,2,107520]{2,1,0:T(2,128)(2,1)}), bf16[4,2,107520]{2,1,0:T(2,128)(2,1)}, u32[]{:S(2)}, u32[]{:S(2)}) async-start(bf16[4,2,107520]{2,1,0:T(2,128)(2,1)} %reshape.338), calls=%async_computation.1 | async-start | bytes 3440640 | tf_op jit(solution)/shard_map/all_to_all | solution.py:179
  223.8 355.7 %reduce-scatter.7.cloned.1.call-start = ((), (), s32[]{:S(2)}) async-start(), calls=%async_computation.8 | async-start | bytes 17203200
  224.5 542.3 %copy-start.62 = (f32[1536]{0:T(1024)}, f32[1536]{0:T(1024)S(1)}, u32[]{:S(2)}) copy-start(f32[1536]{0:T(1024)S(1)} %get-tuple-element.151) | copy-start | bytes 18436
  224.5 558.9 %copy-start.60 = (f32[1536]{0:T(1024)}, f32[1536]{0:T(1024)S(1)}, u32[]{:S(2)}) copy-start(f32[1536]{0:T(1024)S(1)} %get-tuple-element.152) | copy-start | bytes 18436
  288.3 20.3 %copy-start.22 = (bf16[192,1536]{1,0:T(8,128)(2,1)S(1)}, bf16[192,1536]{1,0:T(8,128)(2,1)}, u32[]{:S(2)}) copy-start(bf16[192,1536]{1,0:T(8,128)(2,1)} %param.31) | copy-start | bytes 1769476
  472.6 181.0 %all-reduce.11.cloned.1.call-start = ((), (), s32[]{:S(2)}) async-start(), calls=%async_computation.5 | async-start | bytes 196608 | tf_op jit(solution)/shard_map/psum | solution.py:189
  597.6 18.6 %copy-start.85 = (f32[384]{0:T(512)S(1)}, f32[384]{0:T(512)}, u32[]{:S(2)}) copy-start(f32[384]{0:T(512)} %param.33) | copy-start | bytes 4612
  597.6 18.6 %copy-start.86 = (f32[384]{0:T(512)S(1)}, f32[384]{0:T(512)}, u32[]{:S(2)}) copy-start(f32[384]{0:T(512)} %param.32) | copy-start | bytes 4612
  616.2 4.9 copy-start.29
  616.2 37.4 %copy-start.79 = (f32[768]{0:T(1024)S(1)}, f32[768]{0:T(1024)}, u32[]{:S(2)}) copy-start(f32[768]{0:T(1024)} %param.35) | copy-start | bytes 9220
  616.2 37.4 %copy-start.97 = (f32[384]{0:T(512)S(1)}, f32[384]{0:T(512)}, u32[]{:S(2)}) copy-start(f32[384]{0:T(512)} %param.37) | copy-start | bytes 4612
  622.2 144.6 %all-gather.3.cloned.1.call-start = ((), (), s32[]{:S(2)}) async-start(), calls=%async_computation.6 | async-start | bytes 17203200 | tf_op jit(solution)/shard_map/all_gather | solution.py:218
  686.5 3.2 copy-start.14
  700.1 5.2 copy-start.21
  714.9 47.0 %copy-start.55 = (f32[32,768]{1,0:T(8,128)S(1)}, f32[32,768]{1,0:T(8,128)}, u32[]{:S(2)}) copy-start(f32[32,768]{1,0:T(8,128)} %all-reduce.11.cloned.1.call-done) | copy-start | bytes 294916
  778.2 5.2 copy-start.8
  778.2 36.1 %all-to-all-start.1 = ((bf16[32,10,14,192]{3,2,1,0:T(8,128)(2,1)}), bf16[32,10,14,192]{3,2,1,0:T(8,128)(2,1)}, u32[]{:S(2)}, u32[]{:S(2)}) async-start(bf16[32,10,14,192]{3,2,1,0:T(8,128)(2,1)} %copy.284), calls=%async_computation.2 | async-start | bytes 5242880 | tf_op jit(solution)/shard_map/all_to_all | solution.py:229
  783.0 162.6 %all-gather.5.cloned.1.call-start = ((), (), s32[]{:S(2)}) async-start(), calls=%async_computation.7 | async-start | bytes 8601600 | tf_op jit(solution)/shard_map/all_gather | solution.py:253
  828.4 6.3 copy-start.99
  860.3 4.2 copy-start.28
  860.3 4.2 copy-start.31
  860.3 4.2 copy-start.94
  860.3 4.3 copy-start.96
  864.6 8.1 copy-start.16
  872.7 11.1 copy-start.19
  872.7 15.4 %copy-start.100 = (bf16[8,10,14,6,128]{4,0,3,2,1:T(8,128)(2,1)}, bf16[8,10,14,6,128]{4,0,3,2,1:T(8,128)(2,1)S(1)}, u32[]{:S(2)}) copy-start(bf16[8,10,14,6,128]{4,0,3,2,1:T(8,128)(2,1)S(1)} %get-tuple-element.145) | copy-start | bytes 5160964
  883.8 4.2 copy-start.27
  883.8 4.2 copy-start.30
  883.8 4.2 copy-start.88
  883.8 4.3 copy-start.90
  895.7 222.2 %all-reduce.13.cloned.1.call-start = ((), (), s32[]{:S(2)}) async-start(), calls=%async_computation.9 | async-start | bytes 14155776 | tf_op jit(solution)/shard_map/psum | solution.py:277
  916.7 28.9 %copy-start.26 = (bf16[384,768]{1,0:T(8,128)(2,1)S(1)}, bf16[384,768]{1,0:T(8,128)(2,1)}, u32[]{:S(2)}) copy-start(bf16[384,768]{1,0:T(8,128)(2,1)} %param.22) | copy-start | bytes 1769476
  916.7 28.9 %copy-start.71 = (f32[768]{0:T(1024)S(1)}, f32[768]{0:T(1024)}, u32[]{:S(2)}) copy-start(f32[768]{0:T(1024)} %copy-done.70) | copy-start | bytes 9220
  916.7 378.7 %all-reduce.15.cloned.1.call-start = ((), (), s32[]{:S(2)}) async-start(), calls=%async_computation.10 | async-start | bytes 9437184 | tf_op jit(solution)/shard_map/psum | solution.py:264
  953.6 164.3 %copy-start.59 = (f32[768]{0:T(1024)S(1)}, f32[768]{0:T(1024)}, u32[]{:S(2)}) copy-start(f32[768]{0:T(1024)} %copy-done.58) | copy-start | bytes 9220
  953.6 167.6 %copy-start.75 = (f32[768]{0:T(1024)S(1)}, f32[768]{0:T(1024)}, u32[]{:S(2)}) copy-start(f32[768]{0:T(1024)} %copy-done.74) | copy-start | bytes 9220
  1117.9 3.3 copy-start.3
  1117.9 4.1 copy-start.9
  1117.9 4.1 copy-start.57
  1117.9 4.8 copy-start.73
  1138.8 5.2 copy-start.77
  1138.8 5.2 copy-start.78
  1138.8 52.4 %copy-start.69 = (f32[768]{0:T(1024)S(1)}, f32[768]{0:T(1024)}, u32[]{:S(2)}) copy-start(f32[768]{0:T(1024)} %copy-done.68) | copy-start | bytes 9220
  1191.2 104.2 %copy-start.23 = (bf16[192,1536]{1,0:T(8,128)(2,1)S(1)}, bf16[192,1536]{1,0:T(8,128)(2,1)}, u32[]{:S(2)}) copy-start(bf16[192,1536]{1,0:T(8,128)(2,1)} %param.31) | copy-start | bytes 1769476
  1191.2 104.2 %copy-start.61 = (f32[1536]{0:T(1024)S(1)}, f32[1536]{0:T(1024)}, u32[]{:S(2)}) copy-start(f32[1536]{0:T(1024)} %copy-done.60) | copy-start | bytes 18436
  1191.2 104.2 %copy-start.63 = (f32[1536]{0:T(1024)S(1)}, f32[1536]{0:T(1024)}, u32[]{:S(2)}) copy-start(f32[1536]{0:T(1024)} %copy-done.62) | copy-start | bytes 18436
  1191.2 104.2 %copy-start.76 = (f32[1536]{0:T(1024)S(1)}, f32[1536]{0:T(1024)}, u32[]{:S(2)}) copy-start(f32[1536]{0:T(1024)} %get-tuple-element.150) | copy-start | bytes 18436
  1201.9 96.2 %copy-start.80 = (f32[768]{0:T(1024)S(1)}, f32[768]{0:T(1024)}, u32[]{:S(2)}) copy-start(f32[768]{0:T(1024)} %get-tuple-element.153) | copy-start | bytes 9220
  (47 other events, 63.9 us)
Sparse Core Ops, SparseCore 0:
  34.7 107.1 reduce-scatter.4
  472.7 106.7 reduce-scatter.6
  622.3 31.2 all-reduce.10
  678.0 88.6 all-gather.2
  895.8 49.7 all-gather.4
  953.6 164.2 all-reduce.12
  1123.6 171.7 all-reduce.14
where the time goes:
time: 1320 us; the launch traced here: 1310 us
  waiting for transfers between devices  547 us (41%)
  local copies, waits for them, and re-layouts  399 us (30%)
  matrix products  157 us (12%)
  blocking collectives  108 us (8%)
  other arithmetic  71 us (5%)
  between operations  16.8 us (1%)
    unnamed x216, local copies, waits for them, and re-layouts  305 us
    psum x1, waiting for transfers between devices, body(): lax.psum((grad_kernel_first, grad_kernel_second, reduce_gain_term, reduce...  161 us
    unnamed x8, waiting for transfers between devices  106 us
    psum x1, waiting for transfers between devices, body(): lax.psum((grad_kernel_reduce, expand_rows, excite_down_grad, excite_down_...  93.5 us
    reduce_scatter x1, waiting for transfers between devices, body(): lax.psum_scatter(jnp.einsum('nhwc,cm->nhwm', rows, kernel_reduce, preferr...  91.7 us
    conv_general_dilated x8, matrix products, group_conv(): lax.conv_general_dilated(values, kernel, (1, 1), 'SAME', dimension_number...  47.5 us
    psum x1, blocking collectives, body(): lax.psum((grad_kernel_first, grad_kernel_second, reduce_gain_term, reduce...  47.2 us
    dot_general x36, matrix products, group_weight_grad(): jnp.einsum('nhwgi,nhwgo->igo', window, parted_grad, preferred_element_typ...  44.6 us
  transfers between devices with their start and end apart: 9, of which 9 were waited for; matrix products, arithmetic and copies ran while one was open for 11% of the time, Pallas kernels for 0%

commit v1 on v0

v1 whole, which is shorter than its diff:
```python
import functools
import jax
import jax.numpy as jnp
from jax import lax
from jax.experimental import pallas as pl
from jax.experimental.pallas import tpu as pltpu
from jax.sharding import PartitionSpec as P

INV_BETA = 1.0 / 1.16619037896906
ALPHA_RES = 0.2
GELU_SCALE = 1.7015
STD_EPSILON = 0.0001
ROOT = 0.7978845608028654
CUBIC = 0.044715
MESH = pl.DeviceIdType.MESH
F32 = jnp.float32
BF16 = jnp.bfloat16
LAG = 5


def gelu(v):
    return 0.5 * v * (1.0 + jnp.tanh(ROOT * v * (1.0 + CUBIC * v * v)))


def gelu_slope(v):
    square = v * v
    t = jnp.tanh(ROOT * v * (1.0 + CUBIC * square))
    return 0.5 * (1.0 + t) + 0.5 * v * (1.0 - t * t) * ROOT * (1.0 + 3.0 * CUBIC * square)


def split3(x):
    high = x.astype(BF16)
    rest = x - high.astype(F32)
    middle = rest.astype(BF16)
    low = (rest - middle.astype(F32)).astype(BF16)
    return jnp.concatenate([high, middle, low], axis=0)


def dot3(x, w, over):
    rows = x.shape[0]
    y = lax.dot_general(split3(x), w, (((1,), (over,)), ((), ())), preferred_element_type=F32)
    return y[:rows] + y[rows : 2 * rows] + y[2 * rows :]


def dot_nt(x, w):
    return lax.dot_general(x, w, (((1,), (1,)), ((), ())), preferred_element_type=F32)


def dot_tn(x, y):
    return lax.dot_general(x, y, (((0,), (0,)), ((), ())), preferred_element_type=F32)


def place():
    d, c = lax.axis_index("dp"), lax.axis_index("chan")
    xi, ci = c // 2, c % 2
    sib = (d, xi * 2 + (1 - ci))
    xn = (d, (1 - xi) * 2 + ci)
    dg = (d, (1 - xi) * 2 + (1 - ci))
    return d, c, xi, ci, sib, xn, dg


def greet(peers):
    barrier = pltpu.get_barrier_semaphore()
    for peer in peers:
        pl.semaphore_signal(barrier, inc=1, device_id=peer, device_id_type=MESH)
    pl.semaphore_wait(barrier, len(peers))


def remote(src, dst, send, recv, peer):
    return pltpu.make_async_remote_copy(
        src_ref=src, dst_ref=dst, send_sem=send, recv_sem=recv, device_id=peer, device_id_type=MESH
    )


def patches(ref, h, group, turned, width, taps):
    lanes = slice(group * taps, (group + 1) * taps)
    shifted = [[ref[h + u, v : v + width, :, lanes] for v in range(3)] for u in range(3)]
    parts = []
    for u in range(3):
        for v in range(3):
            if u == v:
                parts.append(shifted[u][v])
            else:
                parts.append(jnp.where(turned, shifted[v][u], shifted[u][v]))
    whole = jnp.concatenate(parts, axis=-1)
    return whole.reshape(whole.shape[0] * whole.shape[1], whole.shape[2])


def conv_row(ref, h, kernel_ref, turned, width, taps):
    groups = kernel_ref.shape[1] // taps
    outs = []
    for g in range(groups):
        outs.append(
            jnp.dot(
                patches(ref, h, g, turned, width, taps),
                kernel_ref[:, g * taps : (g + 1) * taps],
                preferred_element_type=F32,
            )
        )
    whole = jnp.concatenate(outs, axis=-1)
    return whole.reshape(width, -1, whole.shape[-1])


def forward_kernel(
    dims,
    img, og, rw, ew, dn, up, fw, sw, mvec, cvec, db, asp,
    o_preE, o_og, o_img, o_as2, o_kr, o_ke, o_preR, o_preF, o_preS, o_PR, o_PF, o_kt1, o_kt2,
    o_se, o_sum, o_str, o_ste, o_vb,
    imgb, ogb, kraw, ewb, dnb, upb, fraw, sraw, st, kr, ke, k1, k2, kt1, kt2,
    preR, s1, r1, PR, PF, preF, preS, as2, preE, acc, px, hx,
    loc_img, ss_img, rs_img, loc, ss, rs, ss_st, rs_st, ss1, rs1, ss2, rs2, sx, rx, outs,
):
    H, W, NI, CS, CH, MH, M, G = dims
    d, c, xi, ci, sib, xn, dg = place()
    greet((sib, xn, dg))
    mine = pl.ds(pl.multiple_of(ci * NI, NI), NI)
    theirs = pl.ds(pl.multiple_of((1 - ci) * NI, NI), NI)
    clan = pl.ds(pl.multiple_of(ci * CS, CS), CS)
    mlan = pl.ds(pl.multiple_of(xi * MH, MH), MH)
    olan = pl.ds(pl.multiple_of((1 - xi) * MH, MH), MH)

    def img_send(h):
        return remote(img.at[h, :, theirs, :], imgb.at[h, :, :, clan], ss_img.at[h], rs_img.at[h], sib)

    def img_local(h):
        return pltpu.make_async_copy(img.at[h, :, mine, :], imgb.at[h, :, :, clan], loc_img.at[h])

    locals_ = [
        pltpu.make_async_copy(rw, kraw.at[clan, :], loc.at[0]),
        pltpu.make_async_copy(ew.at[:, pl.ds(pl.multiple_of(xi * CH, CH), CH)], ewb.at[c], loc.at[1]),
        pltpu.make_async_copy(dn, dnb.at[clan, :], loc.at[2]),
        pltpu.make_async_copy(up, upb.at[:, clan], loc.at[3]),
        pltpu.make_async_copy(fw.at[:, mlan], fraw, loc.at[4]),
        pltpu.make_async_copy(sw.at[:, mlan], sraw, loc.at[5]),
        pltpu.make_async_copy(cvec, o_vb.at[:, clan], loc.at[6]),
        pltpu.make_async_copy(og.at[:, :, mine, :], ogb.at[:, :, :, clan], loc.at[7]),
    ]
    sends = [
        remote(rw, kraw.at[clan, :], ss.at[0], rs.at[0], sib),
        remote(ew.at[:, pl.ds(pl.multiple_of(xi * CH, CH), CH)], ewb.at[c], ss.at[1], rs.at[1], sib),
        remote(dn, dnb.at[clan, :], ss.at[2], rs.at[2], sib),
        remote(up, upb.at[:, clan], ss.at[3], rs.at[3], sib),
        remote(cvec, o_vb.at[:, clan], ss.at[4], rs.at[4], sib),
        remote(og.at[:, :, theirs, :], ogb.at[:, :, :, clan], ss.at[5], rs.at[5], sib),
        remote(ew.at[:, pl.ds(pl.multiple_of((1 - xi) * CH, CH), CH)], ewb.at[c], ss.at[6], rs.at[6], xn),
        remote(ew.at[:, pl.ds(pl.multiple_of((1 - xi) * CH, CH), CH)], ewb.at[c], ss.at[7], rs.at[7], dg),
    ]
    locals_[0].start()
    sends[0].start()

    def start_img(h, carry):
        img_local(h).start()
        img_send(h).start()
        return carry

    lax.fori_loop(0, H, start_img, 0)
    for k in (4, 5, 1, 6, 2, 3, 7):
        locals_[k].start()

    locals_[0].wait()
    own = kraw[clan, :].astype(F32)
    middle = jnp.mean(own, axis=0, keepdims=True)
    away = own - middle
    st[c] = jnp.concatenate(
        [middle, jnp.sum(away * away, axis=0, keepdims=True), jnp.zeros((6, M), F32)], axis=0
    )
    stats = [remote(st.at[c], st.at[c], ss_st.at[k], rs_st.at[c], peer) for k, peer in enumerate((sib, xn, dg))]
    for s in stats:
        s.start()
    for k in (6, 7, 1, 4, 2, 3, 5):
        sends[k].start()

    edge_w = jnp.zeros((W + 2, NI, MH), BF16)
    for ref in (PR, PF):
        ref[0] = edge_w
        ref[H + 1] = edge_w
        for h in range(1, H + 1):
            ref[h, 0] = edge_w[0]
            ref[h, W + 1] = edge_w[0]
    acc[...] = jnp.zeros_like(acc)

    def stat_of(q):
        return remote(st.at[q], st.at[q], ss_st.at[0], rs_st.at[q], sib)

    for k in (1, 2, 3):
        stat_of(lax.rem(c + k, 4)).wait_recv()
    count = CS
    mean = (st[0, 0:1] + st[1, 0:1] + st[2, 0:1] + st[3, 0:1]) * 0.25
    spread = jnp.zeros_like(mean)
    for q in range(4):
        gap = st[q, 0:1] - mean
        spread = spread + st[q, 1:2] + count * gap * gap
    rate = lax.rsqrt(spread + STD_EPSILON)
    o_str[...] = jnp.concatenate([mean, rate, jnp.zeros((6, M), F32)], axis=0)
    sends[0].wait_recv()

    def kr_block(j, carry):
        rows = pl.ds(pl.multiple_of(j * 128, 128), 128)
        kr[rows, :] = ((kraw[rows, :].astype(F32) - mean) * rate).astype(BF16)
        return carry

    lax.fori_loop(0, CH // 128, kr_block, 0)

    def s1_copy(h):
        return remote(s1.at[h], r1.at[h], ss1.at[h], rs1.at[h], xn)

    def reduce_row(h, carry):
        img_local(h).wait()
        img_send(h).wait_recv()
        scaled = (imgb[h].astype(F32) * INV_BETA).astype(BF16).reshape(W * NI, CH)
        s1[h] = (
            jnp.dot(scaled, kr[:, olan], preferred_element_type=F32).astype(BF16).reshape(W, NI, MH)
        )
        s1_copy(h).start()
        preR[h] = jnp.dot(scaled, kr[:, mlan], preferred_element_type=F32).reshape(W, NI, MH)
        return carry

    lax.fori_loop(0, H, reduce_row, 0)

    for k, raw, kern, trans in ((4, fraw, k1, kt1), (5, sraw, k2, kt2)):
        locals_[k].wait()
        for g in range(MH // G):
            lanes = slice(g * G, (g + 1) * G)
            w = raw[:, lanes].astype(F32)
            w = w - jnp.mean(w, axis=0, keepdims=True)
            w = w * lax.rsqrt(jnp.sum(w * w, axis=0, keepdims=True) + STD_EPSILON)
            kern[:, lanes] = w.astype(BF16)
            for tap in range(9):
                block = kern[(8 - tap) * G : (9 - tap) * G, lanes].astype(F32)
                trans[tap * G : (tap + 1) * G, lanes] = block.T.astype(BF16)

    locals_[1].wait()
    for k, peer in ((1, sib), (6, xn), (7, dg)):
        q = peer[1]
        remote(ewb.at[q], ewb.at[q], ss.at[k], rs.at[k], peer).wait_recv()
    quarter = ewb.shape[1]
    e_stat = []
    for j in range(CH // 128):
        lanes = slice(j * 128, (j + 1) * 128)
        blocks = [ewb[q, :, lanes].astype(F32) for q in range(4)]
        total = sum(jnp.sum(b, axis=0, keepdims=True) for b in blocks)
        e_mean = total / (4 * quarter)
        blocks = [b - e_mean for b in blocks]
        squares = sum(jnp.sum(b * b, axis=0, keepdims=True) for b in blocks)
        e_rate = lax.rsqrt(squares + STD_EPSILON)
        for q in range(4):
            ke[q * quarter : (q + 1) * quarter, lanes] = (blocks[q] * e_rate).astype(BF16)
        e_stat.append(jnp.concatenate([e_mean, e_rate, jnp.zeros((6, 128), F32)], axis=0))
    o_ste[xi] = jnp.concatenate(e_stat, axis=-1)
    ste_copy = remote(o_ste.at[xi], o_ste.at[xi], sx.at[2], rx.at[2], xn)
    ste_copy.start()

    turned = jnp.broadcast_to((asp[ci] > 0.5)[None], (W, NI, G))
    reduce_gain, reduce_bias = mvec[xi, 0:1], mvec[xi, 1:2]
    first_gain, first_bias = mvec[xi, 2:3], mvec[xi, 3:4]
    second_gain, second_bias = mvec[xi, 4:5], mvec[xi, 5:6]

    locals_[7].wait()
    sends[5].wait_recv()

    def s2_copy(h):
        return remote(as2.at[h, :, :, mlan], as2.at[h, :, :, mlan], ss2.at[h], rs2.at[h], xn)

    def s2_arrival(h):
        return remote(as2.at[h, :, :, olan], as2.at[h, :, :, olan], ss2.at[h], rs2.at[h], xn)

    def wave(t, carry):
        @pl.when(t < H)
        def _():
            s1_copy(t).wait_recv()
            pre = preR[t] + r1[t].astype(F32)
            preR[t] = pre
            PR[t + 1, 1 : W + 1] = (GELU_SCALE * gelu(pre * reduce_gain + reduce_bias)).astype(BF16)

        @pl.when((t >= 1) & (t <= H))
        def _():
            pre = conv_row(PR, t - 1, k1, turned, W, G)
            preF[t - 1] = pre
            PF[t, 1 : W + 1] = (GELU_SCALE * gelu(pre * first_gain + first_bias)).astype(BF16)

        @pl.when((t >= 2) & (t <= H + 1))
        def _():
            pre = conv_row(PF, t - 2, k2, turned, W, G)
            preS[t - 2] = pre
            as2[t - 2, :, :, mlan] = (GELU_SCALE * gelu(pre * second_gain + second_bias)).astype(BF16)
            s2_copy(t - 2).start()

        @pl.when(t >= LAG)
        def _():
            h = t - LAG
            s2_arrival(h).wait_recv()
            pre = jnp.dot(as2[h].reshape(W * NI, M), ke[...], preferred_element_type=F32).reshape(W, NI, CH)
            preE[h] = pre
            grad = ogb[h].astype(F32)
            acc[0] += jnp.sum(pre, axis=0)
            acc[1] += jnp.sum(grad, axis=0)
            acc[2] += jnp.sum(grad * pre, axis=0)

        return carry

    lax.fori_loop(0, H + LAG, wave, 0)

    pairs = (
        (preE, o_preE), (ogb, o_og), (imgb, o_img), (as2, o_as2), (kr, o_kr), (ke, o_ke), (preR, o_preR),
        (preF, o_preF), (preS, o_preS), (PR, o_PR), (PF, o_PF), (kt1, o_kt1), (kt2, o_kt2),
    )
    saves = [pltpu.make_async_copy(a, b, outs.at[k]) for k, (a, b) in enumerate(pairs)]
    for s in saves:
        s.start()

    for k in (2, 3, 6):
        locals_[k].wait()
    for k in (2, 3, 4):
        sends[k].wait_recv()
    gain, bias = o_vb[0:1, :], o_vb[1:2, :]
    up_bias, branch_scale = o_vb[2:3, :], o_vb[3:4, :]
    pixels = H * W
    sum_pre, sum_grad, sum_both = acc[0], acc[1], acc[2]
    pooled = gain * (sum_pre * (1.0 / pixels)) + bias
    px[xi] = dot3(pooled, dnb[...], 0)
    p_copy = remote(px.at[xi], px.at[xi], sx.at[0], rx.at[0], xn)
    p_copy.start()
    remote(px.at[1 - xi], px.at[1 - xi], sx.at[0], rx.at[0], xn).wait_recv()
    down = px[0] + px[1] + db[...]
    hidden = gelu(down)
    upper = dot3(hidden, upb[...], 0) + up_bias
    sigma = 1.0 / (1.0 + jnp.exp(-upper))
    gating = 2.0 * sigma
    grad_gating_raw = gain * sum_both + bias * sum_grad
    grad_upper = branch_scale * grad_gating_raw * 2.0 * sigma * (1.0 - sigma)
    hx[xi] = dot3(grad_upper, upb[...], 1)
    h_copy = remote(hx.at[xi], hx.at[xi], sx.at[1], rx.at[1], xn)
    h_copy.start()
    remote(hx.at[1 - xi], hx.at[1 - xi], sx.at[1], rx.at[1], xn).wait_recv()
    grad_down = (hx[0] + hx[1]) * gelu_slope(down)
    grad_pooled = dot3(grad_down, dnb[...], 1)
    scaled_gate = branch_scale * gating
    pool_part = grad_pooled * (1.0 / pixels)
    o_se[0] = scaled_gate
    o_se[1] = pool_part
    o_se[2] = pooled
    o_se[3] = grad_down
    o_se[4] = hidden
    o_se[5] = grad_upper
    gain_grad = jnp.sum(scaled_gate * sum_both + pool_part * sum_pre, axis=0, keepdims=True)
    bias_grad = jnp.sum(scaled_gate * sum_grad + grad_pooled, axis=0, keepdims=True)
    up_bias_grad = jnp.sum(grad_upper, axis=0, keepdims=True)
    skip_row = ALPHA_RES * jnp.sum(gating * grad_gating_raw, axis=0, keepdims=True)
    down_bias_grad = jnp.sum(grad_down, axis=0, keepdims=True)
    o_sum[...] = jnp.concatenate(
        [gain_grad, bias_grad, up_bias_grad, skip_row, down_bias_grad, jnp.zeros((3, CH), F32)], axis=0
    )

    remote(o_ste.at[1 - xi], o_ste.at[1 - xi], sx.at[2], rx.at[2], xn).wait_recv()
    for s in (ste_copy, p_copy, h_copy):
        s.wait_send()
    for s in sends + stats:
        s.wait_send()

    def drain(h, carry):
        img_send(h).wait_send()
        s1_copy(h).wait_send()
        s2_copy(h).wait_send()
        return carry

    lax.fori_loop(0, H, drain, 0)
    for s in saves:
        s.wait()


def backward_kernel(
    dims,
    i_preE, i_og, i_img, i_as2, i_kr, i_ke, i_preR, i_preF, i_preS, i_PR, i_PF, i_kt1, i_kt2,
    se, vb, mvec, asp,
    o_block, o_igrad, o_De, o_Dr, o_D1, o_D2, o_sum,
    preE, ogb, imgb, as2, kr, ke, preR, preF, preS, PR, PF, kt1, kt2,
    gpe, s3, r3, GS, GF, gpr, bst, igst, pbuf,
    ld, ldr, ss3, rs3, ss4, rs4, b_loc, b_ss, b_rs, g_loc, g_ss, g_rs,
):
    H, W, NI, CS, CH, MH, M, G = dims
    d, c, xi, ci, sib, xn, dg = place()
    pairs = (
        (i_kr, kr), (i_ke, ke), (i_kt1, kt1), (i_kt2, kt2), (i_PR, PR), (i_PF, PF), (i_as2, as2),
        (i_preR, preR), (i_preF, preF), (i_preS, preS),
    )
    loads = [pltpu.make_async_copy(a, b, ld.at[k]) for k, (a, b) in enumerate(pairs)]

    def row_loads(h):
        return [
            pltpu.make_async_copy(i_preE.at[h], preE.at[h], ldr.at[h, 0]),
            pltpu.make_async_copy(i_og.at[h], ogb.at[h], ldr.at[h, 1]),
            pltpu.make_async_copy(i_img.at[h], imgb.at[h], ldr.at[h, 2]),
        ]

    loads[1].start()
    for h in range(H):
        for s in row_loads(h):
            s.start()
    for k in (6, 9, 5, 3, 8, 4, 2, 7, 0):
        loads[k].start()

    greet((sib, xn))
    mine = pl.ds(pl.multiple_of(ci * NI, NI), NI)
    clan = pl.ds(pl.multiple_of(ci * CS, CS), CS)
    slan = pl.ds(pl.multiple_of((1 - ci) * CS, CS), CS)
    mlan = pl.ds(pl.multiple_of(xi * MH, MH), MH)
    olan = pl.ds(pl.multiple_of((1 - xi) * MH, MH), MH)
    edge_w = jnp.zeros((W + 2, NI, MH), BF16)
    for ref in (GS, GF):
        ref[0] = edge_w
        ref[H + 1] = edge_w
        for h in range(1, H + 1):
            ref[h, 0] = edge_w[0]
            ref[h, W + 1] = edge_w[0]
    o_sum[...] = jnp.zeros_like(o_sum)

    gain, bias = vb[0:1, :], vb[1:2, :]
    scaled_gate, pool_part = se[0], se[1]
    slots = bst.shape[0]

    def block_local(h):
        return pltpu.make_async_copy(bst.at[lax.rem(h, slots), :, :, clan], o_block.at[h, :, mine, :], b_loc.at[h])

    def block_send(h):
        return remote(
            bst.at[lax.rem(h, slots), :, :, slan], o_block.at[h, :, mine, :], b_ss.at[h], b_rs.at[h], sib
        )

    def igrad_local(h):
        return pltpu.make_async_copy(igst.at[lax.rem(h, slots), :, :, clan], o_igrad.at[h, :, mine, :], g_loc.at[h])

    def igrad_send(h):
        return remote(
            igst.at[lax.rem(h, slots), :, :, slan], o_igrad.at[h, :, mine, :], g_ss.at[h], g_rs.at[h], sib
        )

    def s3_copy(h):
        return remote(s3.at[h], r3.at[h], ss3.at[h], rs3.at[h], xn)

    loads[1].wait()

    def expand_row(h, carry):
        for s in row_loads(h):
            s.wait()

        @pl.when(h >= slots)
        def _():
            block_local(h - slots).wait()
            block_send(h - slots).wait_send()

        pre = preE[h]
        out = pre * gain + bias
        bst[lax.rem(h, slots)] = (imgb[h].astype(F32) + out * scaled_gate).astype(BF16)
        block_local(h).start()
        block_send(h).start()
        grad = ogb[h].astype(F32) * scaled_gate + pool_part
        piece = (grad * gain).astype(BF16).reshape(W * NI, CH)
        gpe[h] = piece.reshape(W, NI, CH)
        s3[h] = dot_nt(piece, ke[olan, :]).astype(BF16).reshape(W, NI, MH)
        s3_copy(h).start()
        preE[h, :, :, 0:MH] = dot_nt(piece, ke[mlan, :]).reshape(W, NI, MH)
        return carry

    lax.fori_loop(0, H, expand_row, 0)

    loads[6].wait()
    step = 128

    def expand_kernel_grad(j, carry):
        lanes = pl.ds(pl.multiple_of(j * step, step), step)
        left = as2[:, :, :, lanes].reshape(H * W * NI, step)
        o_De[lanes, :] = dot_tn(left, gpe[...].reshape(H * W * NI, CH)).astype(BF16)
        return carry

    lax.fori_loop(0, M // step, expand_kernel_grad, 0)

    for k in (9, 5, 3, 8, 4, 2, 7, 0):
        loads[k].wait()
    turned = jnp.broadcast_to((asp[ci] > 0.5)[None], (W, NI, G))
    reduce_gain, reduce_bias = mvec[xi, 0:1], mvec[xi, 1:2]
    first_gain, first_bias = mvec[xi, 2:3], mvec[xi, 3:4]
    second_gain, second_bias = mvec[xi, 4:5], mvec[xi, 5:6]

    def s4_copy(h):
        return remote(gpr.at[h, :, :, mlan], gpr.at[h, :, :, mlan], ss4.at[h], rs4.at[h], xn)

    def s4_arrival(h):
        return remote(gpr.at[h, :, :, olan], gpr.at[h, :, :, olan], ss4.at[h], rs4.at[h], xn)

    def tally(row, grad, pre):
        flat = (grad * pre).reshape(W * NI, MH)
        o_sum[row : row + 1, :] += jnp.sum(flat, axis=0, keepdims=True)
        o_sum[row + 1 : row + 2, :] += jnp.sum(grad.reshape(W * NI, MH), axis=0, keepdims=True)

    def wave(t, carry):
        @pl.when(t < H)
        def _():
            s3_copy(t).wait_recv()
            cot = (preE[t, :, :, 0:MH] + r3[t].astype(F32)).astype(BF16).astype(F32)
            pre = preS[t]
            grad = cot * (GELU_SCALE * gelu_slope(pre * second_gain + second_bias))
            tally(4, grad, pre)
            GS[t + 1, 1 : W + 1] = (grad * second_gain).astype(BF16)

        @pl.when((t >= 1) & (t <= H))
        def _():
            cot = conv_row(GS, t - 1, kt2, turned, W, G)
            pre = preF[t - 1]
            grad = cot * (GELU_SCALE * gelu_slope(pre * first_gain + first_bias))
            tally(2, grad, pre)
            GF[t, 1 : W + 1] = (grad * first_gain).astype(BF16)

        @pl.when((t >= 2) & (t <= H + 1))
        def _():
            cot = conv_row(GF, t - 2, kt1, turned, W, G)
            pre = preR[t - 2]
            grad = cot * (GELU_SCALE * gelu_slope(pre * reduce_gain + reduce_bias))
            tally(0, grad, pre)
            gpr[t - 2, :, :, mlan] = (grad * reduce_gain).astype(BF16)
            s4_copy(t - 2).start()

        @pl.when(t >= LAG)
        def _():
            h = t - LAG
            s4_arrival(h).wait_recv()

            @pl.when(h >= slots)
            def _():
                igrad_local(h - slots).wait()
                igrad_send(h - slots).wait_send()

            rows = dot_nt(gpr[h].reshape(W * NI, M), kr[...]).reshape(W, NI, CH)
            igst[lax.rem(h, slots)] = ogb[h].astype(F32) + INV_BETA * rows
            igrad_local(h).start()
            igrad_send(h).start()

        return carry

    lax.fori_loop(0, H + LAG, wave, 0)

    for act, cot, dst in ((PF, GS, o_D2), (PR, GF, o_D1)):
        for g in range(MH // G):
            total = None
            for part in range(2):
                first = part * (H // 2)

                def fill(h, carry):
                    at = pl.ds(pl.multiple_of(h * (W * NI), W * NI), W * NI)
                    pbuf[at, :] = patches(act, first + h, g, turned, W, G)
                    return carry

                lax.fori_loop(0, H // 2, fill, 0)
                right = cot[1 + first : 1 + first + H // 2, 1 : W + 1, :, g * G : (g + 1) * G]
                term = dot_tn(right.reshape(H // 2 * W * NI, G), pbuf[...])
                total = term if total is None else total + term
            dst[g * G : (g + 1) * G, :] = total.astype(BF16)

    def reduce_kernel_grad(j, carry):
        lanes = pl.ds(pl.multiple_of(j * step, step), step)
        left = (imgb[:, :, :, lanes].astype(F32) * INV_BETA).astype(BF16).reshape(H * W * NI, step)
        o_Dr[lanes, :] = dot_tn(left, gpr[...].reshape(H * W * NI, M)).astype(BF16)
        return carry

    lax.fori_loop(0, CH // step, reduce_kernel_grad, 0)

    def drain(h, carry):
        s3_copy(h).wait_send()
        s4_copy(h).wait_send()
        block_send(h).wait_recv()
        igrad_send(h).wait_recv()
        return carry

    lax.fori_loop(0, H, drain, 0)
    for h in range(H - slots, H):
        block_local(h).wait()
        block_send(h).wait_send()
        igrad_local(h).wait()
        igrad_send(h).wait_send()


def standard_grad(summed, centered, rate, column_sum, column_cross, fan_in):
    return rate * (summed - column_sum / fan_in) - rate * rate * rate * centered * column_cross


def standardize(weight, axes):
    middle = jnp.mean(weight, axis=axes, keepdims=True)
    centered = weight - middle
    spread = jnp.sum(centered * centered, axis=axes, keepdims=True)
    return centered * lax.rsqrt(spread + STD_EPSILON)


def body(
    images, aspect, reduce_weight, reduce_gain, reduce_bias, first_weight, first_gain, first_bias,
    second_weight, second_gain, second_bias, expand_weight, expand_gain, expand_bias, excite_down,
    excite_down_bias, excite_up, excite_up_bias, skip_gain, out_grad,
):
    N, H, W, CS = images.shape
    M = reduce_weight.shape[1]
    G = first_weight.shape[2]
    NI, MH, CH = N // 2, M // 2, 2 * CS
    dims = (H, W, NI, CS, CH, MH, M, G)
    quarter = expand_weight.shape[0]
    index = lax.axis_index("chan")
    img = jnp.transpose(images, (1, 2, 0, 3))
    og = jnp.transpose(out_grad, (1, 2, 0, 3))
    fw = first_weight.reshape(9 * G, M)
    sw = second_weight.reshape(9 * G, M)
    zero = jnp.zeros((M,), F32)
    mvec = jnp.stack([reduce_gain, reduce_bias, first_gain, first_bias, second_gain, second_bias, zero, zero])
    mvec = jnp.transpose(mvec.reshape(8, 2, MH), (1, 0, 2))
    cz = jnp.zeros((CS,), F32)
    cvec = jnp.stack(
        [expand_gain, expand_bias, excite_up_bias, jnp.broadcast_to(ALPHA_RES * skip_gain, (CS,)), cz, cz, cz, cz]
    )
    asp = jnp.broadcast_to(aspect.astype(F32).reshape(2, NI, 1), (2, NI, G))
    db = excite_down_bias.reshape(1, M)

    anyspec = pl.BlockSpec(memory_space=pl.ANY)
    vm = pl.BlockSpec(memory_space=pltpu.VMEM)
    S = jax.ShapeDtypeStruct
    V = pltpu.VMEM
    DMA = pltpu.SemaphoreType.DMA
    big = (
        S((H, W, NI, CH), F32), S((H, W, NI, CH), BF16), S((H, W, NI, CH), BF16), S((H, W, NI, M), BF16),
        S((CH, M), BF16), S((M, CH), BF16), S((H, W, NI, MH), F32), S((H, W, NI, MH), F32), S((H, W, NI, MH), F32),
        S((H + 2, W + 2, NI, MH), BF16), S((H + 2, W + 2, NI, MH), BF16), S((9 * G, MH), BF16), S((9 * G, MH), BF16),
    )
    small = (S((6, NI, CH), F32), S((8, CH), F32), S((8, M), F32), S((2, 8, CH), F32), S((8, CH), F32))
    fwd = pl.pallas_call(
        functools.partial(forward_kernel, dims),
        name="forward",
        out_shape=big + small,
        in_specs=[anyspec] * 8 + [vm, anyspec, vm, vm],
        out_specs=[anyspec] * 13 + [vm] * 5,
        scratch_shapes=[
            V((H, W, NI, CH), BF16), V((H, W, NI, CH), BF16), V((CH, M), BF16), V((4, quarter, CH), BF16),
            V((CH, M), BF16), V((M, CH), BF16), V((9 * G, MH), BF16), V((9 * G, MH), BF16), V((4, 8, M), F32),
            V((CH, M), BF16), V((M, CH), BF16), V((9 * G, MH), BF16), V((9 * G, MH), BF16), V((9 * G, MH), BF16),
            V((9 * G, MH), BF16),
            V((H, W, NI, MH), F32), V((H, W, NI, MH), BF16), V((H, W, NI, MH), BF16),
            V((H + 2, W + 2, NI, MH), BF16), V((H + 2, W + 2, NI, MH), BF16),
            V((H, W, NI, MH), F32), V((H, W, NI, MH), F32), V((H, W, NI, M), BF16), V((H, W, NI, CH), F32),
            V((3, NI, CH), F32), V((2, NI, M), F32), V((2, NI, M), F32),
            DMA((H,)), DMA((H,)), DMA((H,)), DMA((8,)), DMA((8,)), DMA((8,)), DMA((3,)), DMA((4,)),
            DMA((H,)), DMA((H,)), DMA((H,)), DMA((H,)), DMA((3,)), DMA((3,)), DMA((13,)),
        ],
        compiler_params=pltpu.CompilerParams(collective_id=0, has_side_effects=True, vmem_limit_bytes=62 << 20),
    )(img, og, reduce_weight, expand_weight, excite_down, excite_up, fw, sw, mvec, cvec, db, asp)
    saved, (se, fsum, stat_r, stat_e, vb) = fwd[:13], fwd[13:]

    slots = 2
    block_out, images_grad, De, Dr, D1, D2, bsum = pl.pallas_call(
        functools.partial(backward_kernel, dims),
        name="backward",
        out_shape=(
            S((H, W, N, CS), BF16), S((H, W, N, CS), F32), S((M, CH), BF16), S((CH, M), BF16),
            S((MH, 9 * G), BF16), S((MH, 9 * G), BF16), S((8, MH), F32),
        ),
        in_specs=[anyspec] * 13 + [vm] * 4,
        out_specs=[anyspec] * 2 + [vm] * 5,
        scratch_shapes=[
            V((H, W, NI, CH), F32), V((H, W, NI, CH), BF16), V((H, W, NI, CH), BF16), V((H, W, NI, M), BF16),
            V((CH, M), BF16), V((M, CH), BF16), V((H, W, NI, MH), F32), V((H, W, NI, MH), F32), V((H, W, NI, MH), F32),
            V((H + 2, W + 2, NI, MH), BF16), V((H + 2, W + 2, NI, MH), BF16), V((9 * G, MH), BF16), V((9 * G, MH), BF16),
            V((H, W, NI, CH), BF16), V((H, W, NI, MH), BF16), V((H, W, NI, MH), BF16),
            V((H + 2, W + 2, NI, MH), BF16), V((H + 2, W + 2, NI, MH), BF16), V((H, W, NI, M), BF16),
            V((slots, W, NI, CH), BF16), V((slots, W, NI, CH), F32), V((H // 2 * W * NI, 9 * G), BF16),
            DMA((10,)), DMA((H, 3)), DMA((H,)), DMA((H,)), DMA((H,)), DMA((H,)),
            DMA((H,)), DMA((H,)), DMA((H,)), DMA((H,)), DMA((H,)), DMA((H,)),
        ],
        compiler_params=pltpu.CompilerParams(collective_id=1, has_side_effects=True, vmem_limit_bytes=63 << 20),
    )(*saved, se, vb, mvec, asp)

    xi, ci = index // 2, index % 2
    both = ("dp", "chan")
    def put(v, at, length, axis):
        shape = list(v.shape)
        shape[axis] = length
        return lax.dynamic_update_slice_in_dim(jnp.zeros(shape, v.dtype), v, at, axis)

    Dr, De, D1, D2 = (v.astype(F32) for v in (Dr, De, D1, D2))
    dr_all = lax.psum(put(Dr, xi * CH, 2 * CH, 0), both)
    de_all = lax.psum(put(De, xi * CH, 2 * CH, 1), both)
    d12 = lax.psum(put(jnp.stack([D1, D2]), xi * MH, M, 1), both)
    bs = lax.psum(put(bsum, xi * MH, M, 1), both)
    fs = lax.psum(put(fsum, xi * CH, 2 * CH, 1), both)
    ddown = lax.psum(put(jnp.dot(se[2].T, se[3], precision=lax.Precision.HIGHEST), xi * CH, 2 * CH, 0), both)
    dup = lax.psum(put(jnp.dot(se[4].T, se[5], precision=lax.Precision.HIGHEST), xi * CH, 2 * CH, 1), both)

    fan_r = 4 * CS
    r_mean, r_rate = stat_r[0:1], stat_r[1:2]
    own_rows = reduce_weight.astype(F32) - r_mean
    raw_all = lax.all_gather(reduce_weight, "chan", axis=0, tiled=True).astype(F32) - r_mean
    r_sum = jnp.sum(dr_all, axis=0, keepdims=True)
    r_cross = jnp.sum(dr_all * raw_all, axis=0, keepdims=True)
    my_dr = lax.dynamic_slice_in_dim(dr_all, index * CS, CS, 0)
    reduce_weight_grad = standard_grad(my_dr, own_rows, r_rate, r_sum, r_cross, fan_r)
    e_mean = jnp.concatenate([stat_e[0, 0:1], stat_e[1, 0:1]], axis=1)
    e_rate = jnp.concatenate([stat_e[0, 1:2], stat_e[1, 1:2]], axis=1)
    e_own = expand_weight.astype(F32) - e_mean
    e_all = lax.all_gather(expand_weight, "chan", axis=0, tiled=True).astype(F32) - e_mean
    e_sum = jnp.sum(de_all, axis=0, keepdims=True)
    e_cross = jnp.sum(de_all * e_all, axis=0, keepdims=True)
    my_de = lax.dynamic_slice_in_dim(de_all, index * quarter, quarter, 0)
    expand_weight_grad = standard_grad(my_de, e_own, e_rate, e_sum, e_cross, 4 * quarter)
    def group_grad(weight, dt):
        total = jnp.transpose(dt).reshape(3, 3, G, M)
        _, pull = jax.vjp(lambda w: standardize(w, (0, 1, 2)), weight.astype(F32))
        return pull(total)[0]

    first_weight_grad = group_grad(first_weight, d12[0])
    second_weight_grad = group_grad(second_weight, d12[1])
    my = lambda v: lax.dynamic_slice_in_dim(v, index * CS, CS, 0)
    back = lambda v: jnp.transpose(v, (2, 0, 1, 3))
    return (
        back(block_out), back(images_grad), reduce_weight_grad, bs[0], bs[1], first_weight_grad, bs[2], bs[3],
        second_weight_grad, bs[4], bs[5], expand_weight_grad, my(fs[0]), my(fs[1]),
        lax.dynamic_slice_in_dim(ddown, index * CS, CS, 0), fs[4][:M], lax.dynamic_slice_in_dim(dup, index * CS, CS, 1),
        my(fs[2]), jnp.sum(fs[3]).reshape(1),
    )


def solution(mesh):
    rows = P("dp", None, None, "chan")
    placed = (
        rows, P("dp"), P("chan", None), P(), P(), P(), P(), P(), P(), P(), P(), P("chan", None), P("chan"), P("chan"),
        P("chan", None), P(), P(None, "chan"), P("chan"), P(), rows,
    )
    results = (
        rows, rows, P("chan", None), P(), P(), P(), P(), P(), P(), P(), P(), P("chan", None), P("chan"), P("chan"),
        P("chan", None), P(), P(None, "chan"), P("chan"), P(),
    )
    return jax.shard_map(body, mesh=mesh, in_specs=placed, out_specs=results, check_vma=False)
```

time: 1320 us -> 844 us (0.64)
  local copies, waits for them, and re-layouts: 399 us -> 47.7 us
  Pallas kernels: 0 us -> 209 us
  matrix products: 157 us -> 4.11 us
  blocking collectives: 108 us -> 0 us
  other arithmetic: 71 us -> 29.3 us
  waiting for transfers between devices: 547 us -> 523 us
    unnamed x216 -> x62, local copies, waits for them, and re-layouts: 305 us -> 15 us
    psum x3 -> x2, waiting for transfers between devices: 286 us -> 522 us  [the longest x1 410 us: body(): dr_all = lax.psum(put(Dr, xi * CH, 2 * CH, 0), both)]
    pallas_call x0 -> x2, Pallas kernels: none -> 209 us  [the longest x1 108 us: body(): pl.pallas_call(functools.partial(forward_kernel, dims), name='forward', o...]
    psum x4 -> x0, blocking collectives: 108 us -> none  [the longest x1 47.2 us: body(): lax.psum((grad_kernel_first, grad_kernel_second, reduce_gain_term, reduce...]
    dot_general x48 -> x2, matrix products: 110 us -> 4.11 us  [the longest x1 2.06 us: body(): jnp.dot(se[4].T, se[5], precision=lax.Precision.HIGHEST)]
    unnamed x8 -> x4, waiting for transfers between devices: 106 us -> 0.91 us
    reduce_scatter x1 -> x0, waiting for transfers between devices: 91.7 us -> none  [body(): lax.psum_scatter(jnp.einsum('nhwc,cm->nhwm', rows, kernel_reduce, preferr...]
    conv_general_dilated x8 -> x0, matrix products: 47.5 us -> none  [group_conv(): lax.conv_general_dilated(values, kernel, (1, 1), 'SAME', dimension_number...]
  transfers between devices with their start and end apart: 9 -> 4, of which waited for: 9 -> 2; matrix products, arithmetic and copies ran while one was open for 11% -> 5% of each run, Pallas kernels for 0% -> 0%
where the time goes in v1:
time: 844 us; the launch traced here: 830 us
  waiting for transfers between devices  523 us (62%)
  Pallas kernels  209 us (25%)
  local copies, waits for them, and re-layouts  47.7 us (6%)
  other arithmetic  29.3 us (3%)
  between operations  16.8 us (2%)
    psum x1, waiting for transfers between devices, body(): dr_all = lax.psum(put(Dr, xi * CH, 2 * CH, 0), both)  410 us
    psum x1, waiting for transfers between devices, body(): bs = lax.psum(put(bsum, xi * MH, M, 1), both)  112 us
    pallas_call x1, Pallas kernels, body(): pl.pallas_call(functools.partial(forward_kernel, dims), name='forward', o...  108 us
    pallas_call x1, Pallas kernels, body(): pl.pallas_call(functools.partial(backward_kernel, dims), name='backward',...  100 us
  transfers between devices with their start and end apart: 4, of which 2 were waited for; matrix products, arithmetic and copies ran while one was open for 5% of the time, Pallas kernels for 0%

profile of v1, /device:TPU:0, one launch (start us, length us, event | category | flops | bytes accessed | tf_op | source)
XLA Modules:
  0.0 829.5 jit_solution(10063380638170072854)
XLA Ops:
  8.1 0.7 stack.53
  8.8 0.7 stack.54
  9.5 0.7 stack.55
  10.2 0.7 stack.56
  10.9 0.7 stack.57
  11.6 0.7 stack.58
  12.3 0.7 stack.61
  12.9 0.7 stack.62
  13.6 0.7 stack.63
  15.0 1.3 reshape.177.db
  16.2 0.7 convert_element_type.29
  17.0 0.6 stack.65.cvec
  17.6 0.6 stack.60
  18.3 0.7 broadcast_in_dim.37.asp
  18.9 108.3 %forward.1 = (f32[10,14,16,768]{3,2,1,0:T(8,128)}, bf16[10,14,16,768]{3,2,1,0:T(8,128)(2,1)}, bf16[10,14,16,768]{3,2,1,0:T(8,128)(2,1)}, bf16[10,14,16,768]{3,2,...) custom-call(bf16[10,14,32,384]{3,2,1,0:T(8,128)(2,1)} %bitcast.53, ...), custom_call_target="tpu_custom_call" | custom-call | tf_op jit(solution)/shard_map/forward/pallas_call | solution.py:629
  127.2 100.4 %backward.1 = (bf16[10,14,32,384]{3,2,1,0:T(8,128)(2,1)}, f32[10,14,32,384]{3,2,1,0:T(8,128)}, bf16[768,768]{1,0:T(8,128)(2,1)}, bf16[768,768]{1,0:T(8,128)(2,1)...) custom-call(f32[10,14,16,768]{3,2,1,0:T(8,128)} %get-tuple-element.44.i_preE, ...), custom_call_target="tpu_custom_call" | custom-call | tf_op jit(solution)/shard_map/backward/pallas_call | solution.py:652
  227.7 0.8 constant_dynamic-update-slice_fusion.1
  228.5 0.6 copy-done.19
  229.2 0.3 broadcast.73.clone.1
  229.5 2.1 convolution_dynamic-update-slice_fusion.1
  231.6 2.1 copy-done.9
  233.7 0.5 broadcast_in_dim.39
  234.1 0.7 copy-done.15
  235.4 0.6 broadcast.77.clone
  236.3 2.3 copy-done.5
  238.6 0.8 copy-done.14
  239.4 0.5 convert_dynamic-update-slice_fusion.1
  239.9 0.6 broadcast.77.clone.1
  240.5 2.1 convolution_dynamic-update-slice_fusion
  242.6 1.1 copy-done.7
  243.6 1.4 copy-done.8
  245.1 0.5 all-gather.3.cloned.1.call-update
  245.8 0.4 all-gather.5.cloned.1.call-update
  246.5 0.3 convert_reduce_fusion.1
  247.0 0.3 convert_reduce_fusion
  247.3 1.4 slice_reduce_fusion.11
  248.8 0.8 slice_reduce_fusion.10
  249.6 0.6 multiply_multiply_fusion
  250.2 0.6 maximum_reduce_fusion
  250.8 111.8 %all-reduce.5.cloned.1.call-done = (f32[8,768]{1,0:T(8,128)}, f32[8,1536]{1,0:T(8,128)}) async-done(((f32[8,768]{1,0:T(8,128)}, f32[8,1536]{1,0:T(8,128)}), (f32[8,768]{1,0:T(8,128)}, f32[8,1536]{1,0:T(8,128)})) %all-reduce.5.cloned.1.call-update) | async-done | bytes 73744 | tf_op jit(solution)/shard_map/psum | solution.py:685
  362.6 1.6 slice_reduce_fusion
  364.2 1.6 slice_reduce_fusion.2
  365.8 0.6 fusion.23
  366.4 0.6 fusion.21
  367.0 409.8 %all-reduce.7.cloned.1.call-done = (f32[1536,768]{1,0:T(8,128)}, f32[2,768,1152]{2,1,0:T(8,128)}, f32[768,1536]{1,0:T(8,128)}, f32[1536,768]{1,0:T(8,128)}, f32[768,1536]{1,0:T(8,128)}) async-done(((f32[1536,768]{1,0:T(8,128)}, f32[2,768,1152]{2,1,0:T(8,128)}, f32[768,1536]{1,0:T(8,128)}, f32[1536,768]{1,0:T(8,128)}, f32[768,1536]{1,0:T(8,128)}), (f32[1536,768]{1,0:T(8,128)}, f32[2,768,1152]{2,1,0:T(8,128)}, ...) | async-done | bytes 25952272 | tf_op jit(solution)/shard_map/psum | solution.py:682
  776.8 5.3 slice_bitcast_fusion
  782.2 2.9 copy.39
  785.1 3.3 copy.40
  788.5 4.6 fusion.25
  793.1 0.6 broadcast_multiply_fusion.3
  793.7 0.7 fusion.6
  794.5 0.8 fusion.10
  795.3 0.6 copy-done.4
  795.9 0.7 fusion.8
  796.7 0.8 fusion.11
  797.5 2.6 broadcast_add_fusion.1
  800.1 2.6 broadcast_add_fusion
  802.7 3.9 fusion.24
  806.8 2.4 constant_dynamic-slice_fusion.2
  809.2 2.5 constant_dynamic-slice_fusion.1
  811.8 2.7 multiply_subtract_fusion.1
  814.5 2.7 multiply_subtract_fusion
  817.3 1.8 copy.58
  819.0 2.9 copy.59
  (77 shorter events, 2.1 us)
Async XLA Ops:
  8.0 354.6 %all-reduce.5.cloned.1.call-start = ((), (), s32[]{:S(2)}) async-start(), calls=%async_computation.2 | async-start | bytes 147456 | tf_op jit(solution)/shard_map/psum | solution.py:685
  127.2 101.3 %copy-start.23 = (f32[8,768]{1,0:T(8,128)S(1)}, f32[8,768]{1,0:T(8,128)}, u32[]{:S(2)}) copy-start(f32[8,768]{1,0:T(8,128)} %get-tuple-element.68) | copy-start | bytes 73732
  227.7 1.8 copy-start.17
  228.4 0.6 copy-start.19
  228.5 0.6 copy-start.18
  229.1 547.7 %all-reduce.7.cloned.1.call-start = ((), (), s32[]{:S(2)}) async-start(), calls=%async_computation.3 | async-start | bytes 51904512 | tf_op jit(solution)/shard_map/psum | solution.py:682
  231.6 2.1 copy-start.9
  233.7 1.2 copy-start.15
  233.7 1.4 copy-start.16
  235.4 3.2 copy-start.5
  236.0 2.6 copy-start.13
  236.0 3.4 copy-start.14
  239.9 2.7 copy-start.6
  239.9 3.7 copy-start.7
  242.5 2.4 copy-start.8
  245.0 1.5 copy-start.1
  245.0 2.0 copy-start.3
  245.0 543.4 %all-gather.3.cloned.1.call-start = ((), (), s32[]{:S(2)}) async-start(), calls=%async_computation | async-start | bytes 2949120 | tf_op jit(solution)/shard_map/all_gather | solution.py:693
  245.6 557.1 %all-gather.5.cloned.1.call-start = ((), (), s32[]{:S(2)}) async-start(), calls=%async_computation.1 | async-start | bytes 2949120 | tf_op jit(solution)/shard_map/all_gather | solution.py:701
  788.4 5.3 copy-start
  788.4 5.3 copy-start.2
  794.4 1.5 copy-start.4
  806.7 5.1 copy-start.10
  806.7 5.1 copy-start.20
  806.7 5.1 copy-start.24
  806.7 5.0 copy-start.25
  806.7 5.0 copy-start.26
  806.7 5.0 copy-start.27
  806.7 7.8 copy-start.11
  806.8 7.8 copy-start.21
  806.8 7.7 copy-start.22
  809.2 9.8 %slice-start = ((s8[6881280]{0:T(1024)(128)(4,1)}), s8[4194304]{0:T(1024)(128)(4,1)S(1)}, s32[]{:S(2)}) async-start(s8[6881280]{0:T(1024)(128)(4,1)} %bitcast.49), calls=%async_computation.4 | async-start | bytes 8388608
  811.7 5.5 copy-start.12
  814.5 4.5 slice-start.1
Sparse Core Ops, SparseCore 0:
  229.2 133.3 all-reduce.4
  369.6 407.1 all-reduce.6
Sparse Core Ops, SparseCore 1:
  247.1 24.3 all-gather.2
  273.0 24.0 all-gather.4

commit v2 on v1

--- a/solution.py
+++ b/solution.py
@@ -105,8 +105,8 @@
     dims,
     img, og, rw, ew, dn, up, fw, sw, mvec, cvec, db, asp,
     o_preE, o_og, o_img, o_as2, o_kr, o_ke, o_preR, o_preF, o_preS, o_PR, o_PF, o_kt1, o_kt2,
-    o_se, o_sum, o_str, o_ste, o_vb,
-    imgb, ogb, kraw, ewb, dnb, upb, fraw, sraw, st, kr, ke, k1, k2, kt1, kt2,
+    o_kraw, o_ewb, o_rawt, o_fac, o_se, o_sum, o_str, o_ste, o_vb,
+    imgb, ogb, kraw, ewb, dnb, upb, fraw, sraw, st, kr, ke, k1, k2, kt1, kt2, rawt, fac,
     preR, s1, r1, PR, PF, preF, preS, as2, preE, acc, px, hx,
     loc_img, ss_img, rs_img, loc, ss, rs, ss_st, rs_st, ss1, rs1, ss2, rs2, sx, rx, outs,
 ):
@@ -217,7 +217,7 @@
 
     lax.fori_loop(0, H, reduce_row, 0)
 
-    for k, raw, kern, trans in ((4, fraw, k1, kt1), (5, sraw, k2, kt2)):
+    for k, raw, kern, trans, flip in ((4, fraw, k1, kt1, rawt.at[0]), (5, sraw, k2, kt2, rawt.at[1])):
         locals_[k].wait()
         for g in range(MH // G):
             lanes = slice(g * G, (g + 1) * G)
@@ -228,6 +228,8 @@
             for tap in range(9):
                 block = kern[(8 - tap) * G : (9 - tap) * G, lanes].astype(F32)
                 trans[tap * G : (tap + 1) * G, lanes] = block.T.astype(BF16)
+                block = raw[tap * G : (tap + 1) * G, lanes].astype(F32)
+                flip[lanes, tap * G : (tap + 1) * G] = block.T.astype(BF16)
 
     locals_[1].wait()
     for k, peer in ((1, sib), (6, xn), (7, dg)):
@@ -303,6 +305,7 @@
     pairs = (
         (preE, o_preE), (ogb, o_og), (imgb, o_img), (as2, o_as2), (kr, o_kr), (ke, o_ke), (preR, o_preR),
         (preF, o_preF), (preS, o_preS), (PR, o_PR), (PF, o_PF), (kt1, o_kt1), (kt2, o_kt2),
+        (kraw, o_kraw), (ewb, o_ewb), (rawt, o_rawt),
     )
     saves = [pltpu.make_async_copy(a, b, outs.at[k]) for k, (a, b) in enumerate(pairs)]
     for s in saves:
@@ -338,10 +341,11 @@
     pool_part = grad_pooled * (1.0 / pixels)
     o_se[0] = scaled_gate
     o_se[1] = pool_part
-    o_se[2] = pooled
-    o_se[3] = grad_down
-    o_se[4] = hidden
-    o_se[5] = grad_upper
+    for s in range(2):
+        shard = slice(s * CS, (s + 1) * CS)
+        fac[s] = jnp.concatenate([pooled[:, shard], grad_down, hidden, grad_upper[:, shard]], axis=-1).astype(BF16)
+    fac_save = pltpu.make_async_copy(fac, o_fac, outs.at[16])
+    fac_save.start()
     gain_grad = jnp.sum(scaled_gate * sum_both + pool_part * sum_pre, axis=0, keepdims=True)
     bias_grad = jnp.sum(scaled_gate * sum_grad + grad_pooled, axis=0, keepdims=True)
     up_bias_grad = jnp.sum(grad_upper, axis=0, keepdims=True)
@@ -366,40 +370,223 @@
     lax.fori_loop(0, H, drain, 0)
     for s in saves:
         s.wait()
+    fac_save.wait()
+
+
+class DeviceSum:
+    def __init__(self, where, block, rows, sbuf, ysend, ybuf, zsend, zbuf, s_ss, s_rs, y_ss, y_rs, z_ss, z_rs):
+        self.ci, self.yb, self.zz, self.sib, self.yp, self.zpeer, self.zb = where
+        self.block, self.rows = block, rows
+        self.sbuf, self.ysend, self.ybuf, self.zsend, self.zbuf = sbuf, ysend, ybuf, zsend, zbuf
+        self.s_ss, self.s_rs, self.y_ss, self.y_rs, self.z_ss, self.z_rs = s_ss, s_rs, y_ss, y_rs, z_ss, z_rs
+        self.count = sbuf.shape[0]
+        self.half = rows // 2
+
+    def core_copy(self, b):
+        ref, base = self.block(b, 1 - self.ci)
+        src = ref.at[pl.ds(pl.multiple_of(base, 16), self.rows), :]
+        return remote(src, self.sbuf.at[b], self.s_ss.at[b], self.s_rs.at[b], self.sib)
+
+    def y_copy(self):
+        return remote(self.ysend, self.ybuf, self.y_ss.at[0], self.y_rs.at[0], self.yp)
+
+    def z_copy(self, k):
+        to, peer = self.zpeer(k)
+        return remote(self.zsend.at[to], self.zbuf.at[self.zz], self.z_ss.at[k], self.z_rs.at[self.zz], peer)
+
+    def z_arrival(self, k):
+        to, peer = self.zpeer(k)
+        return remote(self.zsend.at[to], self.zbuf.at[to], self.z_ss.at[k], self.z_rs.at[to], peer)
+
+    def core_sum(self, b, y):
+        ref, base = self.block(b, self.ci)
+        at = pl.multiple_of(y * self.half, 16)
+        mine = ref[pl.ds(pl.multiple_of(base + at, 16), self.half), :]
+        return mine.astype(F32) + self.sbuf[b, pl.ds(at, self.half), :].astype(F32)
+
+    def to_core(self, b):
+        self.core_copy(b).start()
+
+    def to_y(self):
+        for b in range(self.count):
+            self.core_copy(b).wait_recv()
+        for b in range(self.count):
+            self.ysend[b] = self.core_sum(b, 1 - self.yb).astype(BF16)
+        self.y_copy().start()
+
+    def to_z(self):
+        self.y_copy().wait_recv()
+        piece = self.half // self.zb
+        for b in range(self.count):
+            total = self.core_sum(b, self.yb) + self.ybuf[b].astype(F32)
+            for z in range(self.zb):
+                self.zsend[z, b] = total[z * piece : (z + 1) * piece].astype(BF16)
+        for k in range(1, self.zb):
+            self.z_copy(k).start()
+
+    def totals(self):
+        for k in range(1, self.zb):
+            self.z_arrival(k).wait_recv()
+        outs = []
+        for b in range(self.count):
+            total = self.zsend[self.zz, b].astype(F32)
+            for k in range(1, self.zb):
+                total = total + self.zbuf[self.zpeer(k)[0], b].astype(F32)
+            outs.append(total)
+        return outs
+
+    def finish(self, cores=True):
+        if cores:
+            for b in range(self.count):
+                self.core_copy(b).wait_send()
+        self.y_copy().wait_send()
+        for k in range(1, self.zb):
+            self.z_copy(k).wait_send()
+
+
+class Spread:
+    def __init__(self, where, full, z_ss, z_rs, y_ss, y_rs):
+        self.ci, self.yb, self.zz, self.sib, self.yp, self.zpeer, self.zb = where
+        self.full = full
+        self.z_ss, self.z_rs, self.y_ss, self.y_rs = z_ss, z_rs, y_ss, y_rs
+
+    def z_copy(self, k):
+        own = self.full.at[self.yb, self.zz]
+        return remote(own, own, self.z_ss.at[k], self.z_rs.at[self.zz], self.zpeer(k)[1])
+
+    def y_copy(self):
+        own = self.full.at[self.yb]
+        return remote(own, own, self.y_ss.at[0], self.y_rs.at[0], self.yp)
+
+    def to_z(self):
+        for k in range(1, self.zb):
+            self.z_copy(k).start()
+
+    def to_y(self):
+        for k in range(1, self.zb):
+            to, peer = self.zpeer(k)
+            slot = self.full.at[self.yb, to]
+            remote(slot, slot, self.z_ss.at[k], self.z_rs.at[to], peer).wait_recv()
+        self.y_copy().start()
+
+    def arrive(self):
+        slot = self.full.at[1 - self.yb]
+        remote(slot, slot, self.y_ss.at[0], self.y_rs.at[0], self.yp).wait_recv()
+
+    def finish(self):
+        for k in range(1, self.zb):
+            self.z_copy(k).wait_send()
+        self.y_copy().wait_send()
+
+
+class VectorSum:
+    def __init__(self, where, xi, xn, vs, vy, vz, vx, ss, rs, z_ss, z_rs):
+        self.ci, self.yb, self.zz, self.sib, self.yp, self.zpeer, self.zb = where
+        self.xi, self.xn = xi, xn
+        self.vs, self.vy, self.vz, self.vx = vs, vy, vz, vx
+        self.ss, self.rs, self.z_ss, self.z_rs = ss, rs, z_ss, z_rs
+
+    def pair(self, ref, slot, k, peer):
+        return remote(ref.at[slot], ref.at[slot], self.ss.at[k], self.rs.at[k], peer)
+
+    def z_pair(self, slot, k, peer):
+        return remote(self.vz.at[slot], self.vz.at[slot], self.z_ss.at[k], self.z_rs.at[slot], peer)
+
+    def to_core(self, value):
+        self.vs[self.ci] = value
+        self.pair(self.vs, self.ci, 0, self.sib).start()
+
+    def to_y(self):
+        self.pair(self.vs, 1 - self.ci, 0, self.sib).wait_recv()
+        self.vy[self.yb] = self.vs[0] + self.vs[1]
+        self.pair(self.vy, self.yb, 1, self.yp).start()
+
+    def to_z(self):
+        self.pair(self.vy, 1 - self.yb, 1, self.yp).wait_recv()
+        self.vz[self.zz] = self.vy[0] + self.vy[1]
+        for k in range(1, self.zb):
+            self.z_pair(self.zz, k, self.zpeer(k)[1]).start()
+
+    def to_x(self):
+        for k in range(1, self.zb):
+            to, peer = self.zpeer(k)
+            self.z_pair(to, k, peer).wait_recv()
+        total = self.vz[0]
+        for z in range(1, self.zb):
+            total = total + self.vz[z]
+        self.vx[self.xi] = total
+        self.pair(self.vx, self.xi, 2, self.xn).start()
+
+    def arrive(self):
+        self.pair(self.vx, 1 - self.xi, 2, self.xn).wait_recv()
+
+    def finish(self):
+        self.pair(self.vs, self.ci, 0, self.sib).wait_send()
+        self.pair(self.vy, self.yb, 1, self.yp).wait_send()
+        for k in range(1, self.zb):
+            self.z_pair(self.zz, k, self.zpeer(k)[1]).wait_send()
+        self.pair(self.vx, self.xi, 2, self.xn).wait_send()
 
 
 def backward_kernel(
-    dims,
+    dims, group,
     i_preE, i_og, i_img, i_as2, i_kr, i_ke, i_preR, i_preF, i_preS, i_PR, i_PF, i_kt1, i_kt2,
-    se, vb, mvec, asp,
-    o_block, o_igrad, o_De, o_Dr, o_D1, o_D2, o_sum,
-    preE, ogb, imgb, as2, kr, ke, preR, preF, preS, PR, PF, kt1, kt2,
-    gpe, s3, r3, GS, GF, gpr, bst, igst, pbuf,
-    ld, ldr, ss3, rs3, ss4, rs4, b_loc, b_ss, b_rs, g_loc, g_ss, g_rs,
+    i_kraw, i_ewb, i_rawt, i_fac, i_ew, se, fsum, str_, ste, vb, mvec, asp,
+    o_block, o_igrad, o_G, o_rw, o_ew, o_dd, o_du, va, vl,
+    preE, gas, ogb, imgb, as2, kr, ke, preR, preF, preS, PR, PF, kt1, kt2, raw, rawt, ewo,
+    wide, s3, r3, GS, GF, bst, Dx, D12, bsum, estat, rstat, FB,
+    e_s, e_ys, e_yb, e_zs, e_zb, e_fin, e_x, e_G,
+    r_s, r_ys, r_yb, r_zs, r_zb, r_G,
+    d_s, d_ys, d_yb, d_zs, d_zb, d_fin,
+    va_s, va_y, va_z, vl_s, vl_y, vl_z,
+    ld, ldr, ldp, ss3, rs3, ss4, rs4, b_loc, b_ss, b_rs, g_loc, g_ss, g_rs,
+    e_sem, e_zsem, r_sem, r_zsem, d_sem, d_zsem, v_sem, v_zsem, f_sem, f_zsem, d_ag, e_xsem, credit,
 ):
     H, W, NI, CS, CH, MH, M, G = dims
+    YB, ZB = group
     d, c, xi, ci, sib, xn, dg = place()
+    yb, zz, first = d % YB, (d // YB) % ZB, (d // (YB * ZB)) * (YB * ZB)
+    yp = (first + zz * YB + (1 - yb), c)
+
+    def zpeer(k):
+        to = lax.rem(zz + k, ZB)
+        return to, (first + to * YB + yb, c)
+
+    where = (ci, yb, zz, sib, yp, zpeer, ZB)
     pairs = (
         (i_kr, kr), (i_ke, ke), (i_kt1, kt1), (i_kt2, kt2), (i_PR, PR), (i_PF, PF), (i_as2, as2),
-        (i_preR, preR), (i_preF, preF), (i_preS, preS),
+        (i_kraw, raw), (i_ewb, raw), (i_ew, ewo),
+        (i_rawt.at[0, ci, yb, zz], rawt.at[0]), (i_rawt.at[1, ci, yb, zz], rawt.at[1]),
+        (i_fac.at[ci], FB.at[yb, zz, ci]),
     )
     loads = [pltpu.make_async_copy(a, b, ld.at[k]) for k, (a, b) in enumerate(pairs)]
+    slots, ring = bst.shape[0], preE.shape[0]
+    igst = preE
+    gpe = pl.ds(0, CH)
 
     def row_loads(h):
         return [
-            pltpu.make_async_copy(i_preE.at[h], preE.at[h], ldr.at[h, 0]),
+            pltpu.make_async_copy(i_preE.at[h], preE.at[h % ring], ldr.at[h, 0]),
             pltpu.make_async_copy(i_og.at[h], ogb.at[h], ldr.at[h, 1]),
             pltpu.make_async_copy(i_img.at[h], imgb.at[h], ldr.at[h, 2]),
         ]
 
     loads[1].start()
-    for h in range(H):
+    for h in range(ring):
         for s in row_loads(h):
             s.start()
-    for k in (6, 9, 5, 3, 8, 4, 2, 7, 0):
+    loads[12].start()
+
+    def pre_load(k, h):
+        src, dst = ((i_preS, preS), (i_preF, preF), (i_preR, preR))[k]
+        return pltpu.make_async_copy(src.at[h], dst.at[lax.rem(h, 4)], ldp.at[h, k])
+
+    greet((sib, xn, yp) + tuple(zpeer(k)[1] for k in range(1, ZB)))
+    fac_core = remote(i_fac.at[1 - ci], FB.at[yb, zz, ci], f_sem.at[0], f_sem.at[1], sib)
+    fac_core.start()
+    for k in (6, 8, 5, 3, 4, 2, 0, 9, 10, 11):
         loads[k].start()
 
-    greet((sib, xn))
     mine = pl.ds(pl.multiple_of(ci * NI, NI), NI)
     clan = pl.ds(pl.multiple_of(ci * CS, CS), CS)
     slan = pl.ds(pl.multiple_of((1 - ci) * CS, CS), CS)
@@ -412,11 +599,12 @@
         for h in range(1, H + 1):
             ref[h, 0] = edge_w[0]
             ref[h, W + 1] = edge_w[0]
-    o_sum[...] = jnp.zeros_like(o_sum)
+    bsum[...] = jnp.zeros_like(bsum)
+    estat[...] = jnp.zeros_like(estat)
+    rstat[...] = jnp.zeros_like(rstat)
 
     gain, bias = vb[0:1, :], vb[1:2, :]
     scaled_gate, pool_part = se[0], se[1]
-    slots = bst.shape[0]
 
     def block_local(h):
         return pltpu.make_async_copy(bst.at[lax.rem(h, slots), :, :, clan], o_block.at[h, :, mine, :], b_loc.at[h])
@@ -439,42 +627,88 @@
 
     loads[1].wait()
 
+    def row_load(h, k):
+        src, dst = ((i_preE, preE.at[lax.rem(h, ring)]), (i_og, ogb.at[h]), (i_img, imgb.at[h]))[k]
+        return pltpu.make_async_copy(src.at[h], dst, ldr.at[h, k])
+
     def expand_row(h, carry):
-        for s in row_loads(h):
-            s.wait()
+        for k in range(3):
+            row_load(h, k).wait()
 
         @pl.when(h >= slots)
         def _():
             block_local(h - slots).wait()
             block_send(h - slots).wait_send()
 
-        pre = preE[h]
+        pre = preE[lax.rem(h, ring)]
         out = pre * gain + bias
         bst[lax.rem(h, slots)] = (imgb[h].astype(F32) + out * scaled_gate).astype(BF16)
         block_local(h).start()
         block_send(h).start()
+
+        @pl.when(h + ring < H)
+        def _():
+            for k in range(3):
+                row_load(h + ring, k).start()
+
         grad = ogb[h].astype(F32) * scaled_gate + pool_part
         piece = (grad * gain).astype(BF16).reshape(W * NI, CH)
-        gpe[h] = piece.reshape(W, NI, CH)
+        wide[pl.ds(pl.multiple_of(h * (W * NI), W * NI), W * NI), gpe] = piece
         s3[h] = dot_nt(piece, ke[olan, :]).astype(BF16).reshape(W, NI, MH)
         s3_copy(h).start()
-        preE[h, :, :, 0:MH] = dot_nt(piece, ke[mlan, :]).reshape(W, NI, MH)
+        gas[h] = dot_nt(piece, ke[mlan, :]).reshape(W, NI, MH)
         return carry
 
     lax.fori_loop(0, H, expand_row, 0)
+    pre_load(0, 0).start()
+    pre_load(0, 1).start()
+    pre_load(1, 0).start()
+
+    loads[12].wait()
+    remote(i_fac.at[1 - ci], FB.at[yb, zz, 1 - ci], f_sem.at[0], f_sem.at[1], sib).wait_recv()
+    fac_spread = Spread(where, FB, f_zsem.at[0], f_zsem.at[1], f_sem.at[pl.ds(2, 1)], f_sem.at[pl.ds(3, 1)])
+    fac_spread.to_z()
 
     loads[6].wait()
+    loads[8].wait()
+    quarter = ewo.shape[0]
     step = 128
+    e_mean = ste[xi, 0:1, :]
 
     def expand_kernel_grad(j, carry):
         lanes = pl.ds(pl.multiple_of(j * step, step), step)
         left = as2[:, :, :, lanes].reshape(H * W * NI, step)
-        o_De[lanes, :] = dot_tn(left, gpe[...].reshape(H * W * NI, CH)).astype(BF16)
+        Dx[lanes, :] = dot_tn(left, wide[:, gpe]).astype(BF16)
         return carry
 
     lax.fori_loop(0, M // step, expand_kernel_grad, 0)
-
-    for k in (9, 5, 3, 8, 4, 2, 7, 0):
+    pl.semaphore_signal(credit, inc=1, device_id=xn, device_id_type=MESH)
+    gpr = as2
+
+    sum_e = DeviceSum(
+        where, lambda b, half: (Dx, b * MH + half * quarter), quarter, e_s, e_ys, e_yb, e_zs, e_zb,
+        e_sem.at[pl.ds(0, 2)], e_sem.at[pl.ds(2, 2)], e_sem.at[pl.ds(4, 1)], e_sem.at[pl.ds(5, 1)],
+        e_zsem.at[0], e_zsem.at[1],
+    )
+    sum_e.to_core(0)
+    sum_e.to_core(1)
+    spread_e = Spread(where, e_G, e_zsem.at[2], e_zsem.at[3], e_sem.at[pl.ds(6, 1)], e_sem.at[pl.ds(7, 1)])
+
+    def e_cross(slot):
+        return remote(e_x.at[1 - slot], e_G.at[yb, zz, slot], e_xsem.at[0], e_xsem.at[1], xn)
+
+    for q in range(4):
+        grads = Dx[q * quarter : (q + 1) * quarter, :].astype(F32)
+        away = raw[q * quarter : (q + 1) * quarter, :].astype(F32) - e_mean
+        estat[0:1, :] += jnp.sum(grads, axis=0, keepdims=True)
+        estat[1:2, :] += jnp.sum(grads * away, axis=0, keepdims=True)
+    loads[7].start()
+    sum_a = VectorSum(
+        where, xi, xn, va_s, va_y, va_z, va, v_sem.at[0], v_sem.at[1], v_zsem.at[0], v_zsem.at[1]
+    )
+    sum_a.to_core(jnp.concatenate([fsum[0:5, :], estat[0:2, :], jnp.zeros((1, CH), F32)], axis=0))
+
+    for k in (5, 3, 4, 2, 0):
         loads[k].wait()
     turned = jnp.broadcast_to((asp[ci] > 0.5)[None], (W, NI, G))
     reduce_gain, reduce_bias = mvec[xi, 0:1], mvec[xi, 1:2]
@@ -489,79 +723,258 @@
 
     def tally(row, grad, pre):
         flat = (grad * pre).reshape(W * NI, MH)
-        o_sum[row : row + 1, :] += jnp.sum(flat, axis=0, keepdims=True)
-        o_sum[row + 1 : row + 2, :] += jnp.sum(grad.reshape(W * NI, MH), axis=0, keepdims=True)
+        bsum[row : row + 1, :] += jnp.sum(flat, axis=0, keepdims=True)
+        bsum[row + 1 : row + 2, :] += jnp.sum(grad.reshape(W * NI, MH), axis=0, keepdims=True)
+
+    def image_row(h):
+        s4_arrival(h).wait_recv()
+
+        @pl.when(h >= slots)
+        def _():
+            igrad_local(h - slots).wait()
+            igrad_send(h - slots).wait_send()
+
+        rows = dot_nt(gpr[h].reshape(W * NI, M), kr[...]).reshape(W, NI, CH)
+        igst[lax.rem(h, slots)] = ogb[h].astype(F32) + INV_BETA * rows
+        igrad_local(h).start()
+        igrad_send(h).start()
 
     def wave(t, carry):
+        @pl.when(t + 2 < H)
+        def _():
+            pre_load(0, t + 2).start()
+
+        @pl.when(t + 1 < H)
+        def _():
+            pre_load(1, t + 1).start()
+
         @pl.when(t < H)
         def _():
+            pre_load(2, t).start()
+
+        @pl.when(t < H)
+        def _():
+            pre_load(0, t).wait()
             s3_copy(t).wait_recv()
-            cot = (preE[t, :, :, 0:MH] + r3[t].astype(F32)).astype(BF16).astype(F32)
-            pre = preS[t]
+            cot = (gas[t] + r3[t].astype(F32)).astype(BF16).astype(F32)
+            pre = preS[lax.rem(t, 4)]
             grad = cot * (GELU_SCALE * gelu_slope(pre * second_gain + second_bias))
             tally(4, grad, pre)
             GS[t + 1, 1 : W + 1] = (grad * second_gain).astype(BF16)
 
         @pl.when((t >= 1) & (t <= H))
         def _():
+            pre_load(1, t - 1).wait()
             cot = conv_row(GS, t - 1, kt2, turned, W, G)
-            pre = preF[t - 1]
+            pre = preF[lax.rem(t - 1, 4)]
             grad = cot * (GELU_SCALE * gelu_slope(pre * first_gain + first_bias))
             tally(2, grad, pre)
             GF[t, 1 : W + 1] = (grad * first_gain).astype(BF16)
 
+        @pl.when(t == 2)
+        def _():
+            pl.semaphore_wait(credit, 1)
+
         @pl.when((t >= 2) & (t <= H + 1))
         def _():
+            pre_load(2, t - 2).wait()
             cot = conv_row(GF, t - 2, kt1, turned, W, G)
-            pre = preR[t - 2]
+            pre = preR[lax.rem(t - 2, 4)]
             grad = cot * (GELU_SCALE * gelu_slope(pre * reduce_gain + reduce_bias))
             tally(0, grad, pre)
             gpr[t - 2, :, :, mlan] = (grad * reduce_gain).astype(BF16)
             s4_copy(t - 2).start()
 
+        @pl.when(t == 1)
+        def _():
+            fac_spread.to_y()
+            sum_e.to_y()
+            sum_a.to_y()
+
+        @pl.when(t == 3)
+        def _():
+            sum_e.to_z()
+            sum_a.to_z()
+
+        @pl.when(t == 5)
+        def _():
+            fac_spread.arrive()
+            sum_a.to_x()
+            for b, total in enumerate(sum_e.totals()):
+                e_x[b] = total.astype(BF16)
+            e_G[yb, zz, xi] = e_x[xi]
+            e_cross(xi).start()
+
+        @pl.when(t == 7)
+        def _():
+            e_cross(1 - xi).wait_recv()
+            spread_e.to_z()
+            sum_a.arrive()
+
+        @pl.when(t == 9)
+        def _():
+            spread_e.to_y()
+
         @pl.when(t >= LAG)
         def _():
-            h = t - LAG
-            s4_arrival(h).wait_recv()
-
-            @pl.when(h >= slots)
-            def _():
-                igrad_local(h - slots).wait()
-                igrad_send(h - slots).wait_send()
-
-            rows = dot_nt(gpr[h].reshape(W * NI, M), kr[...]).reshape(W, NI, CH)
-            igst[lax.rem(h, slots)] = ogb[h].astype(F32) + INV_BETA * rows
-            igrad_local(h).start()
-            igrad_send(h).start()
+            image_row(t - LAG)
 
         return carry
 
-    lax.fori_loop(0, H + LAG, wave, 0)
-
-    for act, cot, dst in ((PF, GS, o_D2), (PR, GF, o_D1)):
+    lax.fori_loop(0, H + 2, wave, 0)
+
+    sum_d = DeviceSum(
+        where, lambda b, half: (D12.at[b], half * quarter), quarter, d_s, d_ys, d_yb, d_zs, d_zb,
+        d_sem.at[pl.ds(0, 2)], d_sem.at[pl.ds(2, 2)], d_sem.at[pl.ds(4, 1)], d_sem.at[pl.ds(5, 1)],
+        d_zsem.at[0], d_zsem.at[1],
+    )
+    for b, act, cot in ((1, PF, GS), (0, PR, GF)):
         for g in range(MH // G):
-            total = None
-            for part in range(2):
-                first = part * (H // 2)
-
-                def fill(h, carry):
-                    at = pl.ds(pl.multiple_of(h * (W * NI), W * NI), W * NI)
-                    pbuf[at, :] = patches(act, first + h, g, turned, W, G)
-                    return carry
-
-                lax.fori_loop(0, H // 2, fill, 0)
-                right = cot[1 + first : 1 + first + H // 2, 1 : W + 1, :, g * G : (g + 1) * G]
-                term = dot_tn(right.reshape(H // 2 * W * NI, G), pbuf[...])
-                total = term if total is None else total + term
-            dst[g * G : (g + 1) * G, :] = total.astype(BF16)
+            def fill(h, carry):
+                at = pl.ds(pl.multiple_of(h * (W * NI), W * NI), W * NI)
+                wide[at, :] = patches(act, h, g, turned, W, G)
+                return carry
+
+            lax.fori_loop(0, H, fill, 0)
+            right = cot[1 : H + 1, 1 : W + 1, :, g * G : (g + 1) * G].reshape(H * W * NI, G)
+            total = dot_tn(right, wide[...])
+            D12[b, g * G : (g + 1) * G, :] = total.astype(BF16)
+        sum_d.to_core(b)
+
+    for h in range(H + 2 - LAG, H):
+        image_row(h)
+    sum_d.to_y()
+
+    loads[7].wait()
+    for b in range(2):
+        sum_e.core_copy(b).wait_send()
+    r_mean, r_rate = str_[0:1, :], str_[1:2, :]
 
     def reduce_kernel_grad(j, carry):
         lanes = pl.ds(pl.multiple_of(j * step, step), step)
         left = (imgb[:, :, :, lanes].astype(F32) * INV_BETA).astype(BF16).reshape(H * W * NI, step)
-        o_Dr[lanes, :] = dot_tn(left, gpr[...].reshape(H * W * NI, M)).astype(BF16)
+        grads = dot_tn(left, gpr[...].reshape(H * W * NI, M))
+        rstat[0:1, :] += jnp.sum(grads, axis=0, keepdims=True)
+        rstat[1:2, :] += jnp.sum(grads * (raw[lanes, :].astype(F32) - r_mean), axis=0, keepdims=True)
+        Dx[lanes, :] = grads.astype(BF16)
         return carry
 
     lax.fori_loop(0, CH // step, reduce_kernel_grad, 0)
+    sum_r = DeviceSum(
+        where, lambda b, half: (Dx, half * CS), CS, r_s, r_ys, r_yb, r_zs, r_zb,
+        r_sem.at[pl.ds(0, 1)], r_sem.at[pl.ds(1, 1)], r_sem.at[pl.ds(2, 1)], r_sem.at[pl.ds(3, 1)],
+        r_zsem.at[0], r_zsem.at[1],
+    )
+    spread_r = Spread(where, r_G, r_zsem.at[2], r_zsem.at[3], r_sem.at[pl.ds(4, 1)], r_sem.at[pl.ds(5, 1)])
+    sum_r.to_core(0)
+    sum_l = VectorSum(
+        where, xi, xn, vl_s, vl_y, vl_z, vl, v_sem.at[2], v_sem.at[3], v_zsem.at[2], v_zsem.at[3]
+    )
+    rstat[2:8, mlan] = bsum[0:6, :]
+    sum_l.to_core(rstat[...])
+    sum_r.to_y()
+    sum_l.to_y()
+    sum_d.to_z()
+    sum_r.to_z()
+    sum_l.to_z()
+
+    loads[10].wait()
+    loads[11].wait()
+    for b, total in enumerate(sum_d.totals()):
+        weight = rawt[b].astype(F32)
+        away = weight - jnp.mean(weight, axis=1, keepdims=True)
+        rate = lax.rsqrt(jnp.sum(away * away, axis=1, keepdims=True) + STD_EPSILON)
+        cross = jnp.sum(total * away, axis=1, keepdims=True)
+        centred = total - jnp.mean(total, axis=1, keepdims=True)
+        d_fin[b] = (rate * centred - rate * rate * rate * away * cross).astype(BF16)
+
+    q = c
+    qx = (1 - xi) * 2 + ci
+    qs = xi * 2 + (1 - ci)
+    qd = (1 - xi) * 2 + (1 - ci)
+    own = o_G.at[q, yb, zz]
+    d_keep = pltpu.make_async_copy(d_fin, own, d_ag.at[0])
+    d_keep.start()
+
+    def d_z(k):
+        return remote(d_fin, own, d_zsem.at[2].at[k], d_zsem.at[3].at[zz], zpeer(k)[1])
+
+    for k in range(1, ZB):
+        d_z(k).start()
+    for b, total in enumerate(sum_r.totals()):
+        r_G[yb, zz, b] = total.astype(BF16)
+    spread_r.to_z()
+    sum_l.to_x()
+
+    def d_block(quad, y, k, peer):
+        ref = o_G.at[quad, y]
+        return remote(ref, ref, d_ag.at[2 * k + 2], d_ag.at[2 * k + 3], peer)
+
+    d_keep.wait()
+    for k in range(1, ZB):
+        to, peer = zpeer(k)
+        ref = o_G.at[q, yb, to]
+        remote(ref, ref, d_zsem.at[2].at[k], d_zsem.at[3].at[to], peer).wait_recv()
+    d_block(q, yb, 0, yp).start()
+    d_block(q, yb, 1, xn).start()
+    d_block(q, yb, 2, sib).start()
+    spread_r.to_y()
+    d_block(q, 1 - yb, 0, yp).wait_recv()
+    d_block(q, 1 - yb, 3, xn).start()
+    d_block(q, 1 - yb, 4, sib).start()
+    d_block(qx, yb, 1, xn).wait_recv()
+    d_block(qx, yb, 5, sib).start()
+
+    fac_all = FB[...].reshape(YB * ZB * 2 * NI, FB.shape[-1])
+    o_dd[...] = dot_tn(fac_all[:, 0:CS], fac_all[:, CS : CS + M])
+    o_du[...] = dot_tn(fac_all[:, CS + M : CS + 2 * M], fac_all[:, CS + 2 * M :])
+    spread_e.arrive()
+    loads[9].wait()
+    piece = e_G.shape[3]
+    for y in range(YB):
+        for z in range(ZB):
+            at = (y * ZB + z) * piece
+            for s in range(2):
+                o_ew[at : at + piece, s * CH : (s + 1) * CH] = e_G[y, z, s].astype(F32)
+    fan = 1.0 / (4 * quarter)
+    for s in range(2):
+        lanes = slice(s * CH, (s + 1) * CH)
+        mean, rate = ste[s, 0:1, :], ste[s, 1:2, :]
+        low, cross = va[s, 5:6, :] * fan, va[s, 6:7, :]
+        away = ewo[:, lanes].astype(F32) - mean
+        o_ew[:, lanes] = rate * (o_ew[:, lanes] - low) - rate * rate * rate * away * cross
+    sum_l.arrive()
+    spread_r.arrive()
+    low = (vl[0, 0:1, :] + vl[1, 0:1, :]) * (1.0 / (4 * CS))
+    cross = vl[0, 1:2, :] + vl[1, 1:2, :]
+    piece = r_G.shape[3]
+    for y in range(YB):
+        for z in range(ZB):
+            at = (y * ZB + z) * piece
+            rows = pl.ds(pl.multiple_of(ci * CS + at, 16), piece)
+            away = raw[rows, :].astype(F32) - r_mean
+            grads = r_G[y, z, 0].astype(F32)
+            o_rw[at : at + piece, :] = r_rate * (grads - low) - r_rate * r_rate * r_rate * away * cross
+
+    d_block(qx, 1 - yb, 3, xn).wait_recv()
+    d_block(qx, 1 - yb, 6, sib).start()
+    d_block(qs, yb, 2, sib).wait_recv()
+    d_block(qs, 1 - yb, 4, sib).wait_recv()
+    d_block(qd, yb, 5, sib).wait_recv()
+    d_block(qd, 1 - yb, 6, sib).wait_recv()
+
+    fac_core.wait_send()
+    fac_spread.finish()
+    e_cross(xi).wait_send()
+    sum_e.finish(cores=False)
+    for job in (spread_e, sum_a, sum_d, sum_r, spread_r, sum_l):
+        job.finish()
+    for k in range(1, ZB):
+        d_z(k).wait_send()
+    for k, (quad, y, peer) in enumerate(
+        ((q, yb, yp), (q, yb, xn), (q, yb, sib), (q, 1 - yb, xn), (q, 1 - yb, sib), (qx, yb, sib), (qx, 1 - yb, sib))
+    ):
+        d_block(quad, y, k, peer).wait_send()
 
     def drain(h, carry):
         s3_copy(h).wait_send()
@@ -576,17 +989,6 @@
         block_send(h).wait_send()
         igrad_local(h).wait()
         igrad_send(h).wait_send()
-
-
-def standard_grad(summed, centered, rate, column_sum, column_cross, fan_in):
-    return rate * (summed - column_sum / fan_in) - rate * rate * rate * centered * column_cross
-
-
-def standardize(weight, axes):
-    middle = jnp.mean(weight, axis=axes, keepdims=True)
-    centered = weight - middle
-    spread = jnp.sum(centered * centered, axis=axes, keepdims=True)
-    return centered * lax.rsqrt(spread + STD_EPSILON)
 
 
 def body(
@@ -620,103 +1022,94 @@
     S = jax.ShapeDtypeStruct
     V = pltpu.VMEM
     DMA = pltpu.SemaphoreType.DMA
+    width = 2 * CS + 2 * M
     big = (
         S((H, W, NI, CH), F32), S((H, W, NI, CH), BF16), S((H, W, NI, CH), BF16), S((H, W, NI, M), BF16),
         S((CH, M), BF16), S((M, CH), BF16), S((H, W, NI, MH), F32), S((H, W, NI, MH), F32), S((H, W, NI, MH), F32),
         S((H + 2, W + 2, NI, MH), BF16), S((H + 2, W + 2, NI, MH), BF16), S((9 * G, MH), BF16), S((9 * G, MH), BF16),
-    )
-    small = (S((6, NI, CH), F32), S((8, CH), F32), S((8, M), F32), S((2, 8, CH), F32), S((8, CH), F32))
+        S((CH, M), BF16), S((4, quarter, CH), BF16), S((2, MH, 9 * G), BF16), S((2, NI, width), BF16),
+    )
+    small = (S((2, NI, CH), F32), S((8, CH), F32), S((8, M), F32), S((2, 8, CH), F32), S((8, CH), F32))
     fwd = pl.pallas_call(
         functools.partial(forward_kernel, dims),
         name="forward",
         out_shape=big + small,
         in_specs=[anyspec] * 8 + [vm, anyspec, vm, vm],
-        out_specs=[anyspec] * 13 + [vm] * 5,
+        out_specs=[anyspec] * 17 + [vm] * 5,
         scratch_shapes=[
             V((H, W, NI, CH), BF16), V((H, W, NI, CH), BF16), V((CH, M), BF16), V((4, quarter, CH), BF16),
             V((CH, M), BF16), V((M, CH), BF16), V((9 * G, MH), BF16), V((9 * G, MH), BF16), V((4, 8, M), F32),
             V((CH, M), BF16), V((M, CH), BF16), V((9 * G, MH), BF16), V((9 * G, MH), BF16), V((9 * G, MH), BF16),
-            V((9 * G, MH), BF16),
+            V((9 * G, MH), BF16), V((2, MH, 9 * G), BF16), V((2, NI, width), BF16),
             V((H, W, NI, MH), F32), V((H, W, NI, MH), BF16), V((H, W, NI, MH), BF16),
             V((H + 2, W + 2, NI, MH), BF16), V((H + 2, W + 2, NI, MH), BF16),
             V((H, W, NI, MH), F32), V((H, W, NI, MH), F32), V((H, W, NI, M), BF16), V((H, W, NI, CH), F32),
             V((3, NI, CH), F32), V((2, NI, M), F32), V((2, NI, M), F32),
             DMA((H,)), DMA((H,)), DMA((H,)), DMA((8,)), DMA((8,)), DMA((8,)), DMA((3,)), DMA((4,)),
-            DMA((H,)), DMA((H,)), DMA((H,)), DMA((H,)), DMA((3,)), DMA((3,)), DMA((13,)),
+            DMA((H,)), DMA((H,)), DMA((H,)), DMA((H,)), DMA((3,)), DMA((3,)), DMA((17,)),
         ],
         compiler_params=pltpu.CompilerParams(collective_id=0, has_side_effects=True, vmem_limit_bytes=62 << 20),
     )(img, og, reduce_weight, expand_weight, excite_down, excite_up, fw, sw, mvec, cvec, db, asp)
-    saved, (se, fsum, stat_r, stat_e, vb) = fwd[:13], fwd[13:]
-
+    saved, fac, (se, fsum, stat_r, stat_e, vb) = list(fwd[:16]), fwd[16], fwd[17:]
+
+    dp = lax.axis_size("dp")
+    YB = 2
+    ZB = 4 if dp % 8 == 0 else dp // 2
+    saved[14] = saved[14].reshape(M, CH)
+    saved[15] = saved[15].reshape(2, 2, YB, ZB, quarter // (YB * ZB), 9 * G)
     slots = 2
-    block_out, images_grad, De, Dr, D1, D2, bsum = pl.pallas_call(
-        functools.partial(backward_kernel, dims),
+    pe, pr = quarter // (YB * ZB), CS // (YB * ZB)
+    block_out, images_grad, grouped, rw_grad, ew_grad, down_grad, up_grad, va, vl = pl.pallas_call(
+        functools.partial(backward_kernel, dims, (YB, ZB)),
         name="backward",
         out_shape=(
-            S((H, W, N, CS), BF16), S((H, W, N, CS), F32), S((M, CH), BF16), S((CH, M), BF16),
-            S((MH, 9 * G), BF16), S((MH, 9 * G), BF16), S((8, MH), F32),
+            S((H, W, N, CS), BF16), S((H, W, N, CS), F32), S((4, YB, ZB, 2, pe, 9 * G), BF16),
+            S((CS, M), F32), S((quarter, 2 * CH), F32), S((CS, M), F32), S((M, CS), F32),
+            S((2, 8, M), F32), S((2, 8, M), F32),
         ),
-        in_specs=[anyspec] * 13 + [vm] * 4,
-        out_specs=[anyspec] * 2 + [vm] * 5,
+        in_specs=[anyspec] * 18 + [vm] * 7,
+        out_specs=[anyspec] * 3 + [vm] * 6,
         scratch_shapes=[
-            V((H, W, NI, CH), F32), V((H, W, NI, CH), BF16), V((H, W, NI, CH), BF16), V((H, W, NI, M), BF16),
-            V((CH, M), BF16), V((M, CH), BF16), V((H, W, NI, MH), F32), V((H, W, NI, MH), F32), V((H, W, NI, MH), F32),
+            V((3, W, NI, CH), F32), V((H, W, NI, MH), F32), V((H, W, NI, CH), BF16), V((H, W, NI, CH), BF16),
+            V((H, W, NI, M), BF16), V((CH, M), BF16), V((M, CH), BF16),
+            V((4, W, NI, MH), F32), V((4, W, NI, MH), F32), V((4, W, NI, MH), F32),
             V((H + 2, W + 2, NI, MH), BF16), V((H + 2, W + 2, NI, MH), BF16), V((9 * G, MH), BF16), V((9 * G, MH), BF16),
-            V((H, W, NI, CH), BF16), V((H, W, NI, MH), BF16), V((H, W, NI, MH), BF16),
-            V((H + 2, W + 2, NI, MH), BF16), V((H + 2, W + 2, NI, MH), BF16), V((H, W, NI, M), BF16),
-            V((slots, W, NI, CH), BF16), V((slots, W, NI, CH), F32), V((H // 2 * W * NI, 9 * G), BF16),
-            DMA((10,)), DMA((H, 3)), DMA((H,)), DMA((H,)), DMA((H,)), DMA((H,)),
+            V((CH, M), BF16), V((2, pe, 9 * G), BF16), V((quarter, 2 * CH), BF16),
+            V((H * W * NI, 9 * G), BF16), V((H, W, NI, MH), BF16), V((H, W, NI, MH), BF16),
+            V((H + 2, W + 2, NI, MH), BF16), V((H + 2, W + 2, NI, MH), BF16),
+            V((slots, W, NI, CH), BF16), V((CH, M), BF16), V((2, MH, 9 * G), BF16), V((8, MH), F32), V((8, CH), F32), V((8, M), F32),
+            V((YB, ZB, 2, NI, width), BF16),
+            V((2, quarter, CH), BF16), V((2, quarter // 2, CH), BF16), V((2, quarter // 2, CH), BF16),
+            V((ZB, 2, pe, CH), BF16), V((ZB, 2, pe, CH), BF16), V((2, pe, CH), BF16), V((2, pe, CH), BF16),
+            V((YB, ZB, 2, pe, CH), BF16),
+            V((1, CS, M), BF16), V((1, CS // 2, M), BF16), V((1, CS // 2, M), BF16),
+            V((ZB, 1, pr, M), BF16), V((ZB, 1, pr, M), BF16), V((YB, ZB, 1, pr, M), BF16),
+            V((2, quarter, 9 * G), BF16), V((2, quarter // 2, 9 * G), BF16), V((2, quarter // 2, 9 * G), BF16),
+            V((ZB, 2, pe, 9 * G), BF16), V((ZB, 2, pe, 9 * G), BF16), V((2, pe, 9 * G), BF16),
+            V((2, 8, M), F32), V((2, 8, M), F32), V((ZB, 8, M), F32),
+            V((2, 8, M), F32), V((2, 8, M), F32), V((ZB, 8, M), F32),
+            DMA((13,)), DMA((H, 3)), DMA((H, 3)), DMA((H,)), DMA((H,)), DMA((H,)), DMA((H,)),
             DMA((H,)), DMA((H,)), DMA((H,)), DMA((H,)), DMA((H,)), DMA((H,)),
+            DMA((8,)), DMA((4, ZB)), DMA((6,)), DMA((4, ZB)), DMA((6,)), DMA((4, ZB)), DMA((4, 3)), DMA((4, ZB)),
+            DMA((4,)), DMA((2, ZB)), DMA((16,)), DMA((2,)), pltpu.SemaphoreType.REGULAR,
         ],
         compiler_params=pltpu.CompilerParams(collective_id=1, has_side_effects=True, vmem_limit_bytes=63 << 20),
-    )(*saved, se, vb, mvec, asp)
-
+    )(*saved, fac, expand_weight, se, fsum, stat_r, stat_e, vb, mvec, asp)
+
+    grouped = jnp.transpose(grouped, (3, 5, 0, 1, 2, 4)).reshape(2, 3, 3, G, M).astype(F32)
+    outs = [grouped[0], grouped[1], rw_grad, ew_grad, down_grad, up_grad, va, vl]
+    parts = YB * ZB
+    if dp > parts:
+        outs = [v / parts for v in lax.psum(tuple(outs), "dp")]
+    first_weight_grad, second_weight_grad, rw_grad, ew_grad, down_grad, up_grad, va, vl = outs
     xi, ci = index // 2, index % 2
-    both = ("dp", "chan")
-    def put(v, at, length, axis):
-        shape = list(v.shape)
-        shape[axis] = length
-        return lax.dynamic_update_slice_in_dim(jnp.zeros(shape, v.dtype), v, at, axis)
-
-    Dr, De, D1, D2 = (v.astype(F32) for v in (Dr, De, D1, D2))
-    dr_all = lax.psum(put(Dr, xi * CH, 2 * CH, 0), both)
-    de_all = lax.psum(put(De, xi * CH, 2 * CH, 1), both)
-    d12 = lax.psum(put(jnp.stack([D1, D2]), xi * MH, M, 1), both)
-    bs = lax.psum(put(bsum, xi * MH, M, 1), both)
-    fs = lax.psum(put(fsum, xi * CH, 2 * CH, 1), both)
-    ddown = lax.psum(put(jnp.dot(se[2].T, se[3], precision=lax.Precision.HIGHEST), xi * CH, 2 * CH, 0), both)
-    dup = lax.psum(put(jnp.dot(se[4].T, se[5], precision=lax.Precision.HIGHEST), xi * CH, 2 * CH, 1), both)
-
-    fan_r = 4 * CS
-    r_mean, r_rate = stat_r[0:1], stat_r[1:2]
-    own_rows = reduce_weight.astype(F32) - r_mean
-    raw_all = lax.all_gather(reduce_weight, "chan", axis=0, tiled=True).astype(F32) - r_mean
-    r_sum = jnp.sum(dr_all, axis=0, keepdims=True)
-    r_cross = jnp.sum(dr_all * raw_all, axis=0, keepdims=True)
-    my_dr = lax.dynamic_slice_in_dim(dr_all, index * CS, CS, 0)
-    reduce_weight_grad = standard_grad(my_dr, own_rows, r_rate, r_sum, r_cross, fan_r)
-    e_mean = jnp.concatenate([stat_e[0, 0:1], stat_e[1, 0:1]], axis=1)
-    e_rate = jnp.concatenate([stat_e[0, 1:2], stat_e[1, 1:2]], axis=1)
-    e_own = expand_weight.astype(F32) - e_mean
-    e_all = lax.all_gather(expand_weight, "chan", axis=0, tiled=True).astype(F32) - e_mean
-    e_sum = jnp.sum(de_all, axis=0, keepdims=True)
-    e_cross = jnp.sum(de_all * e_all, axis=0, keepdims=True)
-    my_de = lax.dynamic_slice_in_dim(de_all, index * quarter, quarter, 0)
-    expand_weight_grad = standard_grad(my_de, e_own, e_rate, e_sum, e_cross, 4 * quarter)
-    def group_grad(weight, dt):
-        total = jnp.transpose(dt).reshape(3, 3, G, M)
-        _, pull = jax.vjp(lambda w: standardize(w, (0, 1, 2)), weight.astype(F32))
-        return pull(total)[0]
-
-    first_weight_grad = group_grad(first_weight, d12[0])
-    second_weight_grad = group_grad(second_weight, d12[1])
-    my = lambda v: lax.dynamic_slice_in_dim(v, index * CS, CS, 0)
+    mine = lax.dynamic_slice_in_dim(lax.dynamic_index_in_dim(va, xi, 0, keepdims=False), ci * CS, CS, 1)
+    late = vl[0] + vl[1]
     back = lambda v: jnp.transpose(v, (2, 0, 1, 3))
     return (
-        back(block_out), back(images_grad), reduce_weight_grad, bs[0], bs[1], first_weight_grad, bs[2], bs[3],
-        second_weight_grad, bs[4], bs[5], expand_weight_grad, my(fs[0]), my(fs[1]),
-        lax.dynamic_slice_in_dim(ddown, index * CS, CS, 0), fs[4][:M], lax.dynamic_slice_in_dim(dup, index * CS, CS, 1),
-        my(fs[2]), jnp.sum(fs[3]).reshape(1),
+        back(block_out), back(images_grad), rw_grad, late[2], late[3], first_weight_grad, late[4], late[5],
+        second_weight_grad, late[6], late[7], ew_grad, mine[0], mine[1], down_grad, va[0, 4], up_grad, mine[2],
+        jnp.sum(va[0, 3] + va[1, 3]).reshape(1),
     )
 
 

time: 844 us -> 320 us (0.38)
  waiting for transfers between devices: 523 us -> 0 us
  Pallas kernels: 209 us -> 259 us
  other arithmetic: 29.3 us -> 4.8 us
  between operations: 16.8 us -> 1.36 us
    psum x2 -> x0, waiting for transfers between devices: 522 us -> none  [the longest x1 410 us: body(): dr_all = lax.psum(put(Dr, xi * CH, 2 * CH, 0), both)]
    pallas_call x1, Pallas kernels: 100 us -> 150 us  [body(): pl.pallas_call(functools.partial(backward_kernel, dims, (YB, ZB)), name='...]
    reduce_sum x9 -> x0, other arithmetic: 13.9 us -> none  [the longest x1 4.65 us: body(): r_sum = jnp.sum(dr_all, axis=0, keepdims=True)]
    transpose x3 -> x0, local copies, waits for them, and re-layouts: 11.6 us -> none  [group_grad(): total = jnp.transpose(dt).reshape(3, 3, G, M)]
    unnamed x62 -> x20, local copies, waits for them, and re-layouts: 15 us -> 25 us
    squeeze x0 -> x2, local copies, waits for them, and re-layouts: none -> 9.7 us  [the longest x1 6.1 us: body(): grouped[0]]
  transfers between devices with their start and end apart: 4 -> 0, of which waited for: 2 -> 0; matrix products, arithmetic and copies ran while one was open for 5% -> 0% of each run, Pallas kernels for 0% -> 0%
where the time goes in v2:
time: 320 us; the launch traced here: 314 us
  Pallas kernels  259 us (81%)
  local copies, waits for them, and re-layouts  48.3 us (15%)
  other arithmetic  4.8 us (2%)
    pallas_call x1, Pallas kernels, body(): pl.pallas_call(functools.partial(backward_kernel, dims, (YB, ZB)), name='...  150 us
    pallas_call x1, Pallas kernels, body(): pl.pallas_call(functools.partial(forward_kernel, dims), name='forward', o...  110 us
    unnamed x20, local copies, waits for them, and re-layouts  25 us

profile of v2, /device:TPU:0, one launch (start us, length us, event | category | flops | bytes accessed | tf_op | source)
XLA Modules:
  0.0 313.9 jit_solution(4210370614473286256)
XLA Ops:
  0.7 0.7 stack.39
  1.4 0.7 stack.40
  2.0 0.7 stack.41
  2.7 0.7 stack.42
  3.4 0.7 stack.43
  4.1 0.7 stack.44
  4.8 0.6 stack.46
  5.5 0.7 convert_element_type.10
  6.1 0.1 broadcast_in_dim.7
  6.2 0.7 broadcast_in_dim.8.asp
  7.6 0.7 stack.47
  8.2 0.7 stack.48
  8.9 0.7 stack.49
  9.6 0.6 stack.51.cvec
  10.2 1.3 reshape.104.db
  11.5 109.6 %forward.1 = (f32[10,14,16,768]{3,2,1,0:T(8,128)}, bf16[10,14,16,768]{3,2,1,0:T(8,128)(2,1)}, bf16[10,14,16,768]{3,2,1,0:T(8,128)(2,1)}, bf16[10,14,16,768]{3,2,...) custom-call(bf16[10,14,32,384]{3,2,1,0:T(8,128)(2,1)} %bitcast.23, ...), custom_call_target="tpu_custom_call" | custom-call | tf_op jit(solution)/shard_map/forward/pallas_call | solution.py:1033
  121.1 149.9 %backward.1 = (bf16[10,14,32,384]{3,2,1,0:T(8,128)(2,1)}, f32[10,14,32,384]{3,2,1,0:T(8,128)}, bf16[4,2,4,2,24,1152]{5,4,3,2,1,0:T(8,128)(2,1)}, f32[384,768]{1,...) custom-call(f32[10,14,16,768]{3,2,1,0:T(8,128)} %get-tuple-element.5, ...), custom_call_target="tpu_custom_call" | custom-call | tf_op jit(solution)/shard_map/backward/pallas_call | solution.py:1062
  270.9 2.6 convert_bitcast_fusion
  273.6 2.6 fusion
  276.2 6.1 %squeeze.44 = f32[3,3,128,768]{2,1,0,3:T(4,128)} reshape(f32[1,1152,4,2,4,24]{1,5,0,4,3,2:T(8,128)} %get-tuple-element.131) | data formatting | bytes 7077888 | tf_op jit(solution)/shard_map/squeeze | solution.py:1100
  282.3 6.2 %copy.41 = f32[3,3,128,768]{3,2,1,0:T(8,128)} copy(f32[3,3,128,768]{2,1,0,3:T(4,128)} %squeeze.44) | data formatting | bytes 7077888
  288.5 3.6 %squeeze.47 = f32[3,3,128,768]{2,1,0,3:T(4,128)} reshape(f32[1,1152,4,2,4,24]{1,5,0,4,3,2:T(8,128)S(1)} %get-tuple-element.130) | data formatting | bytes 7077888 | tf_op jit(solution)/shard_map/squeeze | solution.py:1100
  292.1 0.0 copy-start.5
  292.1 0.0 copy-start
  292.1 6.4 %copy.42 = f32[3,3,128,768]{3,2,1,0:T(8,128)} copy(f32[3,3,128,768]{2,1,0,3:T(4,128)} %squeeze.47) | data formatting | bytes 7077888
  298.5 0.0 copy-done.5
  298.5 1.5 slice_reduce_fusion
  300.0 1.5 dynamic-slice_reduce_fusion
  301.5 0.0 copy-done
  301.5 1.8 copy.50
  303.2 0.0 copy-start.4
  303.2 0.0 copy-start.3
  303.2 6.6 %copy.51 = f32[32,10,14,384]{3,0,2,1:T(8,128)} copy(f32[32,10,14,384]{3,0,2,1:T(8,128)} %bitcast.21) | data formatting | bytes 13762560
  309.8 0.0 copy-done.4
  309.8 0.0 copy-start.2
  309.8 0.0 copy-start.1
  309.8 1.0 copy.52
  310.8 0.0 copy-done.3
  310.9 1.0 copy.53
  311.9 0.0 copy-done.2
  311.9 1.0 copy.54
  312.9 0.0 copy-done.1
  312.9 1.0 copy.55
  (4 shorter events, 0.0 us)
Async XLA Ops:
  292.1 6.4 %copy-start.5 = (f32[2,8,768]{2,1,0:T(8,128)S(1)}, f32[2,8,768]{2,1,0:T(8,128)}, u32[]{:S(2)}) copy-start(f32[2,8,768]{2,1,0:T(8,128)} %get-tuple-element.75) | copy-start | bytes 147460
  292.1 9.4 %copy-start = (bf16[10,14,32,384]{3,2,1,0:T(8,128)(2,1)S(1)}, bf16[10,14,32,384]{3,2,1,0:T(8,128)(2,1)}, u32[]{:S(2)}) copy-start(bf16[10,14,32,384]{3,2,1,0:T(8,128)(2,1)} %get-tuple-element.72) | copy-start | bytes 10321924
  303.2 6.6 %copy-start.4 = (f32[384,768]{1,0:T(8,128)S(1)}, f32[384,768]{1,0:T(8,128)}, u32[]{:S(2)}) copy-start(f32[384,768]{1,0:T(8,128)} %get-tuple-element.155) | copy-start | bytes 3538948
  303.2 7.6 %copy-start.3 = (f32[192,1536]{1,0:T(8,128)S(1)}, f32[192,1536]{1,0:T(8,128)}, u32[]{:S(2)}) copy-start(f32[192,1536]{1,0:T(8,128)} %get-tuple-element.164) | copy-start | bytes 3538948
  309.8 2.0 copy-start.2
  309.8 3.1 copy-start.1

commit v3 on v1

v3 whole, which is shorter than its diff:
```python
import functools
import jax
import jax.numpy as jnp
from jax import lax
from jax.experimental import pallas as pl
from jax.experimental.pallas import tpu as pltpu
from jax.sharding import PartitionSpec as P

INV_BETA = 1.0 / 1.16619037896906
ALPHA_RES = 0.2
GELU_SCALE = 1.7015
STD_EPSILON = 0.0001
ROOT = 0.7978845608028654
CUBIC = 0.044715
MESH = pl.DeviceIdType.MESH
F32 = jnp.float32
BF16 = jnp.bfloat16


def gelu(v):
    return 0.5 * v * (1.0 + jnp.tanh(ROOT * v * (1.0 + CUBIC * v * v)))


def gelu_slope(v):
    square = v * v
    t = jnp.tanh(ROOT * v * (1.0 + CUBIC * square))
    return 0.5 * (1.0 + t) + 0.5 * v * (1.0 - t * t) * ROOT * (1.0 + 3.0 * CUBIC * square)


def split3(x):
    high = x.astype(BF16)
    rest = x - high.astype(F32)
    middle = rest.astype(BF16)
    low = (rest - middle.astype(F32)).astype(BF16)
    return jnp.concatenate([high, middle, low], axis=0)


def dot3(x, w, over):
    rows = x.shape[0]
    y = lax.dot_general(split3(x), w, (((1,), (over,)), ((), ())), preferred_element_type=F32)
    return y[:rows] + y[rows : 2 * rows] + y[2 * rows :]


def dot_nt(x, w):
    return lax.dot_general(x, w, (((1,), (1,)), ((), ())), preferred_element_type=F32)


def dot_tn(x, y):
    return lax.dot_general(x, y, (((0,), (0,)), ((), ())), preferred_element_type=F32)


def place():
    d, c = lax.axis_index("dp"), lax.axis_index("chan")
    xi, ci = c // 2, c % 2
    sib = (d, xi * 2 + (1 - ci))
    xn = (d, (1 - xi) * 2 + ci)
    dg = (d, (1 - xi) * 2 + (1 - ci))
    return d, c, xi, ci, sib, xn, dg


def greet(peers):
    barrier = pltpu.get_barrier_semaphore()
    for peer in peers:
        pl.semaphore_signal(barrier, inc=1, device_id=peer, device_id_type=MESH)
    pl.semaphore_wait(barrier, len(peers))


def remote(src, dst, send, recv, peer):
    return pltpu.make_async_remote_copy(
        src_ref=src, dst_ref=dst, send_sem=send, recv_sem=recv, device_id=peer, device_id_type=MESH
    )


def patches(ref, h, lanes, turned, width):
    shifted = [[ref[h + u, v : v + width, :, lanes] for v in range(3)] for u in range(3)]
    parts = []
    for u in range(3):
        for v in range(3):
            if u == v:
                parts.append(shifted[u][v])
            else:
                parts.append(jnp.where(turned, shifted[v][u], shifted[u][v]))
    whole = jnp.concatenate(parts, axis=-1)
    return whole.reshape(whole.shape[0] * whole.shape[1], whole.shape[2])


def conv_row(ref, h, kernel_ref, turned, width, taps):
    groups = kernel_ref.shape[1] // taps
    outs = []
    for g in range(groups):
        outs.append(
            jnp.dot(
                patches(ref, h, slice(g * taps, (g + 1) * taps), turned, width),
                kernel_ref[:, g * taps : (g + 1) * taps],
                preferred_element_type=F32,
            )
        )
    whole = jnp.concatenate(outs, axis=-1)
    return whole.reshape(width, -1, whole.shape[-1])


class Group:
    def __init__(self, shape):
        YB, ZB = shape
        d, c, xi, ci, sib, xn, dg = place()
        self.zb, self.ci, self.xi, self.sib, self.xn = ZB, ci, xi, sib, xn
        self.yb, self.zz = d % YB, (d // YB) % ZB
        first = (d // (YB * ZB)) * (YB * ZB)
        self.yp = (first + self.zz * YB + (1 - self.yb), c)

        def zpeer(k):
            to = lax.rem(self.zz + k, ZB)
            return to, (first + to * YB + self.yb, c)

        self.zpeer = zpeer
        self.zpeers = [zpeer(k)[1] for k in range(1, ZB)]
        self.others = []
        for k in range(ZB):
            to, same = zpeer(k)
            across = (first + to * YB + (1 - self.yb), c)
            if k:
                self.others.append((self.yb, to, same))
            self.others.append((1 - self.yb, to, across))


def forward_kernel(
    dims, group,
    img, og, rw, ew, dn, up, fw, sw, v_rg, v_rb, v_fg, v_fb, v_sg, v_sb, v_eg, v_eb, v_ub, v_db, v_skip, v_asp,
    o_preE, o_og, o_img, o_as2, o_kr, o_ke, o_preR, o_preF, o_preS, o_PR, o_PF, o_kt1, o_kt2,
    o_kraw, o_ewb, o_fac, o_se, o_sum, o_str, o_ste, o_vb, o_mvec, o_asp,
    imgb, ogb, kraw, ewb, dnb, upb, fraw, sraw, st, kr, ke, k1, k2, kt1, kt2, fac,
    preR, s1, r1, PR, PF, preF, preS, as2, preE, acc, px, hx, cvec, aspv,
    loc_img, ss_img, rs_img, loc, ss, rs, ss_st, rs_st, ss1, rs1, ss2, rs2, sx, rx, outs, q_sem, q_zsem, e_out,
):
    H, W, NI, CS, CH, MH, M, G = dims
    d, c, xi, ci, sib, xn, dg = place()
    at = Group(group)
    greet([sib, xn, dg, at.yp] + at.zpeers)
    mine = pl.ds(pl.multiple_of(ci * NI, NI), NI)
    theirs = pl.ds(pl.multiple_of((1 - ci) * NI, NI), NI)
    clan = pl.ds(pl.multiple_of(ci * CS, CS), CS)
    mlan = pl.ds(pl.multiple_of(xi * MH, MH), MH)
    olan = pl.ds(pl.multiple_of((1 - xi) * MH, MH), MH)
    hlan = pl.ds(pl.multiple_of(xi * CH, CH), CH)
    xlan = pl.ds(pl.multiple_of((1 - xi) * CH, CH), CH)
    yb, zz = at.yb, at.zz
    qx = (1 - xi) * 2 + ci

    def img_send(h):
        return remote(img.at[h, :, theirs, :], imgb.at[h, :, :, clan], ss_img.at[h], rs_img.at[h], sib)

    def img_local(h):
        return pltpu.make_async_copy(img.at[h, :, mine, :], imgb.at[h, :, :, clan], loc_img.at[h])

    locals_ = [
        pltpu.make_async_copy(rw, kraw.at[clan, :], loc.at[0]),
        pltpu.make_async_copy(ew.at[:, :, :, hlan], ewb.at[c], loc.at[1]),
        pltpu.make_async_copy(dn, dnb.at[clan, :], loc.at[2]),
        pltpu.make_async_copy(up, upb.at[:, clan], loc.at[3]),
        pltpu.make_async_copy(fw.at[:, mlan], fraw, loc.at[4]),
        pltpu.make_async_copy(sw.at[:, mlan], sraw, loc.at[5]),
        pltpu.make_async_copy(cvec, o_vb.at[:, clan], loc.at[6]),
        pltpu.make_async_copy(og.at[:, :, mine, :], ogb.at[:, :, :, clan], loc.at[7]),
    ]
    sends = [
        remote(rw, kraw.at[clan, :], ss.at[0], rs.at[0], sib),
        remote(ew.at[:, :, :, hlan], ewb.at[c], ss.at[1], rs.at[1], sib),
        remote(dn, dnb.at[clan, :], ss.at[2], rs.at[2], sib),
        remote(up, upb.at[:, clan], ss.at[3], rs.at[3], sib),
        remote(cvec, o_vb.at[:, clan], ss.at[4], rs.at[4], sib),
        remote(og.at[:, :, theirs, :], ogb.at[:, :, :, clan], ss.at[5], rs.at[5], sib),
        remote(ew.at[yb, zz, :, xlan], ewb.at[c, yb, zz], ss.at[6], rs.at[6], xn),
    ]
    locals_[0].start()
    sends[0].start()

    def start_img(h, carry):
        img_local(h).start()
        img_send(h).start()
        return carry

    lax.fori_loop(0, H, start_img, 0)

    def lane_row(ref, first, count):
        return jnp.concatenate([ref[pl.ds(first + k, 1), :] for k in range(count)], axis=-1)

    per_m, per_c = MH // G, CS // G
    half_rows = [lane_row(v, xi * per_m, per_m) for v in (v_rg, v_rb, v_fg, v_fb, v_sg, v_sb)]
    o_mvec[...] = jnp.concatenate(half_rows + [jnp.zeros((2, MH), F32)], axis=0)
    own_rows = [lane_row(v, 0, per_c) for v in (v_eg, v_eb, v_ub)]
    own_rows.append(jnp.broadcast_to(ALPHA_RES * v_skip[...], (1, CS)))
    cvec[...] = jnp.concatenate(own_rows + [jnp.zeros((4, CS), F32)], axis=0)
    down_bias = lane_row(v_db, 0, M // G)
    turn = jnp.concatenate([v_asp[...].astype(F32), jnp.zeros((1, G - v_asp.shape[1]), F32)], axis=-1)
    aspv[...] = jnp.broadcast_to(turn, (G, G)).T
    asp = aspv[mine, :]
    o_asp[...] = asp
    for k in (4, 5, 1, 6, 2, 3, 7):
        locals_[k].start()

    locals_[0].wait()
    own = kraw[clan, :].astype(F32)
    middle = jnp.mean(own, axis=0, keepdims=True)
    away = own - middle
    st[c] = jnp.concatenate(
        [middle, jnp.sum(away * away, axis=0, keepdims=True), jnp.zeros((6, M), F32)], axis=0
    )
    stats = [remote(st.at[c], st.at[c], ss_st.at[k], rs_st.at[c], peer) for k, peer in enumerate((sib, xn, dg))]
    for s in stats:
        s.start()
    for k in (6, 1, 4, 2, 3, 5):
        sends[k].start()

    edge_w = jnp.zeros((W + 2, NI, MH), BF16)
    for ref in (PR, PF):
        ref[0] = edge_w
        ref[H + 1] = edge_w
        for h in range(1, H + 1):
            ref[h, 0] = edge_w[0]
            ref[h, W + 1] = edge_w[0]
    acc[...] = jnp.zeros_like(acc)

    def stat_of(q):
        return remote(st.at[q], st.at[q], ss_st.at[0], rs_st.at[q], sib)

    for k in (1, 2, 3):
        stat_of(lax.rem(c + k, 4)).wait_recv()
    count = CS
    mean = (st[0, 0:1] + st[1, 0:1] + st[2, 0:1] + st[3, 0:1]) * 0.25
    spread = jnp.zeros_like(mean)
    for q in range(4):
        gap = st[q, 0:1] - mean
        spread = spread + st[q, 1:2] + count * gap * gap
    rate = lax.rsqrt(spread + STD_EPSILON)
    o_str[...] = jnp.concatenate([mean, rate, jnp.zeros((6, M), F32)], axis=0)
    sends[0].wait_recv()

    def kr_block(j, carry):
        rows = pl.ds(pl.multiple_of(j * 128, 128), 128)
        kr[rows, :] = ((kraw[rows, :].astype(F32) - mean) * rate).astype(BF16)
        return carry

    lax.fori_loop(0, CH // 128, kr_block, 0)

    def s1_copy(h):
        return remote(s1.at[h], r1.at[h], ss1.at[h], rs1.at[h], xn)

    def reduce_row(h, carry):
        img_local(h).wait()
        img_send(h).wait_recv()
        scaled = (imgb[h].astype(F32) * INV_BETA).astype(BF16).reshape(W * NI, CH)
        s1[h] = (
            jnp.dot(scaled, kr[:, olan], preferred_element_type=F32).astype(BF16).reshape(W, NI, MH)
        )
        s1_copy(h).start()
        preR[h] = jnp.dot(scaled, kr[:, mlan], preferred_element_type=F32).reshape(W, NI, MH)
        return carry

    lax.fori_loop(0, H, reduce_row, 0)

    def q_slot(z):
        return ewb.at[qx, yb, z]

    def q_copy(k):
        return remote(q_slot(zz), q_slot(zz), q_zsem.at[0, k], q_zsem.at[1, zz], at.zpeer(k)[1])

    def q_y(y):
        return remote(ewb.at[qx, y], ewb.at[qx, y], q_sem.at[0], q_sem.at[1], at.yp)

    def q_core(q):
        return remote(ewb.at[q], ewb.at[q], q_sem.at[2], q_sem.at[3], sib)

    remote(q_slot(zz), q_slot(zz), ss.at[6], rs.at[6], xn).wait_recv()
    for k in range(1, at.zb):
        q_copy(k).start()

    for k, raw, kern, trans in ((4, fraw, k1, kt1), (5, sraw, k2, kt2)):
        locals_[k].wait()
        for g in range(MH // G):
            lanes = slice(g * G, (g + 1) * G)
            w = raw[:, lanes].astype(F32)
            w = w - jnp.mean(w, axis=0, keepdims=True)
            w = w * lax.rsqrt(jnp.sum(w * w, axis=0, keepdims=True) + STD_EPSILON)
            kern[:, lanes] = w.astype(BF16)
            for tap in range(9):
                block = kern[(8 - tap) * G : (9 - tap) * G, lanes].astype(F32)
                trans[tap * G : (tap + 1) * G, lanes] = block.T.astype(BF16)

    for k in range(1, at.zb):
        to, peer = at.zpeer(k)
        remote(q_slot(to), q_slot(to), q_zsem.at[0, k], q_zsem.at[1, to], peer).wait_recv()
    q_y(yb).start()

    def expand_kernel():
        locals_[1].wait()
        sends[1].wait_recv()
        q_core((1 - xi) * 2 + (1 - ci)).wait_recv()
        e_stat = []
        for j in range(CH // G):
            lanes = slice(j * G, (j + 1) * G)
            blocks = [ewb[q, :, :, :, lanes].astype(F32).reshape(M // 4, G) for q in range(4)]
            total = sum(jnp.sum(b, axis=0, keepdims=True) for b in blocks)
            e_mean = total / M
            blocks = [b - e_mean for b in blocks]
            squares = sum(jnp.sum(b * b, axis=0, keepdims=True) for b in blocks)
            e_rate = lax.rsqrt(squares + STD_EPSILON)
            for q in range(4):
                ke[q * (M // 4) : (q + 1) * (M // 4), lanes] = (blocks[q] * e_rate).astype(BF16)
            e_stat.append(jnp.concatenate([e_mean, e_rate, jnp.zeros((6, G), F32)], axis=0))
        o_ste[xi] = jnp.concatenate(e_stat, axis=-1)
        ste_copy.start()

    ste_copy = remote(o_ste.at[xi], o_ste.at[xi], sx.at[2], rx.at[2], xn)
    turned = jnp.broadcast_to((asp > 0.5)[None], (W, NI, G))
    mvec = o_mvec
    reduce_gain, reduce_bias = mvec[0:1, :], mvec[1:2, :]
    first_gain, first_bias = mvec[2:3, :], mvec[3:4, :]
    second_gain, second_bias = mvec[4:5, :], mvec[5:6, :]

    locals_[7].wait()
    sends[5].wait_recv()

    def s2_copy(h):
        return remote(as2.at[h, :, :, mlan], as2.at[h, :, :, mlan], ss2.at[h], rs2.at[h], xn)

    def s2_arrival(h):
        return remote(as2.at[h, :, :, olan], as2.at[h, :, :, olan], ss2.at[h], rs2.at[h], xn)

    pairs = (
        (ogb, o_og), (imgb, o_img), (kr, o_kr), (kt1, o_kt1), (kt2, o_kt2), (kraw, o_kraw), (preR, o_preR),
        (preF, o_preF), (preS, o_preS), (PR, o_PR), (PF, o_PF), (as2, o_as2), (ke, o_ke), (ewb, o_ewb),
    )
    saves = [pltpu.make_async_copy(a, b, outs.at[k]) for k, (a, b) in enumerate(pairs)]

    def wave(t, carry):
        @pl.when(t < H)
        def _():
            s1_copy(t).wait_recv()
            pre = preR[t] + r1[t].astype(F32)
            preR[t] = pre
            PR[t + 1, 1 : W + 1] = (GELU_SCALE * gelu(pre * reduce_gain + reduce_bias)).astype(BF16)

        @pl.when((t >= 1) & (t <= H))
        def _():
            pre = conv_row(PR, t - 1, k1, turned, W, G)
            preF[t - 1] = pre
            PF[t, 1 : W + 1] = (GELU_SCALE * gelu(pre * first_gain + first_bias)).astype(BF16)

        @pl.when((t >= 2) & (t <= H + 1))
        def _():
            pre = conv_row(PF, t - 2, k2, turned, W, G)
            preS[t - 2] = pre
            as2[t - 2, :, :, mlan] = (GELU_SCALE * gelu(pre * second_gain + second_bias)).astype(BF16)
            s2_copy(t - 2).start()

        @pl.when(t == 1)
        def _():
            q_y(1 - yb).wait_recv()
            q_core(qx).start()

        @pl.when(t == 3)
        def _():
            expand_kernel()

        return carry

    lax.fori_loop(0, H + 2, wave, 0)
    for k in (12, 13, 6, 7, 8, 9, 10, 0, 1, 2, 3, 4, 5):
        saves[k].start()

    def expand_row(h, carry):
        s2_arrival(h).wait_recv()
        pre = jnp.dot(as2[h].reshape(W * NI, M), ke[...], preferred_element_type=F32).reshape(W, NI, CH)
        preE[h] = pre
        grad = ogb[h].astype(F32)
        acc[0] += jnp.sum(pre, axis=0)
        acc[1] += jnp.sum(grad, axis=0)
        acc[2] += jnp.sum(grad * pre, axis=0)
        pltpu.make_async_copy(preE.at[h], o_preE.at[h], e_out.at[h]).start()
        return carry

    lax.fori_loop(0, H, expand_row, 0)
    saves[11].start()

    for k in (2, 3, 6):
        locals_[k].wait()
    for k in (2, 3, 4):
        sends[k].wait_recv()
    gain, bias = o_vb[0:1, :], o_vb[1:2, :]
    up_bias, branch_scale = o_vb[2:3, :], o_vb[3:4, :]
    pixels = H * W
    sum_pre, sum_grad, sum_both = acc[0], acc[1], acc[2]
    pooled = gain * (sum_pre * (1.0 / pixels)) + bias
    px[xi] = dot3(pooled, dnb[...], 0)
    p_copy = remote(px.at[xi], px.at[xi], sx.at[0], rx.at[0], xn)
    p_copy.start()
    remote(px.at[1 - xi], px.at[1 - xi], sx.at[0], rx.at[0], xn).wait_recv()
    down = px[0] + px[1] + down_bias
    hidden = gelu(down)
    upper = dot3(hidden, upb[...], 0) + up_bias
    sigma = 1.0 / (1.0 + jnp.exp(-upper))
    gating = 2.0 * sigma
    grad_gating_raw = gain * sum_both + bias * sum_grad
    grad_upper = branch_scale * grad_gating_raw * 2.0 * sigma * (1.0 - sigma)
    hx[xi] = dot3(grad_upper, upb[...], 1)
    h_copy = remote(hx.at[xi], hx.at[xi], sx.at[1], rx.at[1], xn)
    h_copy.start()
    remote(hx.at[1 - xi], hx.at[1 - xi], sx.at[1], rx.at[1], xn).wait_recv()
    grad_down = (hx[0] + hx[1]) * gelu_slope(down)
    grad_pooled = dot3(grad_down, dnb[...], 1)
    scaled_gate = branch_scale * gating
    pool_part = grad_pooled * (1.0 / pixels)
    o_se[0] = scaled_gate
    o_se[1] = pool_part
    for s in range(2):
        shard = slice(s * CS, (s + 1) * CS)
        fac[s] = jnp.concatenate([pooled[:, shard], grad_down, hidden, grad_upper[:, shard]], axis=-1).astype(BF16)
    fac_save = pltpu.make_async_copy(fac, o_fac, outs.at[14])
    fac_save.start()
    gain_grad = jnp.sum(scaled_gate * sum_both + pool_part * sum_pre, axis=0, keepdims=True)
    bias_grad = jnp.sum(scaled_gate * sum_grad + grad_pooled, axis=0, keepdims=True)
    up_bias_grad = jnp.sum(grad_upper, axis=0, keepdims=True)
    skip_row = ALPHA_RES * jnp.sum(gating * grad_gating_raw, axis=0, keepdims=True)
    down_bias_grad = jnp.sum(grad_down, axis=0, keepdims=True)
    o_sum[...] = jnp.concatenate(
        [gain_grad, bias_grad, up_bias_grad, skip_row, down_bias_grad, jnp.zeros((3, CH), F32)], axis=0
    )

    remote(o_ste.at[1 - xi], o_ste.at[1 - xi], sx.at[2], rx.at[2], xn).wait_recv()
    for s in (ste_copy, p_copy, h_copy, q_y(yb), q_core(qx)):
        s.wait_send()
    for k in range(1, at.zb):
        q_copy(k).wait_send()
    for s in sends + stats:
        s.wait_send()

    def drain(h, carry):
        img_send(h).wait_send()
        s1_copy(h).wait_send()
        s2_copy(h).wait_send()
        pltpu.make_async_copy(preE.at[h], o_preE.at[h], e_out.at[h]).wait()
        return carry

    lax.fori_loop(0, H, drain, 0)
    for s in saves:
        s.wait()
    fac_save.wait()


class DeviceSum:
    def __init__(self, at, block, rows, sbuf, ysend, ybuf, zsend, zbuf, sem, zsem):
        self.at, self.block, self.rows = at, block, rows
        self.sbuf, self.ysend, self.ybuf, self.zsend, self.zbuf = sbuf, ysend, ybuf, zsend, zbuf
        self.sem, self.zsem = sem, zsem
        self.count = sbuf.shape[0]
        self.half = rows // 2

    def core_copy(self, b):
        ref, base = self.block(b, 1 - self.at.ci)
        src = ref.at[pl.ds(pl.multiple_of(base, 16), self.rows), :]
        return remote(src, self.sbuf.at[b], self.sem.at[2 + 2 * b], self.sem.at[3 + 2 * b], self.at.sib)

    def y_copy(self):
        return remote(self.ysend, self.ybuf, self.sem.at[0], self.sem.at[1], self.at.yp)

    def z_copy(self, k):
        to, peer = self.at.zpeer(k)
        zz = self.at.zz
        return remote(self.zsend.at[to], self.zbuf.at[zz], self.zsem.at[0, k], self.zsem.at[1, zz], peer)

    def z_arrival(self, k):
        to, peer = self.at.zpeer(k)
        return remote(self.zsend.at[to], self.zbuf.at[to], self.zsem.at[0, k], self.zsem.at[1, to], peer)

    def core_sum(self, b, y):
        ref, base = self.block(b, self.at.ci)
        at = pl.multiple_of(y * self.half, 16)
        mine = ref[pl.ds(pl.multiple_of(base + at, 16), self.half), :]
        return mine.astype(F32) + self.sbuf[b, pl.ds(at, self.half), :].astype(F32)

    def to_core(self):
        for b in range(self.count):
            self.core_copy(b).start()

    def to_y(self):
        for b in range(self.count):
            self.core_copy(b).wait_recv()
        for b in range(self.count):
            self.ysend[b] = self.core_sum(b, 1 - self.at.yb).astype(BF16)
        self.y_copy().start()

    def to_z(self):
        self.y_copy().wait_recv()
        piece = self.half // self.at.zb
        for b in range(self.count):
            total = self.core_sum(b, self.at.yb) + self.ybuf[b].astype(F32)
            for z in range(self.at.zb):
                self.zsend[z, b] = total[z * piece : (z + 1) * piece].astype(BF16)
        for k in range(1, self.at.zb):
            self.z_copy(k).start()

    def totals(self):
        for k in range(1, self.at.zb):
            self.z_arrival(k).wait_recv()
        outs = []
        for b in range(self.count):
            total = self.zsend[self.at.zz, b].astype(F32)
            for k in range(1, self.at.zb):
                total = total + self.zbuf[self.at.zpeer(k)[0], b].astype(F32)
            outs.append(total.astype(BF16))
        return outs

    def finish_cores(self):
        for b in range(self.count):
            self.core_copy(b).wait_send()

    def finish(self):
        self.y_copy().wait_send()
        for k in range(1, self.at.zb):
            self.z_copy(k).wait_send()


class Spread:
    def __init__(self, at, piece, full, sem, zsem, lanes=None):
        self.at, self.piece, self.full, self.sem, self.zsem, self.lanes = at, piece, full, sem, zsem, lanes

    def slot(self, y, z=None):
        if self.lanes is None:
            return self.full.at[y] if z is None else self.full.at[y, z]
        return self.full.at[y, :, :, self.lanes] if z is None else self.full.at[y, z, :, self.lanes]

    def keep(self):
        return pltpu.make_async_copy(self.piece, self.slot(self.at.yb, self.at.zz), self.sem.at[2])

    def z_copy(self, k):
        own = self.slot(self.at.yb, self.at.zz)
        return remote(self.piece, own, self.zsem.at[0, k], self.zsem.at[1, self.at.zz], self.at.zpeer(k)[1])

    def y_copy(self):
        own = self.slot(self.at.yb)
        return remote(own, own, self.sem.at[0], self.sem.at[1], self.at.yp)

    def to_z(self):
        self.keep().start()
        for k in range(1, self.at.zb):
            self.z_copy(k).start()

    def to_y(self):
        self.keep().wait()
        for k in range(1, self.at.zb):
            to, peer = self.at.zpeer(k)
            slot = self.slot(self.at.yb, to)
            remote(slot, slot, self.zsem.at[0, k], self.zsem.at[1, to], peer).wait_recv()
        self.y_copy().start()

    def arrive(self):
        slot = self.slot(1 - self.at.yb)
        remote(slot, slot, self.sem.at[0], self.sem.at[1], self.at.yp).wait_recv()

    def finish(self):
        for k in range(1, self.at.zb):
            self.z_copy(k).wait_send()
        self.y_copy().wait_send()


class SpreadYZ(Spread):
    def y_copy(self):
        own = self.slot(self.at.yb, self.at.zz)
        return remote(self.piece, own, self.sem.at[0], self.sem.at[1], self.at.yp)

    def z_copy(self, k):
        own = self.full.at[:, self.at.zz]
        return remote(own, own, self.zsem.at[0, k], self.zsem.at[1, self.at.zz], self.at.zpeer(k)[1])

    def to_y(self):
        self.keep().start()
        self.y_copy().start()

    def to_z(self):
        self.keep().wait()
        slot = self.slot(1 - self.at.yb, self.at.zz)
        remote(slot, slot, self.sem.at[0], self.sem.at[1], self.at.yp).wait_recv()
        for k in range(1, self.at.zb):
            self.z_copy(k).start()

    def arrive(self):
        for k in range(1, self.at.zb):
            to, peer = self.at.zpeer(k)
            slot = self.full.at[:, to]
            remote(slot, slot, self.zsem.at[0, k], self.zsem.at[1, to], peer).wait_recv()


class DirectSum:
    def __init__(self, at, block, rows, sbuf, dsend, dbuf, fin, full, lanes, sem, send_sem, recv_sem):
        self.at, self.block, self.rows = at, block, rows
        self.sbuf, self.dsend, self.dbuf, self.fin, self.full, self.lanes = sbuf, dsend, dbuf, fin, full, lanes
        self.sem, self.send_sem, self.recv_sem = sem, send_sem, recv_sem

    def core_copy(self):
        ref, base = self.block(1 - self.at.ci)
        src = ref.at[pl.ds(pl.multiple_of(base, 16), self.rows), :]
        return remote(src, self.sbuf, self.sem.at[0], self.sem.at[1], self.at.sib)

    def slot(self, y, z):
        return self.full.at[y, z, :, self.lanes]

    def copy(self, phase, k):
        y, z, peer = self.at.others[k]
        yb, zz = self.at.yb, self.at.zz
        if phase == 0:
            src, dst = self.dsend.at[y, z], self.dbuf.at[yb, zz]
        else:
            src, dst = self.fin, self.slot(yb, zz)
        return remote(src, dst, self.send_sem.at[phase, k], self.recv_sem.at[phase, yb, zz], peer)

    def arrival(self, phase, k):
        y, z, peer = self.at.others[k]
        dst = self.dbuf.at[y, z] if phase == 0 else self.slot(y, z)
        return remote(dst, dst, self.send_sem.at[phase, k], self.recv_sem.at[phase, y, z], peer)

    def to_core(self):
        self.core_copy().start()

    def to_owners(self):
        self.core_copy().wait_recv()
        ref, base = self.block(self.at.ci)
        ys, zs, piece = self.dsend.shape[0], self.dsend.shape[1], self.dsend.shape[2]
        half = self.rows // ys
        for y in range(ys):
            mine = ref[pl.ds(pl.multiple_of(base + y * half, 16), half), :]
            total = mine.astype(F32) + self.sbuf[y * half : (y + 1) * half, :].astype(F32)
            for z in range(zs):
                self.dsend[y, z] = total[z * piece : (z + 1) * piece].astype(BF16)
        for k in range(len(self.at.others)):
            self.copy(0, k).start()

    def keep(self):
        return pltpu.make_async_copy(self.fin, self.slot(self.at.yb, self.at.zz), self.sem.at[2])

    def to_all(self):
        total = self.dsend[self.at.yb, self.at.zz].astype(F32)
        for k, (y, z, _) in enumerate(self.at.others):
            self.arrival(0, k).wait_recv()
            total = total + self.dbuf[y, z].astype(F32)
        self.fin[...] = total.astype(BF16)
        self.keep().start()
        for k in range(len(self.at.others)):
            self.copy(1, k).start()

    def arrive(self):
        for k in range(len(self.at.others)):
            self.arrival(1, k).wait_recv()
        self.keep().wait()

    def finish(self):
        self.core_copy().wait_send()
        for phase in range(2):
            for k in range(len(self.at.others)):
                self.copy(phase, k).wait_send()


class VectorSum:
    def __init__(self, at, vs, vy, vz, vx, sem, zsem):
        self.at = at
        self.vs, self.vy, self.vz, self.vx = vs, vy, vz, vx
        self.sem, self.zsem = sem, zsem

    def pair(self, ref, slot, k, peer):
        return remote(ref.at[slot], ref.at[slot], self.sem.at[2 * k], self.sem.at[2 * k + 1], peer)

    def z_pair(self, slot, k, peer):
        return remote(self.vz.at[slot], self.vz.at[slot], self.zsem.at[0, k], self.zsem.at[1, slot], peer)

    def to_core(self, value):
        self.vs[self.at.ci] = value
        self.pair(self.vs, self.at.ci, 0, self.at.sib).start()

    def to_y(self):
        self.pair(self.vs, 1 - self.at.ci, 0, self.at.sib).wait_recv()
        self.vy[self.at.yb] = self.vs[0] + self.vs[1]
        self.pair(self.vy, self.at.yb, 1, self.at.yp).start()

    def to_z(self):
        self.pair(self.vy, 1 - self.at.yb, 1, self.at.yp).wait_recv()
        self.vz[self.at.zz] = self.vy[0] + self.vy[1]
        for k in range(1, self.at.zb):
            self.z_pair(self.at.zz, k, self.at.zpeer(k)[1]).start()

    def to_x(self):
        for k in range(1, self.at.zb):
            to, peer = self.at.zpeer(k)
            self.z_pair(to, k, peer).wait_recv()
        total = self.vz[0]
        for z in range(1, self.at.zb):
            total = total + self.vz[z]
        self.vx[self.at.xi] = total
        self.pair(self.vx, self.at.xi, 2, self.at.xn).start()

    def arrive(self):
        self.pair(self.vx, 1 - self.at.xi, 2, self.at.xn).wait_recv()

    def finish(self):
        self.pair(self.vs, self.at.ci, 0, self.at.sib).wait_send()
        self.pair(self.vy, self.at.yb, 1, self.at.yp).wait_send()
        for k in range(1, self.at.zb):
            self.z_pair(self.at.zz, k, self.at.zpeer(k)[1]).wait_send()
        self.pair(self.vx, self.at.xi, 2, self.at.xn).wait_send()


def backward_kernel(
    dims, group,
    i_preE, i_og, i_img, i_as2, i_kr, i_ke, i_preR, i_preF, i_preS, i_PR, i_PF, i_kt1, i_kt2,
    i_kraw, i_ewb, i_fac, se, fsum, str_, ste, vb, mvec, asp,
    o_block, o_gs, o_G, o_Ge, o_Gr, o_dd, o_du, va, vl, o_rs, o_es,
    preE, gas, ogb, imgb, as2, kr, ke, preR, preF, preS, PR, PF, kt1, kt2, raw,
    wide, s3, r3, GS, GF, bst, gst, Dx, Da, Dt, bsum, estat, rstat, FB,
    e_s, e_ys, e_yb, e_zs, e_zb, e_x, e_fin,
    ra_s, ra_ys, ra_yb, ra_zs, ra_zb, ra_fin, rb_s, rb_send, rb_buf, rb_fin,
    d_s, d_ys, d_yb, d_zs, d_zb, d_fin,
    va_s, va_y, va_z, vl_s, vl_y, vl_z,
    ld, ldr, ldp, ss3, rs3, ss4, rs4, b_loc, b_ss, b_rs, g_loc, g_ss, g_rs,
    e_sem, e_zsem, es_sem, es_zsem, ra_sem, ra_zsem, ras_sem, ras_zsem, rb_sem, rb_ss, rb_rs,
    d_sem, d_zsem, ds_sem, ds_zsem, dc_sem, va_sem, va_zsem, vl_sem, vl_zsem, f_sem, f_zsem, x_sem, credit,
):
    H, W, NI, CS, CH, MH, M, G = dims
    d, c, xi, ci, sib, xn, dg = place()
    at = Group(group)
    yb, zz = at.yb, at.zz
    NG = MH // G
    rows_all = H * W * NI
    RW = W * NI
    pairs = (
        (i_kr, kr), (i_ke, ke), (i_kt1, kt1), (i_kt2, kt2), (i_PR, PR), (i_PF, PF), (i_as2, as2),
        (i_kraw, raw), (i_ewb, raw), (i_fac.at[ci], FB.at[yb, zz, ci]),
    )
    loads = [pltpu.make_async_copy(a, b, ld.at[k]) for k, (a, b) in enumerate(pairs)]
    slots, ring = bst.shape[0], preE.shape[0]
    gpe = pl.ds(0, CH)

    def row_load(h, k):
        src, dst = ((i_preE, preE.at[lax.rem(h, ring)]), (i_og, ogb.at[h]), (i_img, imgb.at[h]))[k]
        return pltpu.make_async_copy(src.at[h], dst, ldr.at[h, k])

    loads[1].start()
    for h in range(ring):
        for k in range(3):
            row_load(h, k).start()
    loads[9].start()

    def pre_load(k, h):
        src, dst = ((i_preS, preS), (i_preF, preF), (i_preR, preR))[k]
        return pltpu.make_async_copy(src.at[h], dst.at[lax.rem(h, 4)], ldp.at[h, k])

    greet([sib, xn] + [peer for _, _, peer in at.others])
    fac_core = remote(i_fac.at[1 - ci], FB.at[yb, zz, ci], f_sem.at[2], f_sem.at[3], sib)
    fac_core.start()
    for k in (6, 8, 5, 3, 4, 2, 0):
        loads[k].start()

    mine = pl.ds(pl.multiple_of(ci * NI, NI), NI)
    clan = pl.ds(pl.multiple_of(ci * CS, CS), CS)
    slan = pl.ds(pl.multiple_of((1 - ci) * CS, CS), CS)
    mlan = pl.ds(pl.multiple_of(xi * MH, MH), MH)
    olan = pl.ds(pl.multiple_of((1 - xi) * MH, MH), MH)
    hlan = pl.ds(pl.multiple_of(xi * CH, CH), CH)
    edge_w = jnp.zeros((W + 2, NI, MH), BF16)
    for ref in (GS, GF):
        ref[0] = edge_w
        ref[H + 1] = edge_w
        for h in range(1, H + 1):
            ref[h, 0] = edge_w[0]
            ref[h, W + 1] = edge_w[0]
    bsum[...] = jnp.zeros_like(bsum)
    estat[...] = jnp.zeros_like(estat)
    rstat[...] = jnp.zeros_like(rstat)

    gain, bias = vb[0:1, :], vb[1:2, :]
    scaled_gate, pool_part = se[0], se[1]

    def row_out(stage, out, loc, ss, rs):
        def local(h):
            return pltpu.make_async_copy(stage.at[lax.rem(h, slots), :, :, clan], out.at[h, :, mine, :], loc.at[h])

        def send(h):
            return remote(
                stage.at[lax.rem(h, slots), :, :, slan], out.at[h, :, mine, :], ss.at[h], rs.at[h], sib
            )

        return local, send

    block_local, block_send = row_out(bst, o_block, b_loc, b_ss, b_rs)
    gs_local, gs_send = row_out(gst, o_gs, g_loc, g_ss, g_rs)

    def s3_copy(h):
        return remote(s3.at[h], r3.at[h], ss3.at[h], rs3.at[h], xn)

    def row_at(h):
        return pl.ds(pl.multiple_of(h * RW, RW), RW)

    loads[1].wait()

    def expand_row(h, carry):
        for k in range(3):
            row_load(h, k).wait()

        @pl.when(h >= slots)
        def _():
            block_local(h - slots).wait()
            block_send(h - slots).wait_send()

        pre = preE[lax.rem(h, ring)]
        grad = ogb[h].astype(F32) * scaled_gate + pool_part
        piece = (grad * gain).astype(BF16).reshape(RW, CH)
        s3[h] = dot_nt(piece, ke[olan, :]).astype(BF16).reshape(W, NI, MH)
        s3_copy(h).start()
        wide[row_at(h), gpe] = piece
        gas[h] = dot_nt(piece, ke[mlan, :]).reshape(W, NI, MH)
        out = pre * gain + bias
        bst[lax.rem(h, slots)] = (imgb[h].astype(F32) + out * scaled_gate).astype(BF16)
        block_local(h).start()
        block_send(h).start()

        @pl.when(h + ring < H)
        def _():
            for k in range(3):
                row_load(h + ring, k).start()

        return carry

    lax.fori_loop(0, H, expand_row, 0)
    pre_load(0, 0).start()
    pre_load(0, 1).start()
    pre_load(1, 0).start()

    loads[9].wait()
    remote(i_fac.at[1 - ci], FB.at[yb, zz, 1 - ci], f_sem.at[2], f_sem.at[3], sib).wait_recv()

    def f_copy(k):
        own = FB.at[yb, zz]
        return remote(own, own, f_zsem.at[0, k], f_zsem.at[1, zz], at.zpeer(k)[1])

    def f_y():
        return remote(FB.at[yb], FB.at[yb], f_sem.at[0], f_sem.at[1], at.yp)

    for k in range(1, at.zb):
        f_copy(k).start()

    loads[6].wait()
    quarter = e_s.shape[1]
    step = 256
    e_mean = ste[xi, 0:1, :]

    def expand_kernel_grad(j, carry):
        lanes = pl.ds(pl.multiple_of(j * step, step), step)
        left = as2[:, :, :, lanes].reshape(rows_all, step)
        Dx[lanes, :] = dot_tn(left, wide[:, gpe]).astype(BF16)
        return carry

    lax.fori_loop(0, M // step, expand_kernel_grad, 0)
    pl.semaphore_signal(credit, inc=1, device_id=xn, device_id_type=MESH)
    gpr = as2

    sum_e = DeviceSum(
        at, lambda b, half: (Dx, b * MH + half * quarter), quarter, e_s, e_ys, e_yb, e_zs, e_zb, e_sem, e_zsem
    )
    sum_e.to_core()
    spread_e = SpreadYZ(at, e_fin, o_Ge, es_sem, es_zsem)

    def e_cross(x):
        lanes = pl.ds(pl.multiple_of(x * CH, CH), CH)
        return remote(e_x.at[1 - x], e_fin.at[:, lanes], x_sem.at[0], x_sem.at[1], xn)

    loads[8].wait()
    for q in range(4):
        grads = Dx[q * quarter : (q + 1) * quarter, :].astype(F32)
        away = raw[q * quarter : (q + 1) * quarter, :].astype(F32) - e_mean
        estat[0:1, :] += jnp.sum(grads, axis=0, keepdims=True)
        estat[1:2, :] += jnp.sum(grads * away, axis=0, keepdims=True)
    loads[7].start()
    sum_a = VectorSum(at, va_s, va_y, va_z, va, va_sem, va_zsem)
    sum_a.to_core(jnp.concatenate([fsum[0:5, :], estat[0:2, :], jnp.zeros((1, CH), F32)], axis=0))

    for k in (5, 3, 4, 2, 0):
        loads[k].wait()
    turned = jnp.broadcast_to((asp[...] > 0.5)[None], (W, NI, G))
    reduce_gain, reduce_bias = mvec[0:1, :], mvec[1:2, :]
    first_gain, first_bias = mvec[2:3, :], mvec[3:4, :]
    second_gain, second_bias = mvec[4:5, :], mvec[5:6, :]

    def s4_copy(h):
        return remote(gpr.at[h, :, :, mlan], gpr.at[h, :, :, mlan], ss4.at[h], rs4.at[h], xn)

    def s4_arrival(h):
        return remote(gpr.at[h, :, :, olan], gpr.at[h, :, :, olan], ss4.at[h], rs4.at[h], xn)

    def tally(row, grad, pre):
        flat = (grad * pre).reshape(RW, MH)
        bsum[row : row + 1, :] += jnp.sum(flat, axis=0, keepdims=True)
        bsum[row + 1 : row + 2, :] += jnp.sum(grad.reshape(RW, MH), axis=0, keepdims=True)

    def image_row(h):
        s4_arrival(h).wait_recv()

        @pl.when(h >= slots)
        def _():
            gs_local(h - slots).wait()
            gs_send(h - slots).wait_send()

        gst[lax.rem(h, slots)] = dot_nt(gpr[h].reshape(RW, M), kr[...]).astype(BF16).reshape(W, NI, CH)
        gs_local(h).start()
        gs_send(h).start()

    part = H // 2

    def group_term(act, cot, g, low):
        lanes = pl.ds(pl.multiple_of(g * G, G), G)

        def fill(h, carry):
            wide[row_at(h), :] = patches(act, low + h, lanes, turned, W)
            return carry

        lax.fori_loop(0, part, fill, 0)
        right = cot[1 + low : 1 + low + part, 1 : W + 1, :, lanes].reshape(part * RW, G)
        return dot_tn(right, wide[0 : part * RW, :])

    def first_half(b, act, cot, g):
        Da[b, pl.ds(pl.multiple_of(g * G, G), G), :] = group_term(act, cot, g, 0)

    def second_half(b, act, cot, low, high):
        def one(g, carry):
            lanes = pl.ds(pl.multiple_of(g * G, G), G)
            total = Da[b, lanes, :] + group_term(act, cot, g, part)
            for tap in range(9):
                block = total[:, tap * G : (tap + 1) * G]
                Dt[b, tap * G : (tap + 1) * G, lanes] = block.T.astype(BF16)
            return carry

        lax.fori_loop(low, high, one, 0)

    def wave(t, carry):
        @pl.when(t + 2 < H)
        def _():
            pre_load(0, t + 2).start()

        @pl.when(t + 1 < H)
        def _():
            pre_load(1, t + 1).start()

        @pl.when(t < H)
        def _():
            pre_load(2, t).start()

        @pl.when(t < H)
        def _():
            pre_load(0, t).wait()
            s3_copy(t).wait_recv()
            cot = (gas[t] + r3[t].astype(F32)).astype(BF16).astype(F32)
            pre = preS[lax.rem(t, 4)]
            grad = cot * (GELU_SCALE * gelu_slope(pre * second_gain + second_bias))
            tally(4, grad, pre)
            GS[t + 1, 1 : W + 1] = (grad * second_gain).astype(BF16)

        @pl.when((t >= 1) & (t <= H))
        def _():
            pre_load(1, t - 1).wait()
            cot = conv_row(GS, t - 1, kt2, turned, W, G)
            pre = preF[lax.rem(t - 1, 4)]
            grad = cot * (GELU_SCALE * gelu_slope(pre * first_gain + first_bias))
            tally(2, grad, pre)
            GF[t, 1 : W + 1] = (grad * first_gain).astype(BF16)

        @pl.when(t == 2)
        def _():
            pl.semaphore_wait(credit, 1)

        @pl.when((t >= 2) & (t <= H + 1))
        def _():
            pre_load(2, t - 2).wait()
            cot = conv_row(GF, t - 2, kt1, turned, W, G)
            pre = preR[lax.rem(t - 2, 4)]
            grad = cot * (GELU_SCALE * gelu_slope(pre * reduce_gain + reduce_bias))
            tally(0, grad, pre)
            gpr[t - 2, :, :, mlan] = (grad * reduce_gain).astype(BF16)
            s4_copy(t - 2).start()

        @pl.when(t == 1)
        def _():
            sum_e.to_y()
            sum_a.to_y()

        @pl.when(t == 2)
        def _():
            for k in range(1, at.zb):
                to, peer = at.zpeer(k)
                slot = FB.at[yb, to]
                remote(slot, slot, f_zsem.at[0, k], f_zsem.at[1, to], peer).wait_recv()
            f_y().start()

        @pl.when(t == 3)
        def _():
            sum_e.to_z()
            sum_a.to_z()

        @pl.when(t == 4)
        def _():
            sum_a.to_x()
            outs = sum_e.totals()
            for b in range(2):
                e_x[b] = outs[b]
            e_fin[:, hlan] = e_x[xi]
            e_cross(xi).start()

        @pl.when(t == H)
        def _():
            e_cross(1 - xi).wait_recv()
            spread_e.to_y()

        @pl.when((t >= 5) & (t < 5 + NG))
        def _():
            first_half(1, PF, GS, t - 5)

        @pl.when((t >= 6) & (t < 6 + NG))
        def _():
            first_half(0, PR, GF, t - 6)

        return carry

    lax.fori_loop(0, H + 2, wave, 0)

    half = 9 * G // 2

    def grouped_jobs(b):
        job = DeviceSum(
            at, lambda _, h: (Dt.at[b], h * half), half, d_s.at[b], d_ys.at[b], d_yb.at[b], d_zs.at[b], d_zb.at[b],
            d_sem.at[b], d_zsem.at[b],
        )
        return job, Spread(at, d_fin.at[b], o_G.at[b, ci], ds_sem.at[b], ds_zsem.at[b], mlan)

    def d_cross(b, y, lanes):
        block = o_G.at[b, ci, y, :, :, lanes]
        return remote(block, block, dc_sem.at[b, y, 0], dc_sem.at[b, y, 1], xn)

    def d_core(b, h, y, lanes, k):
        block = o_G.at[b, h, y, :, :, lanes]
        return remote(block, block, dc_sem.at[b, y, 2 + 2 * k], dc_sem.at[b, y, 3 + 2 * k], sib)

    def reduce_kernel_grad(lanes_m, base):
        r_step = 256
        mean = str_[0:1, lanes_m]

        def one(j, carry):
            lanes = pl.ds(pl.multiple_of(j * r_step, r_step), r_step)
            left = (imgb[:, :, :, lanes].astype(F32) * INV_BETA).astype(BF16).reshape(rows_all, r_step)
            grads = dot_tn(left, gpr[:, :, :, lanes_m].reshape(rows_all, MH))
            rstat[0:1, lanes_m] += jnp.sum(grads, axis=0, keepdims=True)
            rstat[1:2, lanes_m] += jnp.sum(grads * (raw[lanes, lanes_m].astype(F32) - mean), axis=0, keepdims=True)
            Dx[lanes, base : base + MH] = grads.astype(BF16)
            return carry

        lax.fori_loop(0, CH // r_step, one, 0)

    def reduce_jobs(base, lanes, bufs, sem, zsem, fin, s_sem, s_zsem):
        job = DeviceSum(at, lambda b, h: (Dx.at[:, base : base + MH], h * CS), CS, *bufs, sem, zsem)
        return job, Spread(at, fin, o_Gr, s_sem, s_zsem, lanes)

    sum_1, spread_1 = grouped_jobs(0)
    sum_2, spread_2 = grouped_jobs(1)
    sum_ra, spread_ra = reduce_jobs(
        0, mlan, (ra_s, ra_ys, ra_yb, ra_zs, ra_zb), ra_sem, ra_zsem, ra_fin, ras_sem, ras_zsem
    )
    sum_rb = DirectSum(
        at, lambda h: (Dx.at[:, MH : 2 * MH], h * CS), CS, rb_s, rb_send, rb_buf, rb_fin, o_Gr, olan, rb_sem, rb_ss, rb_rs
    )
    sum_l = VectorSum(at, vl_s, vl_y, vl_z, vl, vl_sem, vl_zsem)

    rows = iter(range(H))

    def image(count):
        for _ in range(count):
            for h in rows:
                image_row(h)
                break

    spread_e.to_z()
    second_half(1, PF, GS, 0, NG)
    sum_2.to_core()
    second_half(0, PR, GF, 0, 1)
    sum_2.to_y()
    second_half(0, PR, GF, 1, NG)
    sum_1.to_core()
    sum_2.to_z()
    loads[7].wait()
    sum_e.finish_cores()
    reduce_kernel_grad(mlan, 0)
    sum_ra.to_core()
    sum_1.to_y()
    d_fin[1] = sum_2.totals()[0]
    spread_2.to_z()
    image(2)
    sum_ra.to_y()
    sum_1.to_z()
    image(2)
    spread_2.to_y()
    d_core(1, ci, yb, mlan, 0).start()
    d_cross(1, yb, mlan).start()
    image(1)
    d_fin[0] = sum_1.totals()[0]
    spread_1.to_z()
    sum_ra.to_z()
    image(2)
    spread_1.to_y()
    d_core(0, ci, yb, mlan, 0).start()
    d_cross(0, yb, mlan).start()
    spread_2.arrive()
    d_core(1, ci, 1 - yb, mlan, 0).start()
    d_cross(1, 1 - yb, mlan).start()
    image(1)
    ra_fin[...] = sum_ra.totals()[0]
    spread_ra.to_z()
    for h in rows:
        image_row(h)
    reduce_kernel_grad(olan, MH)
    sum_rb.to_core()
    rstat[2:8, mlan] = bsum[0:6, :]
    sum_l.to_core(rstat[...])
    spread_1.arrive()
    d_core(0, ci, 1 - yb, mlan, 0).start()
    d_cross(0, 1 - yb, mlan).start()
    sum_rb.to_owners()
    sum_l.to_y()
    spread_ra.to_y()
    sum_l.to_z()
    sum_rb.to_all()
    sum_l.to_x()
    d_cross(1, yb, olan).wait_recv()
    d_core(1, ci, yb, olan, 1).start()
    remote(FB.at[1 - yb], FB.at[1 - yb], f_sem.at[0], f_sem.at[1], at.yp).wait_recv()
    fac_all = FB[...].reshape(-1, FB.shape[-1])
    o_dd[...] = dot_tn(fac_all[:, 0:CS], fac_all[:, CS : CS + M]).astype(BF16)
    o_du[...] = dot_tn(fac_all[:, CS + M : CS + 2 * M], fac_all[:, CS + 2 * M :]).astype(BF16)
    d_cross(0, yb, olan).wait_recv()
    d_core(0, ci, yb, olan, 1).start()
    d_cross(1, 1 - yb, olan).wait_recv()
    d_core(1, ci, 1 - yb, olan, 1).start()
    d_cross(0, 1 - yb, olan).wait_recv()
    d_core(0, ci, 1 - yb, olan, 1).start()
    spread_e.arrive()
    spread_ra.arrive()
    sum_rb.arrive()
    sum_a.arrive()
    sum_l.arrive()
    late = vl[0] + vl[1]
    o_rs[...] = jnp.concatenate([str_[0:2, :], late[0:1] * (1.0 / (4 * CS)), late[1:2]], axis=0)
    for x in range(2):
        o_es[:, x * CH : (x + 1) * CH] = jnp.concatenate(
            [ste[x, 0:2, :], va[x, 5:6, :] * (1.0 / (4 * quarter)), va[x, 6:7, :]], axis=0
        )
    for b in range(2):
        for y in range(2):
            for k, lanes in ((0, mlan), (1, olan)):
                d_core(b, 1 - ci, y, lanes, k).wait_recv()

    fac_core.wait_send()
    for k in range(1, at.zb):
        f_copy(k).wait_send()
    f_y().wait_send()
    e_cross(xi).wait_send()
    for b in range(2):
        for y in range(2):
            d_cross(b, y, mlan).wait_send()
            d_core(b, ci, y, mlan, 0).wait_send()
            d_core(b, ci, y, olan, 1).wait_send()
    for job in (sum_1, sum_2, sum_ra):
        job.finish_cores()
    for job in (sum_e, spread_e, sum_a, sum_1, sum_2, spread_1, spread_2, sum_ra, spread_ra, sum_rb, sum_l):
        job.finish()

    def drain(h, carry):
        s3_copy(h).wait_send()
        s4_copy(h).wait_send()
        block_send(h).wait_recv()
        gs_send(h).wait_recv()
        return carry

    lax.fori_loop(0, H, drain, 0)
    for h in range(H - slots, H):
        block_local(h).wait()
        block_send(h).wait_send()
        gs_local(h).wait()
        gs_send(h).wait_send()


def finish_kernel(steps, og, gs, g1, g2, fw, sw, gr, rw, rs, ge, ew, es, dd, du,
                  o_ig, o_g1, o_g2, o_rw, o_ew, o_dd, o_du):
    o_ig[...] = og[...].astype(F32) + INV_BETA * gs[...].astype(F32)

    @pl.when(pl.program_id(0) < steps)
    def _():
        for grad, weight, out in ((g1, fw, o_g1), (g2, sw, o_g2)):
            total, away = grad[...].astype(F32), weight[...].astype(F32)
            away = away - jnp.mean(away, axis=0, keepdims=True)
            rate = lax.rsqrt(jnp.sum(away * away, axis=0, keepdims=True) + STD_EPSILON)
            cross = jnp.sum(total * away, axis=0, keepdims=True) * (rate * rate * rate)
            out[...] = rate * (total - jnp.mean(total, axis=0, keepdims=True)) - away * cross
        for grad, weight, rows, out in ((gr, rw, rs, o_rw), (ge, ew, es, o_ew)):
            mean, rate, low, cross = (rows[k : k + 1, :] for k in range(4))
            away = weight[...].astype(F32) - mean
            out[...] = rate * (grad[...].astype(F32) - low) - away * (cross * (rate * rate * rate))
        o_dd[...] = dd[...].astype(F32)
        o_du[...] = du[...].astype(F32)


def body(
    images, aspect, reduce_weight, reduce_gain, reduce_bias, first_weight, first_gain, first_bias,
    second_weight, second_gain, second_bias, expand_weight, expand_gain, expand_bias, excite_down,
    excite_down_bias, excite_up, excite_up_bias, skip_gain, out_grad,
):
    N, H, W, CS = images.shape
    M = reduce_weight.shape[1]
    G = first_weight.shape[2]
    NI, MH, CH = N // 2, M // 2, 2 * CS
    dims = (H, W, NI, CS, CH, MH, M, G)
    quarter = expand_weight.shape[0]
    index = lax.axis_index("chan")
    dp = lax.axis_size("dp")
    YB = 2
    ZB = 4 if dp % 8 == 0 else dp // 2
    group = (YB, ZB)
    pe, pr, pd = quarter // (YB * ZB), CS // (YB * ZB), 9 * G // (2 * YB * ZB)
    img = jnp.transpose(images, (1, 2, 0, 3))
    og = jnp.transpose(out_grad, (1, 2, 0, 3))
    fw = first_weight.reshape(9 * G, M)
    sw = second_weight.reshape(9 * G, M)
    vectors = [reduce_gain, reduce_bias, first_gain, first_bias, second_gain, second_bias, expand_gain, expand_bias,
               excite_up_bias, excite_down_bias]
    vectors = [v.reshape(-1, G) for v in vectors] + [skip_gain.reshape(1, 1), aspect.reshape(1, N)]

    anyspec = pl.BlockSpec(memory_space=pl.ANY)
    vm = pl.BlockSpec(memory_space=pltpu.VMEM)
    S = jax.ShapeDtypeStruct
    V = pltpu.VMEM
    DMA = pltpu.SemaphoreType.DMA
    width = 2 * CS + 2 * M
    big = (
        S((H, W, NI, CH), F32), S((H, W, NI, CH), BF16), S((H, W, NI, CH), BF16), S((H, W, NI, M), BF16),
        S((CH, M), BF16), S((M, CH), BF16), S((H, W, NI, MH), F32), S((H, W, NI, MH), F32), S((H, W, NI, MH), F32),
        S((H + 2, W + 2, NI, MH), BF16), S((H + 2, W + 2, NI, MH), BF16), S((9 * G, MH), BF16), S((9 * G, MH), BF16),
        S((CH, M), BF16), S((4, YB, ZB, pe, CH), BF16), S((2, NI, width), BF16),
    )
    few = (
        S((2, NI, CH), F32), S((8, CH), F32), S((8, M), F32), S((2, 8, CH), F32), S((8, CH), F32), S((8, MH), F32),
        S((NI, G), F32),
    )
    fwd = pl.pallas_call(
        functools.partial(forward_kernel, dims, group),
        name="forward",
        out_shape=big + few,
        in_specs=[anyspec] * 8 + [vm] * 12,
        out_specs=[anyspec] * 16 + [vm] * 7,
        scratch_shapes=[
            V((H, W, NI, CH), BF16), V((H, W, NI, CH), BF16), V((CH, M), BF16), V((4, YB, ZB, pe, CH), BF16),
            V((CH, M), BF16), V((M, CH), BF16), V((9 * G, MH), BF16), V((9 * G, MH), BF16), V((4, 8, M), F32),
            V((CH, M), BF16), V((M, CH), BF16), V((9 * G, MH), BF16), V((9 * G, MH), BF16), V((9 * G, MH), BF16),
            V((9 * G, MH), BF16), V((2, NI, width), BF16),
            V((H, W, NI, MH), F32), V((H, W, NI, MH), BF16), V((H, W, NI, MH), BF16),
            V((H + 2, W + 2, NI, MH), BF16), V((H + 2, W + 2, NI, MH), BF16),
            V((H, W, NI, MH), F32), V((H, W, NI, MH), F32), V((H, W, NI, M), BF16), V((H, W, NI, CH), F32),
            V((3, NI, CH), F32), V((2, NI, M), F32), V((2, NI, M), F32), V((8, CS), F32), V((G, G), F32),
            DMA((H,)), DMA((H,)), DMA((H,)), DMA((8,)), DMA((8,)), DMA((8,)), DMA((3,)), DMA((4,)),
            DMA((H,)), DMA((H,)), DMA((H,)), DMA((H,)), DMA((3,)), DMA((3,)), DMA((16,)), DMA((4,)), DMA((2, ZB)), DMA((H,)),
        ],
        compiler_params=pltpu.CompilerParams(collective_id=0, has_side_effects=True, vmem_limit_bytes=62 << 20),
    )(img, og, reduce_weight, expand_weight.reshape(YB, ZB, pe, 2 * CH), excite_down, excite_up, fw, sw, *vectors)
    saved, fac, (se, fsum, stat_r, stat_e, vb, mvec, asp) = list(fwd[:15]), fwd[15], fwd[16:]
    saved[14] = saved[14].reshape(M, CH)

    slots = 2
    sums_e = [V((2, quarter, CH), BF16)] + [V((2, quarter // 2, CH), BF16)] * 2 + [V((ZB, 2, pe, CH), BF16)] * 2
    sums_r = [V((1, CS, MH), BF16)] + [V((1, CS // 2, MH), BF16)] * 2 + [V((ZB, 1, pr, MH), BF16)] * 2
    half = 9 * G // 2
    sums_d = [V((2, 1, half, MH), BF16)] + [V((2, 1, half // 2, MH), BF16)] * 2 + [V((2, ZB, 1, pd, MH), BF16)] * 2
    sums_v = [V((2, 8, M), F32), V((2, 8, M), F32), V((ZB, 8, M), F32)]
    block_out, gs, grouped, ew_sum, rw_sum, down_sum, up_sum, va, vl, rs, es = pl.pallas_call(
        functools.partial(backward_kernel, dims, group),
        name="backward",
        out_shape=(
            S((H, W, N, CS), BF16), S((H, W, N, CS), BF16), S((2, 2, YB, ZB, pd, M), BF16),
            S((YB, ZB, pe, 2 * CH), BF16), S((YB, ZB, pr, M), BF16), S((CS, M), BF16), S((M, CS), BF16),
            S((2, 8, M), F32), S((2, 8, M), F32), S((4, M), F32), S((4, 2 * CH), F32),
        ),
        in_specs=[anyspec] * 16 + [vm] * 7,
        out_specs=[anyspec] * 5 + [vm] * 6,
        scratch_shapes=[
            V((3, W, NI, CH), F32), V((H, W, NI, MH), F32), V((H, W, NI, CH), BF16), V((H, W, NI, CH), BF16),
            V((H, W, NI, M), BF16), V((CH, M), BF16), V((M, CH), BF16),
            V((4, W, NI, MH), F32), V((4, W, NI, MH), F32), V((4, W, NI, MH), F32),
            V((H + 2, W + 2, NI, MH), BF16), V((H + 2, W + 2, NI, MH), BF16), V((9 * G, MH), BF16), V((9 * G, MH), BF16),
            V((CH, M), BF16),
            V((H * W * NI, 9 * G), BF16), V((H, W, NI, MH), BF16), V((H, W, NI, MH), BF16),
            V((H + 2, W + 2, NI, MH), BF16), V((H + 2, W + 2, NI, MH), BF16),
            V((slots, W, NI, CH), BF16), V((slots, W, NI, CH), BF16), V((CH, M), BF16), V((2, MH, 9 * G), F32),
            V((2, 9 * G, MH), BF16), V((8, MH), F32), V((8, CH), F32), V((8, M), F32), V((YB, ZB, 2, NI, width), BF16),
            *sums_e, V((2, pe, CH), BF16), V((pe, 2 * CH), BF16),
            *sums_r, V((pr, MH), BF16),
            V((CS, MH), BF16), V((YB, ZB, pr, MH), BF16), V((YB, ZB, pr, MH), BF16), V((pr, MH), BF16),
            *sums_d, V((2, pd, MH), BF16),
            *sums_v, *sums_v,
            DMA((10,)), DMA((H, 3)), DMA((H, 3)), DMA((H,)), DMA((H,)), DMA((H,)), DMA((H,)),
            DMA((H,)), DMA((H,)), DMA((H,)), DMA((H,)), DMA((H,)), DMA((H,)),
            DMA((6,)), DMA((2, ZB)), DMA((3,)), DMA((2, ZB)), DMA((4,)), DMA((2, ZB)), DMA((3,)), DMA((2, ZB)),
            DMA((3,)), DMA((2, YB * ZB)), DMA((2, YB, ZB)),
            DMA((2, 4)), DMA((2, 2, ZB)), DMA((2, 3)), DMA((2, 2, ZB)), DMA((2, 2, 6)),
            DMA((6,)), DMA((2, ZB)), DMA((6,)), DMA((2, ZB)), DMA((4,)), DMA((2, ZB)), DMA((6,)),
            pltpu.SemaphoreType.REGULAR,
        ],
        compiler_params=pltpu.CompilerParams(collective_id=1, has_side_effects=True, vmem_limit_bytes=63 << 20),
    )(*saved, fac, se, fsum, stat_r, stat_e, vb, mvec, asp)

    parts = YB * ZB
    grouped = grouped.reshape(2, 9 * G, M)
    ew_sum, rw_sum = ew_sum.reshape(quarter, 2 * CH), rw_sum.reshape(CS, M)
    if dp > parts:
        whole = [v.astype(F32) for v in (grouped, ew_sum, rw_sum, down_sum, up_sum, va, vl)]
        whole = [v / parts for v in lax.psum(tuple(whole), "dp")]
        grouped, ew_sum, rw_sum, down_sum, up_sum = (v.astype(BF16) for v in whole[:5])
        va, vl = whole[5:]
        low = (vl[0] + vl[1])[0:2]
        rs = jnp.concatenate([rs[0:2], low[0:1] * (1.0 / (4 * CS)), low[1:2]], axis=0)
        low = jnp.concatenate([va[0, 5:7], va[1, 5:7]], axis=1)
        es = jnp.concatenate([es[0:2], low[0:1] * (1.0 / (4 * quarter)), low[1:2]], axis=0)
    late = vl[0] + vl[1]

    per = 5 if H % 5 == 0 else 1
    share = 3 * G
    steps = M // share
    spot = lambda h: jnp.minimum(h, steps - 1)
    row = pl.BlockSpec((per, W, N, CS), lambda h: (h, 0, 0, 0))
    lane = lambda rows, lanes: pl.BlockSpec((rows, lanes), lambda h: (0, spot(h)))
    tall = lambda rows, lanes: pl.BlockSpec((rows, lanes), lambda h: (spot(h), 0))
    which = lambda k: pl.BlockSpec((None, 9 * G, share), lambda h: (k, 0, spot(h)))
    wide = 2 * CH // steps
    outs = pl.pallas_call(
        functools.partial(finish_kernel, steps),
        name="finish",
        grid=(H // per,),
        out_shape=(
            S((H, W, N, CS), F32), S((9 * G, M), F32), S((9 * G, M), F32),
            S((CS, M), F32), S((quarter, 2 * CH), F32), S((CS, M), F32), S((M, CS), F32),
        ),
        in_specs=[
            row, row, which(0), which(1), lane(9 * G, share), lane(9 * G, share), lane(CS, share), lane(CS, share), lane(4, share),
            lane(quarter, wide), lane(quarter, wide), lane(4, wide), lane(CS, share), tall(share, CS),
        ],
        out_specs=[
            row, lane(9 * G, share), lane(9 * G, share), lane(CS, share), lane(quarter, wide), lane(CS, share), tall(share, CS),
        ],
        compiler_params=pltpu.CompilerParams(vmem_limit_bytes=60 << 20),
    )(og, gs, grouped, grouped, fw, sw, rw_sum, reduce_weight, rs, ew_sum, expand_weight, es, down_sum, up_sum)
    images_grad, first_grad, second_grad, rw_grad, ew_grad, down_grad, up_grad = outs

    xi, ci = index // 2, index % 2
    mine = lax.dynamic_slice_in_dim(lax.dynamic_index_in_dim(va, xi, 0, keepdims=False), ci * CS, CS, 1)
    back = lambda v: jnp.transpose(v, (2, 0, 1, 3))
    return (
        back(block_out), back(images_grad), rw_grad, late[2], late[3], first_grad.reshape(3, 3, G, M), late[4], late[5],
        second_grad.reshape(3, 3, G, M), late[6], late[7], ew_grad, mine[0], mine[1], down_grad, va[0, 4], up_grad, mine[2],
        jnp.sum(va[0, 3] + va[1, 3]).reshape(1),
    )


def solution(mesh):
    rows = P("dp", None, None, "chan")
    placed = (
        rows, P("dp"), P("chan", None), P(), P(), P(), P(), P(), P(), P(), P(), P("chan", None), P("chan"), P("chan"),
        P("chan", None), P(), P(None, "chan"), P("chan"), P(), rows,
    )
    results = (
        rows, rows, P("chan", None), P(), P(), P(), P(), P(), P(), P(), P(), P("chan", None), P("chan"), P("chan"),
        P("chan", None), P(), P(None, "chan"), P("chan"), P(),
    )
    return jax.shard_map(body, mesh=mesh, in_specs=placed, out_specs=results, check_vma=False)
```

time: 844 us -> 242 us (0.29); the launches traced: 830 us -> 241 us
  waiting for transfers between devices: 523 us -> 0 us
  local copies, waits for them, and re-layouts: 47.7 us -> 3.28 us
  other arithmetic: 29.3 us -> 2.26 us
  Pallas kernels: 209 us -> 235 us
  between operations: 16.8 us -> 1.36 us
    psum x2 -> x0, waiting for transfers between devices: 522 us -> none  [the longest x1 410 us: body(): dr_all = lax.psum(put(Dr, xi * CH, 2 * CH, 0), both)]
    pallas_call x2 -> x3, Pallas kernels: 209 us -> 235 us  [the longest x1 124 us: body(): pl.pallas_call(functools.partial(backward_kernel, dims, group), name='bac...]
    reduce_sum x9 -> x0, other arithmetic: 13.9 us -> none  [the longest x1 4.65 us: body(): r_sum = jnp.sum(dr_all, axis=0, keepdims=True)]
    unnamed x62 -> x3, local copies, waits for them, and re-layouts: 15 us -> 1.76 us
    transpose x3 -> x0, local copies, waits for them, and re-layouts: 11.6 us -> none  [group_grad(): total = jnp.transpose(dt).reshape(3, 3, G, M)]
    another operation x18 -> x0, local copies, waits for them, and re-layouts: 9.25 us -> none  [the longest x8 4.82 us: body(): jnp.stack([reduce_gain, reduce_bias, first_gain, first_bias, second_gain,...]
  transfers between devices with their start and end apart: 4 -> 0, of which waited for: 2 -> 0; matrix products, arithmetic and copies ran while one was open for 5% -> 0% of each run, Pallas kernels for 0% -> 0%
where the time goes in v3:
time: 242 us; the launch traced here: 241 us
  Pallas kernels  235 us (97%)
  local copies, waits for them, and re-layouts  3.28 us (1%)
    pallas_call x1, Pallas kernels, body(): pl.pallas_call(functools.partial(backward_kernel, dims, group), name='bac...  124 us
    pallas_call x1, Pallas kernels, body(): pl.pallas_call(functools.partial(forward_kernel, dims, group), name='forw...  97.8 us
    pallas_call x1, Pallas kernels, body(): pl.pallas_call(functools.partial(finish_kernel, steps), name='finish', gr...  13.1 us

profile of v3, /device:TPU:0, one launch (start us, length us, event | category | flops | bytes accessed | tf_op | source)
XLA Modules:
  0.0 241.4 jit_solution(11071436531835012901)
XLA Ops:
  1.3 97.8 %forward.1 = (f32[10,14,16,768]{3,2,1,0:T(8,128)}, bf16[10,14,16,768]{3,2,1,0:T(8,128)(2,1)}, bf16[10,14,16,768]{3,2,1,0:T(8,128)(2,1)}, bf16[10,14,16,768]{3,2,...) custom-call(bf16[10,14,32,384]{3,2,1,0:T(8,128)(2,1)} %bitcast.35, ...), custom_call_target="tpu_custom_call" | custom-call | tf_op jit(solution)/shard_map/forward/pallas_call | solution.py:1254
  99.1 123.7 %backward.1 = (bf16[10,14,32,384]{3,2,1,0:T(8,128)(2,1)}, bf16[10,14,32,384]{3,2,1,0:T(8,128)(2,1)}, bf16[2,2,2,4,72,768]{5,4,3,2,1,0:T(8,128)(2,1)}, bf16[2,4,2...) custom-call(f32[10,14,16,768]{3,2,1,0:T(8,128)} %get-tuple-element.6, ...), custom_call_target="tpu_custom_call" | custom-call | tf_op jit(solution)/shard_map/backward/pallas_call | solution.py:1283
  222.8 0.8 slice_add_fusion
  223.5 1.5 slice_reduce_fusion
  225.0 0.0 copy-start
  225.0 13.1 %finish.1 = (f32[10,14,32,384]{3,2,1,0:T(8,128)}, f32[1152,768]{1,0:T(8,128)}, f32[1152,768]{1,0:T(8,128)}, f32[384,768]{1,0:T(8,128)}, f32[192,1536]{1,0:T(8,12...) custom-call(bf16[10,14,32,384]{3,2,1,0:T(8,128)(2,1)} %bitcast.30, bf16[10,14,32,384]{3,2,1,0:T(8,128)(2,1)} %get-tuple-element.84.gs, ...), custom_call_target="tpu_custom_call" | custom-call | tf_op jit(solution)/shard_map/finish/pallas_call | solution.py:1342
  238.1 1.5 dynamic-slice_reduce_fusion
  239.7 0.0 copy-done
  239.7 1.8 copy.41
Async XLA Ops:
  225.0 14.6 %copy-start = (bf16[10,14,32,384]{3,2,1,0:T(8,128)(2,1)S(1)}, bf16[10,14,32,384]{3,2,1,0:T(8,128)(2,1)}, u32[]{:S(2)}) copy-start(bf16[10,14,32,384]{3,2,1,0:T(8,128)(2,1)} %get-tuple-element.83) | copy-start | bytes 10321924
